TPU v7x, 32 devices: a whole 2x2x4 slice. The times are simulated.
32 devices in a mesh: seq: 8 (over z, x), head: 4 (over y, core).
Axes of the slice: x: 2, y: 2, z: 4, core: 2. Of those that a mesh axis runs over, the one named last changes fastest.
Arguments:
- queries: bfloat16 [768, 16384], P('head', 'seq'), may hold values from -10 to 10
- key_vectors: bfloat16 [768, 16384], P('head', 'seq'), may hold values from -4 to 4
- value_vectors: bfloat16 [768, 16384], P('head', 'seq'), may hold values from -6 to 6
- offsets: int32 [3, 12], replicated, may hold values from 0 to 15, as said below
- out_weight: bfloat16 [768, 768], replicated, may hold values from -0.75 to 0.75
Outputs:
- layer_out: bfloat16 [16384, 768], P(('seq', 'head'))
Inputs may be any that keep to these rules, and one draw needn't show every extreme that they name: offsets[0, h] < 4, offsets[1, h] < 16 and offsets[2, h] < 16; in each row some head has 0 and some head the largest allowed value.
All inputs are finite; a program needn't handle non-finite values.
Results may differ from a plain program's by a relative error of at most 0.0052.
Values may be sent and summed in bfloat16 or wider, within the bound.
No kernel may reach another device: no remote copies, remote signals or barrier semaphores. Data moves between devices by JAX's collectives and lax.ppermute only.
A program may use at most 128 MiB of HBM per device.

v0:
```python
import functools
import math

import jax
import jax.numpy as jnp
from jax import lax
from jax.experimental import pallas as pl
from jax.experimental.pallas import tpu as pltpu
from jax.sharding import PartitionSpec as P

DH = 64
KEYS = 1024
LANES = 128
QBLK = 256
EXP2_SCALE = DH ** (-0.5) * math.log2(math.e)
NT = (((1,), (1,)), ((), ()))
NN = (((1,), (0,)), ((), ()))
VMEM_BYTES = 24 << 20
BF16, F32 = jnp.bfloat16, jnp.float32


def dot(a, b, dims):
    return lax.dot_general(a, b, dims, preferred_element_type=F32)


def lane_of(shape):
    return lax.broadcasted_iota(jnp.int32, shape, len(shape) - 1)


def in_values(shape, head):
    return (lane_of(shape) < DH) == (head % 2 == 0)


def stack_halves(values, others, head):
    return jnp.concatenate([values, others] if head % 2 == 0 else [others, values], 0)


def max_lane(head):
    return LANES - 1 if head % 2 == 0 else 0


def max_of(rows, head):
    at = max_lane(head)
    return rows[:, at : at + 1]


def over_sum(rows, head):
    at = DH if head % 2 == 0 else DH - 1
    return rows / rows[:, at : at + 1]


def put_max(rows, row_max, head):
    return jnp.where(lane_of(rows.shape) == max_lane(head), row_max, rows)


def swap(rows):
    return pltpu.roll(rows, DH, 1)


def softmax_block(scores):
    row_max = jnp.max(scores, axis=1, keepdims=True)
    weights = jnp.exp2((scores - row_max) * EXP2_SCALE).astype(BF16)
    return row_max, weights


def merge_rows(cur, cur_max, new, new_max):
    both = jnp.maximum(cur_max, new_max)
    keep_cur = jnp.exp2((cur_max - both) * EXP2_SCALE)
    keep_new = jnp.exp2((new_max - both) * EXP2_SCALE)
    return both, cur * keep_cur + new * keep_new


def select_kernel(dils, off_ref, q_hbm, k_hbm, v_hbm, q_ref, k_ref, v_ref, q1_ref, near_ref, far_ref, kvt, qt, sems):
    heads = q_ref.shape[0] // DH
    tok = q_ref.shape[1]
    n1 = tok // dils[0]
    copies = []
    for h in range(heads):
        rows = pl.ds(h * DH, DH)
        for i, (src, dst) in enumerate(((k_hbm, k_ref), (v_hbm, v_ref), (q_hbm, q_ref))):
            copy = pltpu.make_async_copy(src.at[rows, :], dst.at[rows, :], sems.at[h, i])
            copy.start()
            copies.append(copy)
    for h in range(heads):
        rows = slice(h * DH, (h + 1) * DH)
        head = lax.axis_index("head") * heads + h
        for copy in copies[3 * h : 3 * h + 3]:
            copy.wait()
        kvt[...] = stack_halves(v_ref[rows, :], k_ref[rows, :], h).T.astype(F32)
        query = q_ref[rows, :]
        qt[...] = stack_halves(jnp.zeros_like(query), query, h).T.astype(F32)
        picks = [pl.ds(off_ref[b, head], tok // d, stride=d) for b, d in enumerate(dils)]
        q1_ref[h] = qt[picks[0], :].astype(BF16)
        near_ref[h, :n1, :] = kvt[picks[0], :].astype(BF16)
        far_q = qt[picks[1], :]
        if len(dils) == 3:
            far_q = far_q + swap(qt[picks[2], :])
        near_ref[h, n1:, :] = far_q.astype(BF16)
        for b in range(1, len(dils)):
            far_ref[b - 1, h] = kvt[picks[b], :].astype(BF16)


def local_kernel(q_ref, k_ref, v_ref, acc_ref):
    tok = q_ref.shape[1]
    for h in range(q_ref.shape[0] // DH):
        rows = slice(h * DH, (h + 1) * DH)
        qt = q_ref[rows, :].T
        for seg in range(tok // KEYS):
            cols = slice(seg * KEYS, (seg + 1) * KEYS)
            keys = k_ref[rows, cols]
            vals = v_ref[rows, cols]
            vals = stack_halves(vals, jnp.ones_like(vals), h)
            for blk in range(KEYS // QBLK):
                at = seg * KEYS + blk * QBLK
                row_max, weights = softmax_block(dot(qt[at : at + QBLK], keys, NN))
                acc_ref[h, at : at + QBLK, :] = put_max(dot(weights, vals, NT), row_max, h)


def pair_kernel(dils, off_ref, q_ref, own_ref, other_ref, acc_in, m0, m1, m2, m3, cur_ref, acc):
    heads, n1, _ = q_ref.shape
    tok = acc.shape[0]
    me = lax.axis_index("head")
    mains = (m0, m1, m2, m3)
    width = tok // len(mains)
    held = None
    for h in range(heads):
        head = me * heads + h
        acc[...] = acc_in[h]
        kv = jnp.concatenate([own_ref[h, :n1, :], other_ref[h, :n1, :]], 0)
        vals = jnp.where(in_values(kv.shape, h), kv, jnp.ones_like(kv))
        for blk in range(n1 // QBLK):
            rows = pl.ds(off_ref[0, head] + blk * QBLK * dils[0], QBLK, stride=dils[0])
            row_max, weights = softmax_block(dot(q_ref[h, blk * QBLK : (blk + 1) * QBLK], kv, NT))
            out = dot(weights, vals, NN)
            cur = acc[rows, :]
            both, new = merge_rows(cur, max_of(cur, h), out, row_max)
            acc[rows, :] = put_max(new, both, h)
        for b in range(1, len(dils)):
            cur_ref[b - 1, h] = acc[pl.ds(off_ref[b, head], tok // dils[b], stride=dils[b]), :]
        whole = acc[...]
        done = over_sum(whole, h)
        if h % 2 == 0:
            held = done
            if h + 1 < heads:
                continue
            pieces = []
            for dest in range(len(mains)):
                half = width // 2
                lo = done[dest * width : dest * width + half]
                hi = done[dest * width + half : (dest + 1) * width]
                pieces.append(jnp.where(lane_of(lo.shape) < DH, lo, swap(hi)))
            packed = jnp.concatenate(pieces, 0).astype(BF16)
        else:
            packed = jnp.where(lane_of(done.shape) < DH, held, done).astype(BF16)
        size = packed.shape[0] // len(mains)
        start = (h // 2) * width
        for s, out in enumerate(mains):
            for dest in range(len(mains)):

                @pl.when((me ^ s) == dest)
                def _():
                    out[start : start + size, :] = packed[dest * size : (dest + 1) * size]


def far_kernel(branches, own_ref, other_ref, kv0, kv1, kv2, kv3, part_ref, send_ref):
    heads = own_ref.shape[0]
    n = kv0.shape[2]
    n1 = own_ref.shape[1] - n
    for h in range(heads):
        q_all = jnp.concatenate([own_ref[h, n1:, :], other_ref[h, n1:, :]], 0)
        outs, tops = [], []
        for b in range(branches):
            kv = jnp.concatenate([r[b, h] for r in (kv0, kv1, kv2, kv3)], 0)
            q_b = q_all if b == 0 else swap(q_all.astype(F32)).astype(BF16)
            q_b = jnp.where(in_values(q_b.shape, h), jnp.zeros_like(q_b), q_b)
            row_max, weights = softmax_block(dot(q_b, kv, NT))
            out = dot(weights, jnp.where(in_values(kv.shape, h), kv, jnp.ones_like(kv)), NN)
            part_ref[b, h] = put_max(out[:n], row_max[:n], h)
            outs.append(out[n:])
            tops.append(row_max[n:])
        a_lanes = in_values((n, LANES), h)
        other, other_top = (swap(outs[1]), tops[1]) if branches == 2 else (outs[0], tops[0])
        send_ref[h, :n, :] = jnp.where(a_lanes, outs[0], other).astype(BF16)
        slot = lane_of((n, LANES)) % DH
        stats = jnp.where(
            slot >= 3, jnp.where(a_lanes, other, outs[0]), jnp.where(a_lanes, other_top, tops[0])
        )
        high = stats.astype(BF16).astype(F32)
        mid = (stats - high).astype(BF16).astype(F32)
        low = stats - high - mid
        coded = jnp.where(slot % 3 == 0, high, jnp.where(slot % 3 == 1, mid, low))
        send_ref[h, n:, :] = coded.astype(BF16)


def patch_kernel(branches, off_ref, cur_ref, part_ref, got_ref, p0, p1, p2, p3):
    heads, two_n, _ = got_ref.shape
    n = two_n // 2
    me = lax.axis_index("head")
    patches = (p0, p1, p2, p3)
    size = n // len(patches)
    done = []
    for h in range(heads):
        a_lanes = in_values((n, LANES), h)
        got = got_ref[h, :n, :].astype(F32)
        coded = got_ref[h, n:, :].astype(F32)
        merged, states = [], []
        for b in range(branches):
            c = DH * (1 - h % 2) if b == 0 else DH * (h % 2)
            got_max = coded[:, c : c + 1] + coded[:, c + 1 : c + 2] + coded[:, c + 2 : c + 3]
            got_sum = coded[:, c + 3 : c + 4] + coded[:, c + 4 : c + 5] + coded[:, c + 5 : c + 6]
            new = jnp.where(a_lanes, got if b == 0 else swap(got), got_sum)
            part = part_ref[b, h]
            states.append(merge_rows(part, max_of(part, h), new, got_max))
        head = me * heads + h
        cur = cur_ref[0, h]
        first_max, first = merge_rows(cur, max_of(cur, h), states[0][1], states[0][0])
        merged.append(first)
        if branches == 2:
            same = off_ref[1, head] == off_ref[2, head]
            cur = cur_ref[1, h]
            base = jnp.where(same, first, cur)
            base_max = jnp.where(same, first_max, max_of(cur, h))
            _, second = merge_rows(base, base_max, states[1][1], states[1][0])
            merged = [jnp.where(same, second, first), second]
        done.append([over_sum(m, h) for m in merged])
    lane = lane_of((n, LANES))
    rows = []
    for b in range(branches):
        rows.append(jnp.where(lane < DH, done[0][b], done[1][b]).astype(BF16))
    last = done[2]
    rows.append(jnp.where(lane < DH, last[0], swap(last[-1])).astype(BF16))
    for s, out in enumerate(patches):
        for dest in range(len(patches)):

            @pl.when((me ^ s) == dest)
            def _():
                for i, r in enumerate(rows):
                    out[i * size : (i + 1) * size, :] = r[dest * size : (dest + 1) * size]


def project_kernel(branches, dil, off_ref, x0, x1, x2, x3, p0, p1, p2, p3, w_ref, out_ref, pairs, lasts):
    me = lax.axis_index("head")
    width = out_ref.shape[0]
    half = width // 2
    size = width // dil
    heads = 3
    rows = heads * DH
    sources = [me ^ s for s in range(4)]
    xs, ps = (x0, x1, x2, x3), (p0, p1, p2, p3)
    low = lane_of((size, LANES)) < DH
    for s in range(4):
        pairs[s] = xs[s][:width, :].astype(F32)
    for t in range(2):
        a = xs[2 * t][width:, :].astype(F32)
        b = xs[2 * t + 1][width:, :].astype(F32)
        lane = lane_of(a.shape)
        lasts[t, :half, :] = jnp.where(lane < DH, a, swap(b))
        lasts[t, half:, :] = jnp.where(lane < DH, swap(a), b)
    for s in range(4):
        for b in range(branches):
            new = ps[s][b * size : (b + 1) * size, :].astype(F32)
            for h in range(2):
                at = pl.ds(off_ref[b + 1, sources[s] * heads + h], size, stride=dil)
                pairs[s, at, :] = jnp.where(low == (h == 0), new, pairs[s, at, :])
            new = ps[s][branches * size :, :].astype(F32)
            if b != s % 2:
                new = swap(new)
            at = pl.ds(off_ref[b + 1, sources[s] * heads + 2], size, stride=dil)
            lasts[s // 2, at, :] = jnp.where(low == (s % 2 == 0), new, lasts[s // 2, at, :])

    def w_rows(s, start, count):
        return w_ref[pl.ds(pl.multiple_of(sources[s] * rows + start, DH), count), :]

    total = None
    for t in range(3):
        if t < 2:
            x = jnp.concatenate([pairs[2 * t], pairs[2 * t + 1]], 1)
            w = jnp.concatenate([w_rows(2 * t, 0, LANES), w_rows(2 * t + 1, 0, LANES)], 0)
        else:
            x = jnp.concatenate([lasts[0], lasts[1]], 1)
            w = jnp.concatenate([w_rows(s, LANES, DH) for s in range(4)], 0)
        part = dot(x.astype(BF16), w, NN)
        total = part if total is None else total + part
    out_ref[...] = total.astype(BF16)


def partner(block, axis, apart):
    count = lax.axis_size(axis)
    return lax.ppermute(block, axis, [(i, i ^ apart) for i in range(count)])


def call(kernel, name, outs, in_specs, scratch=(), queries=0, keys=0):
    estimate = None
    if queries:
        estimate = pl.CostEstimate(
            flops=queries * keys * 512, bytes_accessed=queries * 1024, transcendentals=queries * keys
        )
    return pl.pallas_call(
        kernel,
        out_shape=tuple(jax.ShapeDtypeStruct(*o) for o in outs),
        in_specs=in_specs,
        out_specs=(pl.BlockSpec(memory_space=pltpu.VMEM),) * len(outs),
        scratch_shapes=scratch,
        compiler_params=pltpu.CompilerParams(vmem_limit_bytes=VMEM_BYTES),
        cost_estimate=estimate,
        name=name,
    )


def spread_far(acc, query_h, key_h, value_h, dil, head_offsets):
    hit = jnp.arange(dil)[None, :] == head_offsets[:, None]

    def pick(x):
        shaped = x.reshape(x.shape[:2] + (x.shape[2] // dil, dil))
        return jnp.sum(shaped * hit[:, None, None, :].astype(x.dtype), axis=-1, dtype=x.dtype)

    pair = lax.all_gather(jnp.stack([pick(key_h), pick(value_h)], 0), "seq", axis=3, tiled=True)
    scores = jnp.einsum("hdq,hdk->hqk", pick(query_h), pair[0], preferred_element_type=F32)
    new_max = jnp.max(scores, axis=2, keepdims=True)
    e = jnp.exp2((scores - new_max) * EXP2_SCALE)
    new_sum = jnp.sum(e, axis=2, keepdims=True)
    new_acc = jnp.einsum("hqk,hdk->hqd", e.astype(BF16), pair[1], preferred_element_type=F32)
    heads, tok, _ = acc.shape
    shaped = acc.reshape(heads, tok // dil, dil, LANES)
    cur = jnp.sum(jnp.where(hit[:, None, :, None], shaped, 0.0), axis=2)
    sums = jnp.broadcast_to(new_sum, new_acc.shape)
    rows = []
    for h in range(heads):
        halves = [new_acc[h], sums[h]] if h % 2 == 0 else [sums[h], new_acc[h]]
        both, out = merge_rows(cur[h], max_of(cur[h], h), jnp.concatenate(halves, 1), new_max[h])
        rows.append(put_max(out, both, h))
    out = jnp.stack(rows, 0)
    return jnp.where(hit[:, None, :, None], out[:, :, None, :], shaped).reshape(acc.shape)


def local(queries, key_vectors, value_vectors, offsets, out_weight):
    tok = queries.shape[1]
    heads = queries.shape[0] // DH
    seq_count = lax.axis_size("seq")
    far_rate = tok * seq_count // KEYS
    dils = (4, 16, 16) if far_rate == 16 else (4, 16)
    branches = len(dils) - 1
    n1, n2 = tok // 4, tok // 16
    width = tok // 4
    whole = pl.BlockSpec(memory_space=pltpu.VMEM)
    smem = pl.BlockSpec(memory_space=pltpu.SMEM)
    hbm = pl.BlockSpec(memory_space=pltpu.HBM)

    q, k, v, q1, near, far = call(
        functools.partial(select_kernel, dils),
        "select",
        [(queries.shape, BF16)] * 3
        + [
            ((heads, n1, LANES), BF16),
            ((heads, n1 + n2, LANES), BF16),
            ((branches, heads, n2, LANES), BF16),
        ],
        [smem, hbm, hbm, hbm],
        [
            pltpu.VMEM((tok, LANES), F32),
            pltpu.VMEM((tok, LANES), F32),
            pltpu.SemaphoreType.DMA((heads, 3)),
        ],
    )(offsets, queries, key_vectors, value_vectors)

    near_other = partner(near, "seq", 1)
    fars = [far] + [partner(far, "seq", apart) for apart in (2, 4, 6)]

    (acc,) = call(
        local_kernel, "local", [((heads, tok, LANES), F32)], [whole] * 3, queries=heads * tok, keys=KEYS
    )(q, k, v)

    if branches == 1:
        shape = (heads, DH, tok)
        my_offsets = lax.dynamic_slice_in_dim(offsets[2], lax.axis_index("head") * heads, heads, 0)
        parts = [a.reshape(shape) for a in (queries, key_vectors, value_vectors)]
        acc = spread_far(acc, *parts, far_rate, my_offsets)

    *mains, cur = call(
        functools.partial(pair_kernel, dils),
        "pair",
        [((heads * width // 2, LANES), BF16)] * 4 + [((branches, heads, n2, LANES), F32)],
        [smem] + [whole] * 4,
        [pltpu.VMEM((tok, LANES), F32)],
        queries=heads * n1,
        keys=KEYS,
    )(offsets, q1, near, near_other, acc)
    landed = [mains[0]] + [partner(mains[s], "head", s) for s in range(1, 4)]

    fars, cur, landed[1] = lax.optimization_barrier((fars, cur, landed[1]))
    part, send = call(
        functools.partial(far_kernel, branches),
        "far",
        [((branches, heads, n2, LANES), F32), ((heads, 2 * n2, LANES), BF16)],
        [whole] * 6,
        queries=heads * n2 * 4,
        keys=KEYS // 2,
    )(near, near_other, *fars)
    got = partner(send, "seq", 1)

    patches = call(
        functools.partial(patch_kernel, branches),
        "patch",
        [(((branches + 1) * n2 // 4, LANES), BF16)] * 4,
        [smem] + [whole] * 3,
    )(offsets, cur, part, got)
    fixes = [patches[0]] + [partner(patches[s], "head", s) for s in range(1, 4)]

    (out,) = call(
        functools.partial(project_kernel, branches, dils[1]),
        "project",
        [((width, out_weight.shape[1]), BF16)],
        [smem] + [whole] * 9,
        [pltpu.VMEM((4, width, LANES), F32), pltpu.VMEM((2, width, LANES), F32)],
    )(offsets, *landed, *fixes, out_weight)
    return out


def solution(mesh):
    in_specs = (P("head", "seq"), P("head", "seq"), P("head", "seq"), P(), P())
    out_specs = P(("seq", "head"), None)
    return jax.shard_map(local, mesh=mesh, in_specs=in_specs, out_specs=out_specs, check_vma=False)
```

profile of v0, /device:TPU:0, one launch (start us, length us, event | category | flops | bytes accessed | tf_op | source)
XLA Modules:
  0.0 48.1 jit_solution(18332118023364077207)
XLA Ops:
  0.0 1.1 %copy-done.1 = bf16[192,2048]{1,0:T(8,128)(2,1)S(1)} copy-done((bf16[192,2048]{1,0:T(8,128)(2,1)S(1)}, bf16[192,2048]{1,0:T(8,128)(2,1)}, u32[]{:S(2)}) %copy-start.1) | copy-done | bytes 786456
  1.1 1.1 %copy-done.2 = bf16[192,2048]{1,0:T(8,128)(2,1)S(1)} copy-done((bf16[192,2048]{1,0:T(8,128)(2,1)S(1)}, bf16[192,2048]{1,0:T(8,128)(2,1)}, u32[]{:S(2)}) %copy-start.2) | copy-done | bytes 786456
  2.3 1.1 %copy-done.3 = bf16[192,2048]{1,0:T(8,128)(2,1)S(1)} copy-done((bf16[192,2048]{1,0:T(8,128)(2,1)S(1)}, bf16[192,2048]{1,0:T(8,128)(2,1)}, u32[]{:S(2)}) %copy-start.3) | copy-done | bytes 786456
  3.4 0.7 %copy-done.4 = s32[3,12]{1,0:T(4,128)S(1)} copy-done((s32[3,12]{1,0:T(4,128)S(1)}, s32[3,12]{1,0:T(4,128)}, u32[]{:S(2)}) %copy-start.4) | copy-done | bytes 168
  4.1 2.4 %select.1 = (bf16[192,2048]{1,0:T(8,128)(2,1)S(1)}, bf16[192,2048]{1,0:T(8,128)(2,1)S(1)}, bf16[192,2048]{1,0:T(8,128)(2,1)S(1)}, bf16[3,512,128]{2,1,0:T(8,128)...) custom-call(s32[3,12]{1,0:T(4,128)S(1)} %copy-done.4, bf16[192,2048]{1,0:T(8,128)(2,1)S(1)} %copy-done.1, ...), custom_call_target="tpu_custom_call" | custom-call | tf_op jit(solution)/shard_map/select/pallas_call | solution.py:349
  6.5 3.0 %collective-permute-start = (bf16[3,640,128]{2,1,0:T(8,128)(2,1)S(1)}, bf16[3,640,128]{2,1,0:T(8,128)(2,1)S(1)}, u32[]{:S(2)}, u32[]{:S(2)}) collective-permute-start(bf16[3,640,128]{2,1,0:T(8,128)(2,1)S(1)} %get-tuple-element.29.own_ref), channel_id=1, source_target_pairs={{0,4},{4,0},{8,12},{12,8},{16,20},{20,16},{24,28},{28,24},{1,5},{5... | collective-permute-start | bytes 1474568 | tf_op jit(solution)/shard_map/ppermute | solution.py:289
  9.5 1.6 %collective-permute-start.1 = (bf16[2,3,128,128]{3,2,1,0:T(8,128)(2,1)S(1)}, bf16[2,3,128,128]{3,2,1,0:T(8,128)(2,1)S(1)}, u32[]{:S(2)}, u32[]{:S(2)}) collective-permute-start(bf16[2,3,128,128]{3,2,1,0:T(8,128)(2,1)S(1)} %get-tuple-element.41.kv0), channel_id=1, source_target_pairs={{0,8},{4,12},{8,0},{12,4},{16,24},{20,28},{24,16},{28,20},{1,9},{5... | collective-permute-start | bytes 589832 | tf_op jit(solution)/shard_map/ppermute | solution.py:289
  11.1 2.6 %collective-permute-start.2 = (bf16[2,3,128,128]{3,2,1,0:T(8,128)(2,1)S(1)}, bf16[2,3,128,128]{3,2,1,0:T(8,128)(2,1)S(1)}, u32[]{:S(2)}, u32[]{:S(2)}) collective-permute-start(bf16[2,3,128,128]{3,2,1,0:T(8,128)(2,1)S(1)} %get-tuple-element.41.kv0), channel_id=1, source_target_pairs={{0,16},{4,20},{8,24},{12,28},{16,0},{20,4},{24,8},{28,12},{1,17},{... | collective-permute-start | bytes 589832 | tf_op jit(solution)/shard_map/ppermute | solution.py:289
  13.7 0.2 collective-permute-start.3
  13.9 7.6 %local.1.acc_in = f32[3,2048,128]{2,1,0:T(8,128)S(1)} custom-call(bf16[192,2048]{1,0:T(8,128)(2,1)S(1)} %get-tuple-element.30.q_ref, bf16[192,2048]{1,0:T(8,128)(2,1)S(1)} %get-tuple-element.31.k_ref, bf16[192,2048]{1,0:T(8,128)(2,1)S(1)} %get-tuple-element.32.v_ref), custom_call_target="tpu_custom_call" | custom-call | flops 3221225472 | bytes 6291456 | tf_op jit(solution)/shard_map/local/pallas_call | solution.py:369
  21.5 5.5 %pair.1 = (bf16[768,128]{1,0:T(8,128)(2,1)S(1)}, bf16[768,128]{1,0:T(8,128)(2,1)S(1)}, bf16[768,128]{1,0:T(8,128)(2,1)S(1)}, bf16[768,128]{1,0:T(8,128)(2,1)S(1)}, f32[2,3,128,128]{3,2,1,0:T(8,128)S(1)}) custom-call(s32[3,12]{1,0:T(4,128)S(1)} %copy-done.5, bf16[3,512,128]{2,1,0:T(8,128)(2,1)S(1)} %get-tuple-element.28.q_ref, ...), custom_call_target="tpu_custom_call" | custom-call | flops 805306368 | bytes 1572864 | tf_op jit(solution)/shard_map/pair/pallas_call | solution.py:379
  27.1 1.1 %collective-permute-done.2.kv2 = bf16[2,3,128,128]{3,2,1,0:T(8,128)(2,1)S(1)} collective-permute-done((bf16[2,3,128,128]{3,2,1,0:T(8,128)(2,1)S(1)}, bf16[2,3,128,128]{3,2,1,0:T(8,128)(2,1)S(1)}, u32[]{:S(2)}, u32[]{:S(2)}) %collective-permute-start.2) | collective-permute-done | bytes 196640 | tf_op jit(solution)/shard_map/ppermute | solution.py:289
  28.2 0.3 collective-permute-done.4.x1
  28.5 2.0 %far.1 = (f32[2,3,128,128]{3,2,1,0:T(8,128)S(1)}, bf16[3,256,128]{2,1,0:T(8,128)(2,1)S(1)}) custom-call(bf16[3,640,128]{2,1,0:T(8,128)(2,1)S(1)} %get-tuple-element.29.own_ref, bf16[3,640,128]{2,1,0:T(8,128)(2,1)S(1)} %collective-permute-done.other_ref, bf16[2,3,128,128]{3,2,1,0:T(8,128)(2,1)S(1)} %get-tuple-element.41.kv0, ...), custom_call_target="tpu_custom_call" | custom-call | flops 402653184 | bytes 1572864 | tf_op jit(solution)/shard_map/far/pallas_call | solution.py:391
  30.6 1.0 %collective-permute-start.7 = (bf16[3,256,128]{2,1,0:T(8,128)(2,1)S(1)}, bf16[3,256,128]{2,1,0:T(8,128)(2,1)S(1)}, u32[]{:S(2)}, u32[]{:S(2)}) collective-permute-start(bf16[3,256,128]{2,1,0:T(8,128)(2,1)S(1)} %get-tuple-element.46), channel_id=1, source_target_pairs={{0,4},{4,0},{8,12},{12,8},{16,20},{20,16},{24,28},{28,24},{1,5},{5... | collective-permute-start | bytes 589832 | tf_op jit(solution)/shard_map/ppermute | solution.py:289
  31.6 1.5 %collective-permute-start.5 = (bf16[768,128]{1,0:T(8,128)(2,1)S(1)}, bf16[768,128]{1,0:T(8,128)(2,1)S(1)}, u32[]{:S(2)}, u32[]{:S(2)}) collective-permute-start(bf16[768,128]{1,0:T(8,128)(2,1)S(1)} %get-tuple-element.38), channel_id=1, source_target_pairs={{0,2},{1,3},{2,0},{3,1},{4,6},{5,7},{6,4},{7,5},{8,10},{9,11},{10,... | collective-permute-start | bytes 589832 | tf_op jit(solution)/shard_map/ppermute | solution.py:289
  33.1 4.5 %collective-permute-done.7.got_ref = bf16[3,256,128]{2,1,0:T(8,128)(2,1)S(1)} collective-permute-done((bf16[3,256,128]{2,1,0:T(8,128)(2,1)S(1)}, bf16[3,256,128]{2,1,0:T(8,128)(2,1)S(1)}, u32[]{:S(2)}, u32[]{:S(2)}) %collective-permute-start.7) | collective-permute-done | bytes 196640 | tf_op jit(solution)/shard_map/ppermute | solution.py:289
  37.6 2.4 %patch.1 = (bf16[96,128]{1,0:T(8,128)(2,1)S(1)}, bf16[96,128]{1,0:T(8,128)(2,1)S(1)}, bf16[96,128]{1,0:T(8,128)(2,1)S(1)}, bf16[96,128]{1,0:T(8,128)(2,1)S(1)}) custom-call(s32[3,12]{1,0:T(4,128)S(1)} %copy-done.5, f32[2,3,128,128]{3,2,1,0:T(8,128)S(1)} %get-tuple-element.40.cur_ref, f32[2,3,128,128]{3,2,1,0:T(8,128)S(1)} %get-tuple-element.45.part_ref, ...), custom_call_target="tpu_custom_call" | custom-call | tf_op jit(solution)/shard_map/patch/pallas_call | solution.py:401
  40.0 0.5 %collective-permute-start.10 = (bf16[96,128]{1,0:T(8,128)(2,1)S(1)}, bf16[96,128]{1,0:T(8,128)(2,1)S(1)}, u32[]{:S(2)}, u32[]{:S(2)}) collective-permute-start(bf16[96,128]{1,0:T(8,128)(2,1)S(1)} %get-tuple-element.50), channel_id=1, source_target_pairs={{0,3},{1,2},{2,1},{3,0},{4,7},{5,6},{6,5},{7,4},{8,11},{9,10},{10,... | collective-permute-start | bytes 73736 | tf_op jit(solution)/shard_map/ppermute | solution.py:289
  40.5 1.2 %collective-permute-start.8 = (bf16[96,128]{1,0:T(8,128)(2,1)S(1)}, bf16[96,128]{1,0:T(8,128)(2,1)S(1)}, u32[]{:S(2)}, u32[]{:S(2)}) collective-permute-start(bf16[96,128]{1,0:T(8,128)(2,1)S(1)} %get-tuple-element.48), channel_id=1, source_target_pairs={{0,1},{1,0},{2,3},{3,2},{4,5},{5,4},{6,7},{7,6},{8,9},{9,8},{10,11... | collective-permute-start | bytes 73736 | tf_op jit(solution)/shard_map/ppermute | solution.py:289
  41.7 0.5 %collective-permute-start.9 = (bf16[96,128]{1,0:T(8,128)(2,1)S(1)}, bf16[96,128]{1,0:T(8,128)(2,1)S(1)}, u32[]{:S(2)}, u32[]{:S(2)}) collective-permute-start(bf16[96,128]{1,0:T(8,128)(2,1)S(1)} %get-tuple-element.49), channel_id=1, source_target_pairs={{0,2},{1,3},{2,0},{3,1},{4,6},{5,7},{6,4},{7,5},{8,10},{9,11},{10,... | collective-permute-start | bytes 73736 | tf_op jit(solution)/shard_map/ppermute | solution.py:289
  42.2 1.3 %collective-permute-done.10.p3 = bf16[96,128]{1,0:T(8,128)(2,1)S(1)} collective-permute-done((bf16[96,128]{1,0:T(8,128)(2,1)S(1)}, bf16[96,128]{1,0:T(8,128)(2,1)S(1)}, u32[]{:S(2)}, u32[]{:S(2)}) %collective-permute-start.10) | collective-permute-done | bytes 24608 | tf_op jit(solution)/shard_map/ppermute | solution.py:289
  43.5 2.0 %collective-permute-done.9.p2 = bf16[96,128]{1,0:T(8,128)(2,1)S(1)} collective-permute-done((bf16[96,128]{1,0:T(8,128)(2,1)S(1)}, bf16[96,128]{1,0:T(8,128)(2,1)S(1)}, u32[]{:S(2)}, u32[]{:S(2)}) %collective-permute-start.9) | collective-permute-done | bytes 24608 | tf_op jit(solution)/shard_map/ppermute | solution.py:289
  45.5 2.6 %project.1 = bf16[512,768]{1,0:T(8,128)(2,1)} custom-call(s32[3,12]{1,0:T(4,128)S(1)} %copy-done.5, bf16[768,128]{1,0:T(8,128)(2,1)S(1)} %get-tuple-element.33.x0, bf16[768,128]{1,0:T(8,128)(2,1)S(1)} %collective-permute-done.4.x1, bf16[768,128]{1,0:T(8,128)(2,1)S(1)} %collective-permute-done.5.x2, bf16[768,128]{1,0:T(8,128)(2,1)S(1)} %collective-permute-done.6.x3, ...), custom_call_target="tpu_custom_call" | custom-call | tf_op jit(solution)/shard_map/project/pallas_call | solution.py:409
  (16 shorter events, 0.1 us)
Async XLA Ops:
  0.0 1.1 %copy-start.1 = (bf16[192,2048]{1,0:T(8,128)(2,1)S(1)}, bf16[192,2048]{1,0:T(8,128)(2,1)}, u32[]{:S(2)}) copy-start(bf16[192,2048]{1,0:T(8,128)(2,1)} %q_hbm.1) | copy-start | bytes 2359300
  1.1 1.1 %copy-start.2 = (bf16[192,2048]{1,0:T(8,128)(2,1)S(1)}, bf16[192,2048]{1,0:T(8,128)(2,1)}, u32[]{:S(2)}) copy-start(bf16[192,2048]{1,0:T(8,128)(2,1)} %k_hbm.1) | copy-start | bytes 2359300
  2.3 1.1 %copy-start.3 = (bf16[192,2048]{1,0:T(8,128)(2,1)S(1)}, bf16[192,2048]{1,0:T(8,128)(2,1)}, u32[]{:S(2)}) copy-start(bf16[192,2048]{1,0:T(8,128)(2,1)} %v_hbm.1) | copy-start | bytes 2359300
  3.4 0.7 %copy-start.4 = (s32[3,12]{1,0:T(4,128)S(1)}, s32[3,12]{1,0:T(4,128)}, u32[]{:S(2)}) copy-start(s32[3,12]{1,0:T(4,128)} %off_ref.7) | copy-start | bytes 436
  6.5 15.0 %collective-permute-start = (bf16[3,640,128]{2,1,0:T(8,128)(2,1)S(1)}, bf16[3,640,128]{2,1,0:T(8,128)(2,1)S(1)}, u32[]{:S(2)}, u32[]{:S(2)}) collective-permute-start(bf16[3,640,128]{2,1,0:T(8,128)(2,1)S(1)} %get-tuple-element.29.own_ref), channel_id=1, source_target_pairs={{0,4},{4,0},{8,12},{12,8},{16,20},{20,16},{24,28},{28,24},{1,5},{5... | collective-permute-start | bytes 1474568 | tf_op jit(solution)/shard_map/ppermute | solution.py:289
  9.5 17.6 %collective-permute-start.1 = (bf16[2,3,128,128]{3,2,1,0:T(8,128)(2,1)S(1)}, bf16[2,3,128,128]{3,2,1,0:T(8,128)(2,1)S(1)}, u32[]{:S(2)}, u32[]{:S(2)}) collective-permute-start(bf16[2,3,128,128]{3,2,1,0:T(8,128)(2,1)S(1)} %get-tuple-element.41.kv0), channel_id=1, source_target_pairs={{0,8},{4,12},{8,0},{12,4},{16,24},{20,28},{24,16},{28,20},{1,9},{5... | collective-permute-start | bytes 589832 | tf_op jit(solution)/shard_map/ppermute | solution.py:289
  11.1 17.2 %collective-permute-start.2 = (bf16[2,3,128,128]{3,2,1,0:T(8,128)(2,1)S(1)}, bf16[2,3,128,128]{3,2,1,0:T(8,128)(2,1)S(1)}, u32[]{:S(2)}, u32[]{:S(2)}) collective-permute-start(bf16[2,3,128,128]{3,2,1,0:T(8,128)(2,1)S(1)} %get-tuple-element.41.kv0), channel_id=1, source_target_pairs={{0,16},{4,20},{8,24},{12,28},{16,0},{20,4},{24,8},{28,12},{1,17},{... | collective-permute-start | bytes 589832 | tf_op jit(solution)/shard_map/ppermute | solution.py:289
  13.7 14.6 %collective-permute-start.3 = (bf16[2,3,128,128]{3,2,1,0:T(8,128)(2,1)S(1)}, bf16[2,3,128,128]{3,2,1,0:T(8,128)(2,1)S(1)}, u32[]{:S(2)}, u32[]{:S(2)}) collective-permute-start(bf16[2,3,128,128]{3,2,1,0:T(8,128)(2,1)S(1)} %get-tuple-element.41.kv0), channel_id=1, source_target_pairs={{0,24},{4,28},{8,16},{12,20},{16,8},{20,12},{24,0},{28,4},{1,25},{... | collective-permute-start | bytes 589832 | tf_op jit(solution)/shard_map/ppermute | solution.py:289
  13.9 7.6 %copy-start.5 = (s32[3,12]{1,0:T(4,128)S(1)}, s32[3,12]{1,0:T(4,128)}, u32[]{:S(2)}) copy-start(s32[3,12]{1,0:T(4,128)} %off_ref.7) | copy-start | bytes 436
  21.5 24.0 %copy-start = (bf16[768,768]{1,0:T(8,128)(2,1)S(1)}, bf16[768,768]{1,0:T(8,128)(2,1)}, u32[]{:S(2)}) copy-start(bf16[768,768]{1,0:T(8,128)(2,1)} %w_ref.1) | copy-start | bytes 3538948
  27.0 1.5 %collective-permute-start.4 = (bf16[768,128]{1,0:T(8,128)(2,1)S(1)}, bf16[768,128]{1,0:T(8,128)(2,1)S(1)}, u32[]{:S(2)}, u32[]{:S(2)}) collective-permute-start(bf16[768,128]{1,0:T(8,128)(2,1)S(1)} %get-tuple-element.36), channel_id=1, source_target_pairs={{0,1},{1,0},{2,3},{3,2},{4,5},{5,4},{6,7},{7,6},{8,9},{9,8},{10,11... | collective-permute-start | bytes 589832 | tf_op jit(solution)/shard_map/ppermute | solution.py:289
  30.6 7.0 %collective-permute-start.7 = (bf16[3,256,128]{2,1,0:T(8,128)(2,1)S(1)}, bf16[3,256,128]{2,1,0:T(8,128)(2,1)S(1)}, u32[]{:S(2)}, u32[]{:S(2)}) collective-permute-start(bf16[3,256,128]{2,1,0:T(8,128)(2,1)S(1)} %get-tuple-element.46), channel_id=1, source_target_pairs={{0,4},{4,0},{8,12},{12,8},{16,20},{20,16},{24,28},{28,24},{1,5},{5... | collective-permute-start | bytes 589832 | tf_op jit(solution)/shard_map/ppermute | solution.py:289
  31.6 10.6 %collective-permute-start.5 = (bf16[768,128]{1,0:T(8,128)(2,1)S(1)}, bf16[768,128]{1,0:T(8,128)(2,1)S(1)}, u32[]{:S(2)}, u32[]{:S(2)}) collective-permute-start(bf16[768,128]{1,0:T(8,128)(2,1)S(1)} %get-tuple-element.38), channel_id=1, source_target_pairs={{0,2},{1,3},{2,0},{3,1},{4,6},{5,7},{6,4},{7,5},{8,10},{9,11},{10,... | collective-permute-start | bytes 589832 | tf_op jit(solution)/shard_map/ppermute | solution.py:289
  33.1 9.1 %collective-permute-start.6 = (bf16[768,128]{1,0:T(8,128)(2,1)S(1)}, bf16[768,128]{1,0:T(8,128)(2,1)S(1)}, u32[]{:S(2)}, u32[]{:S(2)}) collective-permute-start(bf16[768,128]{1,0:T(8,128)(2,1)S(1)} %get-tuple-element.39), channel_id=1, source_target_pairs={{0,3},{1,2},{2,1},{3,0},{4,7},{5,6},{6,5},{7,4},{8,11},{9,10},{10,... | collective-permute-start | bytes 589832 | tf_op jit(solution)/shard_map/ppermute | solution.py:289
  40.0 3.5 %collective-permute-start.10 = (bf16[96,128]{1,0:T(8,128)(2,1)S(1)}, bf16[96,128]{1,0:T(8,128)(2,1)S(1)}, u32[]{:S(2)}, u32[]{:S(2)}) collective-permute-start(bf16[96,128]{1,0:T(8,128)(2,1)S(1)} %get-tuple-element.50), channel_id=1, source_target_pairs={{0,3},{1,2},{2,1},{3,0},{4,7},{5,6},{6,5},{7,4},{8,11},{9,10},{10,... | collective-permute-start | bytes 73736 | tf_op jit(solution)/shard_map/ppermute | solution.py:289
  40.5 3.0 %collective-permute-start.8 = (bf16[96,128]{1,0:T(8,128)(2,1)S(1)}, bf16[96,128]{1,0:T(8,128)(2,1)S(1)}, u32[]{:S(2)}, u32[]{:S(2)}) collective-permute-start(bf16[96,128]{1,0:T(8,128)(2,1)S(1)} %get-tuple-element.48), channel_id=1, source_target_pairs={{0,1},{1,0},{2,3},{3,2},{4,5},{5,4},{6,7},{7,6},{8,9},{9,8},{10,11... | collective-permute-start | bytes 73736 | tf_op jit(solution)/shard_map/ppermute | solution.py:289
  41.7 3.8 %collective-permute-start.9 = (bf16[96,128]{1,0:T(8,128)(2,1)S(1)}, bf16[96,128]{1,0:T(8,128)(2,1)S(1)}, u32[]{:S(2)}, u32[]{:S(2)}) collective-permute-start(bf16[96,128]{1,0:T(8,128)(2,1)S(1)} %get-tuple-element.49), channel_id=1, source_target_pairs={{0,2},{1,3},{2,0},{3,1},{4,6},{5,7},{6,4},{7,5},{8,10},{9,11},{10,... | collective-permute-start | bytes 73736 | tf_op jit(solution)/shard_map/ppermute | solution.py:289
where the time goes:
time: 48.3 us; the launch traced here: 48.1 us
  Pallas kernels  22.5 us (47%)
  starting transfers between devices  12.2 us (25%)
  waiting for transfers between devices  9.2 us (19%)
  local copies, waits for them, and re-layouts  4.09 us (8%)
    ppermute x11, starting transfers between devices, partner(): return lax.ppermute(block, axis, [(i, i ^ apart) for i in range(count)])  12.2 us
    ppermute x11, waiting for transfers between devices, partner(): return lax.ppermute(block, axis, [(i, i ^ apart) for i in range(count)])  9.2 us
    pallas_call x1, Pallas kernels, local(): call(local_kernel, 'local', [((heads, tok, LANES), F32)], [whole] * 3, qu...  7.57 us
    pallas_call x1, Pallas kernels, local(): call(functools.partial(pair_kernel, dils), 'pair', [((heads * width // 2,...  5.5 us
    unnamed x12, local copies, waits for them, and re-layouts  4.09 us
    pallas_call x1, Pallas kernels, local(): call(functools.partial(project_kernel, branches, dils[1]), 'project', [((...  2.57 us
    pallas_call x1, Pallas kernels, local(): call(functools.partial(select_kernel, dils), 'select', [(queries.shape, B...  2.41 us
    pallas_call x1, Pallas kernels, local(): call(functools.partial(patch_kernel, branches), 'patch', [(((branches + 1...  2.39 us
  transfers between devices with their start and end apart: 11, of which 5 were waited for; matrix products, arithmetic and copies ran while one was open for 0% of the time, Pallas kernels for 32%

commit v1 on v0

v1 whole, which is shorter than its diff:
```python
import functools
import math

import jax
import jax.numpy as jnp
from jax import lax
from jax.experimental import pallas as pl
from jax.experimental.pallas import tpu as pltpu
from jax.sharding import PartitionSpec as P

DH = 64
KEYS = 1024
LANES = 128
QBLK = 256
EXP2_SCALE = DH ** (-0.5) * math.log2(math.e)
NT = (((1,), (1,)), ((), ()))
NN = (((1,), (0,)), ((), ()))
VMEM_BYTES = 24 << 20
BF16, F32 = jnp.bfloat16, jnp.float32


def dot(a, b, dims):
    return lax.dot_general(a, b, dims, preferred_element_type=F32)


def lane_of(shape):
    return lax.broadcasted_iota(jnp.int32, shape, len(shape) - 1)


def in_values(shape, head):
    return (lane_of(shape) < DH) == (head % 2 == 0)


def stack_halves(values, others, head):
    return jnp.concatenate([values, others] if head % 2 == 0 else [others, values], 0)


def swap(rows):
    return pltpu.roll(rows, DH, 1)


def softmax_block(scores):
    row_max = jnp.max(scores, axis=1, keepdims=True)
    weights = jnp.exp2((scores - row_max) * EXP2_SCALE).astype(BF16)
    return row_max, weights


def merge_rows(cur, cur_max, new, new_max):
    both = jnp.maximum(cur_max, new_max)
    keep_cur = jnp.exp2((cur_max - both) * EXP2_SCALE)
    keep_new = jnp.exp2((new_max - both) * EXP2_SCALE)
    return both, cur * keep_cur + new * keep_new


def pack_pair(even, odd):
    low = lane_of(even.shape) < DH
    return jnp.where(low, even, odd) / swap(jnp.where(low, odd, even))


def pack_even(first, second):
    low = lane_of(first.shape) < DH
    return jnp.where(low, first, swap(second)) / jnp.where(low, swap(first), second)


def select_kernel(dils, off_hbm, q_hbm, k_hbm, v_hbm, q_ref, k_ref, v_ref, near_ref, far_ref, kvt, off_ref, sems, off_sem):
    heads = q_ref.shape[0] // DH
    tok = q_ref.shape[1]
    off_copy = pltpu.make_async_copy(off_hbm, off_ref, off_sem)
    off_copy.start()
    copies = []
    for h in range(heads):
        rows = pl.ds(h * DH, DH)
        for i, (src, dst) in enumerate(((k_hbm, k_ref), (v_hbm, v_ref))):
            copies.append(pltpu.make_async_copy(src.at[rows, :], dst.at[rows, :], sems.at[h, i]))
            copies[-1].start()
    q_copy = pltpu.make_async_copy(q_hbm, q_ref, sems.at[0, 2])
    q_copy.start()
    off_copy.wait()
    for h in range(heads):
        rows = slice(h * DH, (h + 1) * DH)
        head = lax.axis_index("head") * heads + h
        copies[2 * h].wait()
        copies[2 * h + 1].wait()
        kvt[h] = stack_halves(v_ref[rows, :], k_ref[rows, :], h).T.astype(F32)
        near_ref[h] = kvt[h, pl.ds(off_ref[0, head], tok // dils[0], stride=dils[0]), :].astype(BF16)
        for b in range(1, len(dils)):
            pick = pl.ds(off_ref[b, head], tok // dils[b], stride=dils[b])
            far_ref[b - 1, h] = kvt[h, pick, :].astype(BF16)
    q_copy.wait()


def query_kernel(dils, off_ref, q_ref, q1_ref, q23_ref, qt):
    heads = q_ref.shape[0] // DH
    tok = q_ref.shape[1]
    for h in range(heads):
        head = lax.axis_index("head") * heads + h
        query = q_ref[h * DH : (h + 1) * DH, :]
        qt[h] = stack_halves(jnp.zeros_like(query), query, h).T.astype(F32)
        picks = [pl.ds(off_ref[b, head], tok // d, stride=d) for b, d in enumerate(dils)]
        q1_ref[h] = qt[h, picks[0], :].astype(BF16)
        far_q = qt[h, picks[1], :]
        if len(dils) == 3:
            far_q = far_q + swap(qt[h, picks[2], :])
        q23_ref[h] = far_q.astype(BF16)


def local_kernel(q_ref, k_ref, v_ref, acc_ref, max_ref):
    tok = q_ref.shape[1]
    for h in range(q_ref.shape[0] // DH):
        rows = slice(h * DH, (h + 1) * DH)
        qt = q_ref[rows, :].T
        for seg in range(tok // KEYS):
            cols = slice(seg * KEYS, (seg + 1) * KEYS)
            keys = k_ref[rows, cols]
            vals = v_ref[rows, cols]
            vals = stack_halves(vals, jnp.ones_like(vals), h)
            for blk in range(KEYS // QBLK):
                at = seg * KEYS + blk * QBLK
                row_max, weights = softmax_block(dot(qt[at : at + QBLK], keys, NN))
                acc_ref[h, at : at + QBLK, :] = dot(weights, vals, NT)
                max_ref[h, at : at + QBLK, :] = jnp.broadcast_to(row_max, (QBLK, LANES))


def pair_kernel(dils, off_ref, q_ref, own_ref, other_ref, acc_in, max_in, m0, m1, m2, m3, cur_ref, top_ref, acc, top):
    heads, n1, _ = q_ref.shape
    tok = acc.shape[1]
    me = lax.axis_index("head")
    mains = (m0, m1, m2, m3)
    width = tok // len(mains)
    half = width // 2
    for h in range(heads):
        head = me * heads + h
        kv = jnp.concatenate([own_ref[h], other_ref[h]], 0)
        vals = jnp.where(in_values(kv.shape, h), kv, jnp.ones_like(kv))
        for blk in range(n1 // QBLK):
            rows = pl.ds(off_ref[0, head] + blk * QBLK * dils[0], QBLK, stride=dils[0])
            row_max, weights = softmax_block(dot(q_ref[h, blk * QBLK : (blk + 1) * QBLK], kv, NT))
            out = dot(weights, vals, NN)
            both, new = merge_rows(acc[h, rows, :], top[h, rows, :], out, row_max)
            acc[h, rows, :] = new
            top[h, rows, :] = both
        for b in range(1, len(dils)):
            pick = pl.ds(off_ref[b, head], tok // dils[b], stride=dils[b])
            cur_ref[b - 1, h] = acc[h, pick, :]
            top_ref[b - 1, h] = top[h, pick, :]
        for s, out in enumerate(mains):
            start = pl.multiple_of((me ^ s) * width, width)
            if h == 1:
                rows = pl.ds(start, width)
                out[:width, :] = pack_pair(acc[0, rows, :], acc[1, rows, :]).astype(BF16)
            elif h == 2:
                lo = acc[2, pl.ds(start, half), :]
                hi = acc[2, pl.ds(start + half, half), :]
                out[width:, :] = pack_even(lo, hi).astype(BF16)


def far_kernel(branches, q_own, q_other, kv0, kv1, kv2, kv3, part_ref, top_ref, send_ref):
    heads, n, _ = q_own.shape
    for h in range(heads):
        q_all = jnp.concatenate([q_own[h], q_other[h]], 0)
        outs, tops = [], []
        for b in range(branches):
            kv = jnp.concatenate([r[b, h] for r in (kv0, kv1, kv2, kv3)], 0)
            q_b = q_all if b == 0 else swap(q_all.astype(F32)).astype(BF16)
            q_b = jnp.where(in_values(q_b.shape, h), jnp.zeros_like(q_b), q_b)
            row_max, weights = softmax_block(dot(q_b, kv, NT))
            out = dot(weights, jnp.where(in_values(kv.shape, h), kv, jnp.ones_like(kv)), NN)
            part_ref[b, h] = out[:n]
            top_ref[b, h] = jnp.broadcast_to(row_max[:n], (n, LANES))
            outs.append(out[n:])
            tops.append(row_max[n:])
        a_lanes = in_values((n, LANES), h)
        other, other_top = (swap(outs[1]), tops[1]) if branches == 2 else (outs[0], tops[0])
        send_ref[h, :n, :] = jnp.where(a_lanes, outs[0], other).astype(BF16)
        slot = lane_of((n, LANES)) % DH
        stats = jnp.where(
            slot >= 3, jnp.where(a_lanes, other, outs[0]), jnp.where(a_lanes, other_top, tops[0])
        )
        high = stats.astype(BF16).astype(F32)
        mid = (stats - high).astype(BF16).astype(F32)
        low = stats - high - mid
        coded = jnp.where(slot % 3 == 0, high, jnp.where(slot % 3 == 1, mid, low))
        send_ref[h, n:, :] = coded.astype(BF16)


def patch_kernel(branches, off_ref, cur_ref, cur_top, part_ref, part_top, got_ref, p0, p1, p2, p3, packed):
    heads, two_n, _ = got_ref.shape
    n = two_n // 2
    me = lax.axis_index("head")
    patches = (p0, p1, p2, p3)
    size = n // len(patches)
    spread = []
    for parity in range(2):
        first = lax.broadcasted_iota(jnp.int32, (LANES, 4 * LANES), 0)
        kind = lax.broadcasted_iota(jnp.int32, (LANES, 4 * LANES), 1) // LANES
        base = jnp.where((kind // 2 == 0) == (parity == 0), DH, 0) + 3 * (kind % 2)
        spread.append(jnp.where((first >= base) & (first < base + 3), 1.0, 0.0).astype(BF16))
    done = []
    for h in range(heads):
        a_lanes = in_values((n, LANES), h)
        got = got_ref[h, :n, :].astype(F32)
        stats = dot(got_ref[h, n:, :], spread[h % 2], NN)
        states = []
        for b in range(branches):
            got_max = stats[:, 2 * b * LANES : (2 * b + 1) * LANES]
            got_sum = stats[:, (2 * b + 1) * LANES : (2 * b + 2) * LANES]
            new = jnp.where(a_lanes, got if b == 0 else swap(got), got_sum)
            states.append(merge_rows(part_ref[b, h], part_top[b, h], new, got_max))
        head = me * heads + h
        first_max, first = merge_rows(cur_ref[0, h], cur_top[0, h], states[0][1], states[0][0])
        merged = [first]
        if branches == 2:
            same = off_ref[1, head] == off_ref[2, head]
            base = jnp.where(same, first, cur_ref[1, h])
            base_max = jnp.where(same, first_max, cur_top[1, h])
            _, second = merge_rows(base, base_max, states[1][1], states[1][0])
            merged = [jnp.where(same, second, first), second]
        done.append(merged)
    for b in range(branches):
        packed[b] = pack_pair(done[0][b], done[1][b])
    packed[branches] = pack_even(done[2][0], done[2][-1])
    for s, out in enumerate(patches):
        start = pl.multiple_of((me ^ s) * size, size)
        for i in range(branches + 1):
            out[i * size : (i + 1) * size, :] = packed[i, pl.ds(start, size), :].astype(BF16)


def project_kernel(branches, dil, off_ref, x0, x1, x2, x3, p0, p1, p2, p3, w_ref, out_hbm, pairs, lasts, out_ref, sems):
    me = lax.axis_index("head")
    width = out_ref.shape[0]
    half = width // 2
    size = width // dil
    heads = 3
    rows = heads * DH
    sources = [me ^ s for s in range(4)]
    xs, ps = (x0, x1, x2, x3), (p0, p1, p2, p3)
    low = lane_of((size, LANES)) < DH
    for s in range(4):
        pairs[s] = xs[s][:width, :].astype(F32)
    for t in range(2):
        a = xs[2 * t][width:, :].astype(F32)
        b = xs[2 * t + 1][width:, :].astype(F32)
        lane = lane_of(a.shape)
        lasts[t, :half, :] = jnp.where(lane < DH, a, swap(b))
        lasts[t, half:, :] = jnp.where(lane < DH, swap(a), b)
    for s in range(4):
        for b in range(branches):
            new = ps[s][b * size : (b + 1) * size, :].astype(F32)
            for h in range(2):
                at = pl.ds(off_ref[b + 1, sources[s] * heads + h], size, stride=dil)
                pairs[s, at, :] = jnp.where(low == (h == 0), new, pairs[s, at, :])
            new = ps[s][branches * size :, :].astype(F32)
            if b != s % 2:
                new = swap(new)
            at = pl.ds(off_ref[b + 1, sources[s] * heads + 2], size, stride=dil)
            lasts[s // 2, at, :] = jnp.where(low == (s % 2 == 0), new, lasts[s // 2, at, :])

    def w_rows(s, start, count):
        return w_ref[pl.ds(pl.multiple_of(sources[s] * rows + start, DH), count), :]

    ws = [jnp.concatenate([w_rows(2 * t, 0, LANES), w_rows(2 * t + 1, 0, LANES)], 0) for t in range(2)]
    ws.append(jnp.concatenate([w_rows(s, LANES, DH) for s in range(4)], 0))
    copies = []
    step = width // 4
    for c in range(4):
        at = slice(c * step, (c + 1) * step)
        total = None
        for t in range(3):
            halves = (pairs[2 * t, at], pairs[2 * t + 1, at]) if t < 2 else (lasts[0, at], lasts[1, at])
            part = dot(jnp.concatenate(halves, 1).astype(BF16), ws[t], NN)
            total = part if total is None else total + part
        out_ref[at, :] = total.astype(BF16)
        copies.append(pltpu.make_async_copy(out_ref.at[pl.ds(c * step, step), :], out_hbm.at[pl.ds(c * step, step), :], sems.at[c]))
        copies[-1].start()
    for copy in copies:
        copy.wait()


def partner(block, axis, apart):
    count = lax.axis_size(axis)
    return lax.ppermute(block, axis, [(i, i ^ apart) for i in range(count)])


def call(kernel, name, outs, in_specs, scratch=(), queries=0, keys=0, aliases={}, space=pltpu.VMEM):
    estimate = None
    if queries:
        estimate = pl.CostEstimate(
            flops=queries * keys * 512, bytes_accessed=queries * 1024, transcendentals=queries * keys
        )
    return pl.pallas_call(
        kernel,
        out_shape=tuple(jax.ShapeDtypeStruct(*o) for o in outs),
        in_specs=in_specs,
        out_specs=(pl.BlockSpec(memory_space=space),) * len(outs),
        input_output_aliases=aliases,
        scratch_shapes=scratch,
        compiler_params=pltpu.CompilerParams(vmem_limit_bytes=VMEM_BYTES),
        cost_estimate=estimate,
        name=name,
    )


def spread_far(acc, top, query_h, key_h, value_h, dil, head_offsets):
    hit = jnp.arange(dil)[None, :] == head_offsets[:, None]

    def pick(x):
        shaped = x.reshape(x.shape[:2] + (x.shape[2] // dil, dil))
        return jnp.sum(shaped * hit[:, None, None, :].astype(x.dtype), axis=-1, dtype=x.dtype)

    pair = lax.all_gather(jnp.stack([pick(key_h), pick(value_h)], 0), "seq", axis=3, tiled=True)
    scores = jnp.einsum("hdq,hdk->hqk", pick(query_h), pair[0], preferred_element_type=F32)
    new_max = jnp.max(scores, axis=2, keepdims=True)
    e = jnp.exp2((scores - new_max) * EXP2_SCALE)
    new_sum = jnp.sum(e, axis=2, keepdims=True)
    new_acc = jnp.einsum("hqk,hdk->hqd", e.astype(BF16), pair[1], preferred_element_type=F32)
    heads, tok, _ = acc.shape
    shaped = acc.reshape(heads, tok // dil, dil, LANES)
    cur = jnp.sum(jnp.where(hit[:, None, :, None], shaped, 0.0), axis=2)
    sums = jnp.broadcast_to(new_sum, new_acc.shape)
    cur_top = jnp.sum(jnp.where(hit[:, None, :, None], top.reshape(shaped.shape), 0.0), axis=2)
    rows = []
    for h in range(heads):
        halves = [new_acc[h], sums[h]] if h % 2 == 0 else [sums[h], new_acc[h]]
        rows.append(merge_rows(cur[h], cur_top[h], jnp.concatenate(halves, 1), new_max[h]))

    def put(update, old):
        return jnp.where(hit[:, None, :, None], update[:, :, None, :], old).reshape(acc.shape)

    out_top, out = (jnp.stack(r, 0) for r in zip(*rows))
    return put(out, shaped), put(out_top, top.reshape(shaped.shape))


def local(queries, key_vectors, value_vectors, offsets, out_weight):
    tok = queries.shape[1]
    heads = queries.shape[0] // DH
    seq_count = lax.axis_size("seq")
    far_rate = tok * seq_count // KEYS
    dils = (4, 16, 16) if far_rate == 16 else (4, 16)
    branches = len(dils) - 1
    n1, n2 = tok // 4, tok // 16
    width = tok // 4
    whole = pl.BlockSpec(memory_space=pltpu.VMEM)
    smem = pl.BlockSpec(memory_space=pltpu.SMEM)
    hbm = pl.BlockSpec(memory_space=pltpu.HBM)
    far_shape = ((branches, heads, n2, LANES), F32)
    acc_shape = ((heads, tok, LANES), F32)

    stay = [
        pltpu.with_memory_space_constraint(a, pltpu.HBM) for a in (offsets, queries, key_vectors, value_vectors)
    ]
    q, k, v, near, far = call(
        functools.partial(select_kernel, dils),
        "select",
        [(queries.shape, BF16)] * 3 + [((heads, n1, LANES), BF16), ((branches, heads, n2, LANES), BF16)],
        [hbm] * 4,
        [
            pltpu.VMEM((heads, tok, LANES), F32),
            pltpu.SMEM(offsets.shape, jnp.int32),
            pltpu.SemaphoreType.DMA((heads, 3)),
            pltpu.SemaphoreType.DMA,
        ],
    )(*stay)
    fars = [far] + [partner(far, "seq", apart) for apart in (2, 4, 6)]
    near_other = partner(near, "seq", 1)

    q1, q23 = call(
        functools.partial(query_kernel, dils),
        "query",
        [((heads, n1, LANES), BF16), ((heads, n2, LANES), BF16)],
        [smem, whole],
        [pltpu.VMEM((heads, tok, LANES), F32)],
    )(offsets, q)
    q23_other = partner(q23, "seq", 1)

    acc, top = call(local_kernel, "local", [acc_shape] * 2, [whole] * 3, queries=heads * tok, keys=KEYS)(q, k, v)

    if branches == 1:
        shape = (heads, DH, tok)
        my_offsets = lax.dynamic_slice_in_dim(offsets[2], lax.axis_index("head") * heads, heads, 0)
        parts = [a.reshape(shape) for a in (queries, key_vectors, value_vectors)]
        acc, top = spread_far(acc, top, *parts, far_rate, my_offsets)

    acc, q23_other = lax.optimization_barrier((acc, q23_other))
    *mains, cur, cur_top, _, _ = call(
        functools.partial(pair_kernel, dils),
        "pair",
        [((heads * width // 2, LANES), BF16)] * 4 + [far_shape] * 2 + [acc_shape] * 2,
        [smem] + [whole] * 5,
        queries=heads * n1,
        keys=KEYS,
        aliases={4: 6, 5: 7},
    )(offsets, q1, near, near_other, acc, top)
    landed = [mains[0]] + [partner(mains[s], "head", s) for s in range(1, 4)]

    fars, cur, landed[1] = lax.optimization_barrier((fars, cur, landed[1]))
    part, part_top, send = call(
        functools.partial(far_kernel, branches),
        "far",
        [far_shape] * 2 + [((heads, 2 * n2, LANES), BF16)],
        [whole] * 6,
        queries=heads * n2 * 4,
        keys=KEYS // 2,
    )(q23, q23_other, *fars)
    got = partner(send, "seq", 1)

    patches = call(
        functools.partial(patch_kernel, branches),
        "patch",
        [(((branches + 1) * n2 // 4, LANES), BF16)] * 4,
        [smem] + [whole] * 5,
        [pltpu.VMEM((branches + 1, n2, LANES), F32)],
    )(offsets, cur, cur_top, part, part_top, got)
    fixes = [patches[0]] + [partner(patches[s], "head", s) for s in range(1, 4)]

    out_shape = (width, out_weight.shape[1])
    (out,) = call(
        functools.partial(project_kernel, branches, dils[1]),
        "project",
        [(out_shape, BF16)],
        [smem] + [whole] * 9,
        [
            pltpu.VMEM((4, width, LANES), F32),
            pltpu.VMEM((2, width, LANES), F32),
            pltpu.VMEM(out_shape, BF16),
            pltpu.SemaphoreType.DMA((4,)),
        ],
        space=pltpu.HBM,
    )(offsets, *landed, *fixes, out_weight)
    return out


def solution(mesh):
    in_specs = (P("head", "seq"), P("head", "seq"), P("head", "seq"), P(), P())
    out_specs = P(("seq", "head"), None)
    return jax.shard_map(local, mesh=mesh, in_specs=in_specs, out_specs=out_specs, check_vma=False)
```

time: 48.3 us -> 43.9 us (0.909)
  local copies, waits for them, and re-layouts: 4.09 us -> 0.69 us
  Pallas kernels: 22.5 us -> 21.1 us
  starting transfers between devices: 12.2 us -> 13.4 us
  waiting for transfers between devices: 9.2 us -> 8.3 us
    unnamed x12 -> x6, local copies, waits for them, and re-layouts: 4.09 us -> 0.69 us
    pallas_call x1, Pallas kernels: 2.39 us -> 1.21 us  [local(): call(functools.partial(patch_kernel, branches), 'patch', [(((branches + 1...]
    pallas_call x3 -> x4, Pallas kernels: 12.2 us -> 13.4 us  [the longest x1 7.5 us: local(): call(local_kernel, 'local', [acc_shape] * 2, [whole] * 3, queries=heads *...]
    ppermute x11 -> x12, starting transfers between devices: 12.2 us -> 13.4 us  [partner(): return lax.ppermute(block, axis, [(i, i ^ apart) for i in range(count)])]
    pallas_call x1, Pallas kernels: 5.5 us -> 4.52 us  [local(): call(functools.partial(pair_kernel, dils), 'pair', [((heads * width // 2,...]
    ppermute x11 -> x12, waiting for transfers between devices: 9.2 us -> 8.3 us  [partner(): return lax.ppermute(block, axis, [(i, i ^ apart) for i in range(count)])]
  transfers between devices with their start and end apart: 11 -> 12, of which waited for: 5 -> 5; matrix products, arithmetic and copies ran while one was open for 0% -> 0% of each run, Pallas kernels for 32% -> 33%
where the time goes in v1:
time: 43.9 us; the launch traced here: 43.7 us
  Pallas kernels  21.1 us (48%)
  starting transfers between devices  13.4 us (31%)
  waiting for transfers between devices  8.3 us (19%)
  local copies, waits for them, and re-layouts  0.69 us (2%)
    ppermute x12, starting transfers between devices, partner(): return lax.ppermute(block, axis, [(i, i ^ apart) for i in range(count)])  13.4 us
    ppermute x12, waiting for transfers between devices, partner(): return lax.ppermute(block, axis, [(i, i ^ apart) for i in range(count)])  8.3 us
    pallas_call x1, Pallas kernels, local(): call(local_kernel, 'local', [acc_shape] * 2, [whole] * 3, queries=heads *...  7.5 us
    pallas_call x1, Pallas kernels, local(): call(functools.partial(pair_kernel, dils), 'pair', [((heads * width // 2,...  4.52 us
    pallas_call x1, Pallas kernels, local(): call(functools.partial(project_kernel, branches, dils[1]), 'project', [(o...  2.5 us
    pallas_call x1, Pallas kernels, local(): call(functools.partial(far_kernel, branches), 'far', [far_shape] * 2 + [(...  2.04 us
    pallas_call x1, Pallas kernels, local(): call(functools.partial(select_kernel, dils), 'select', [(queries.shape, B...  2.01 us
    pallas_call x1, Pallas kernels, local(): call(functools.partial(query_kernel, dils), 'query', [((heads, n1, LANES)...  1.33 us
  transfers between devices with their start and end apart: 12, of which 5 were waited for; matrix products, arithmetic and copies ran while one was open for 0% of the time, Pallas kernels for 33%

profile of v1, /device:TPU:0, one launch (start us, length us, event | category | flops | bytes accessed | tf_op | source)
XLA Modules:
  0.0 43.7 jit_solution(9858402750620254456)
XLA Ops:
  0.0 2.0 %select.1 = (bf16[192,2048]{1,0:T(8,128)(2,1)S(1)}, bf16[192,2048]{1,0:T(8,128)(2,1)S(1)}, bf16[192,2048]{1,0:T(8,128)(2,1)S(1)}, bf16[3,512,128]{2,1,0:T(8,128)(2,1)S(1)}, bf16[2,3,128,128]{3,2,1,0:T(8,128)(2,1)S(1)}) custom-call(s32[3,12]{1,0:T(4,128)} %off_ref.7, bf16[192,2048]{1,0:T(8,128)(2,1)} %q_hbm.1, bf16[192,2048]{1,0:T(8,128)(2,1)} %k_hbm.1, ...), custom_call_target="tpu_custom_call" | custom-call | tf_op jit(solution)/shard_map/select/pallas_call | solution.py:351
  2.0 3.0 %collective-permute-start = (bf16[3,512,128]{2,1,0:T(8,128)(2,1)S(1)}, bf16[3,512,128]{2,1,0:T(8,128)(2,1)S(1)}, u32[]{:S(2)}, u32[]{:S(2)}) collective-permute-start(bf16[3,512,128]{2,1,0:T(8,128)(2,1)S(1)} %get-tuple-element.37.own_ref), channel_id=1, source_target_pairs={{0,4},{4,0},{8,12},{12,8},{16,20},{20,16},{24,28},{28,24},{1,5},{5... | collective-permute-start | bytes 1179656 | tf_op jit(solution)/shard_map/ppermute | solution.py:281
  5.0 1.6 %collective-permute-start.2 = (bf16[2,3,128,128]{3,2,1,0:T(8,128)(2,1)S(1)}, bf16[2,3,128,128]{3,2,1,0:T(8,128)(2,1)S(1)}, u32[]{:S(2)}, u32[]{:S(2)}) collective-permute-start(bf16[2,3,128,128]{3,2,1,0:T(8,128)(2,1)S(1)} %get-tuple-element.54.kv0), channel_id=1, source_target_pairs={{0,8},{4,12},{8,0},{12,4},{16,24},{20,28},{24,16},{28,20},{1,9},{5... | collective-permute-start | bytes 589832 | tf_op jit(solution)/shard_map/ppermute | solution.py:281
  6.6 2.6 %collective-permute-start.3 = (bf16[2,3,128,128]{3,2,1,0:T(8,128)(2,1)S(1)}, bf16[2,3,128,128]{3,2,1,0:T(8,128)(2,1)S(1)}, u32[]{:S(2)}, u32[]{:S(2)}) collective-permute-start(bf16[2,3,128,128]{3,2,1,0:T(8,128)(2,1)S(1)} %get-tuple-element.54.kv0), channel_id=1, source_target_pairs={{0,16},{4,20},{8,24},{12,28},{16,0},{20,4},{24,8},{28,12},{1,17},{... | collective-permute-start | bytes 589832 | tf_op jit(solution)/shard_map/ppermute | solution.py:281
  9.2 0.2 collective-permute-start.4
  9.4 0.7 %copy-done.1 = s32[3,12]{1,0:T(4,128)S(1)} copy-done((s32[3,12]{1,0:T(4,128)S(1)}, s32[3,12]{1,0:T(4,128)}, u32[]{:S(2)}) %copy-start.1) | copy-done | bytes 168
  10.1 1.3 %query.1 = (bf16[3,512,128]{2,1,0:T(8,128)(2,1)S(1)}, bf16[3,128,128]{2,1,0:T(8,128)(2,1)S(1)}) custom-call(s32[3,12]{1,0:T(4,128)S(1)} %copy-done.1, bf16[192,2048]{1,0:T(8,128)(2,1)S(1)} %get-tuple-element.35.q_ref), custom_call_target="tpu_custom_call" | custom-call | tf_op jit(solution)/shard_map/query/pallas_call | solution.py:366
  11.4 0.4 collective-permute-start.1
  11.8 7.5 %local.1 = (f32[3,2048,128]{2,1,0:T(8,128)S(1)}, f32[3,2048,128]{2,1,0:T(8,128)S(1)}) custom-call(bf16[192,2048]{1,0:T(8,128)(2,1)S(1)} %get-tuple-element.35.q_ref, bf16[192,2048]{1,0:T(8,128)(2,1)S(1)} %get-tuple-element.38.k_ref, bf16[192,2048]{1,0:T(8,128)(2,1)S(1)} %get-tuple-element.39.v_ref), custom_call_target="tpu_custom_call" | custom-call | flops 3221225472 | bytes 6291456 | tf_op jit(solution)/shard_map/local/pallas_call | solution.py:375
  19.3 0.0 copy-start.2
  19.3 4.5 %pair.1 = (bf16[768,128]{1,0:T(8,128)(2,1)S(1)}, bf16[768,128]{1,0:T(8,128)(2,1)S(1)}, bf16[768,128]{1,0:T(8,128)(2,1)S(1)}, bf16[768,128]{1,0:T(8,128)(2,1)S(1)...) custom-call(s32[3,12]{1,0:T(4,128)S(1)} %copy-done.1, ...), custom_call_target="tpu_custom_call", output_to_operand_aliasing={{6}: (4, {}), {7}: (5, {})} | custom-call | flops 805306368 | bytes 1572864 | tf_op jit(solution)/shard_map/pair/pallas_call | solution.py:384
  23.9 0.1 collective-permute-start.5
  24.0 1.4 %collective-permute-done.5.x1 = bf16[768,128]{1,0:T(8,128)(2,1)S(1)} collective-permute-done((bf16[768,128]{1,0:T(8,128)(2,1)S(1)}, bf16[768,128]{1,0:T(8,128)(2,1)S(1)}, u32[]{:S(2)}, u32[]{:S(2)}) %collective-permute-start.5) | collective-permute-done | bytes 196640 | tf_op jit(solution)/shard_map/ppermute | solution.py:281
  25.4 2.0 %far.1 = (f32[2,3,128,128]{3,2,1,0:T(8,128)S(1)}, f32[2,3,128,128]{3,2,1,0:T(8,128)S(1)}, bf16[3,256,128]{2,1,0:T(8,128)(2,1)S(1)}) custom-call(bf16[3,128,128]{2,1,0:T(8,128)(2,1)S(1)} %get-tuple-element.41.q_own, bf16[3,128,128]{2,1,0:T(8,128)(2,1)S(1)} %collective-permute-done.1.q_other, bf16[2,3,128,128]{3,2,1,0:T(8,128)(2,1)S(1)} %get-tuple-element.54.kv0, ...), custom_call_target="tpu_custom_call" | custom-call | flops 402653184 | bytes 1572864 | tf_op jit(solution)/shard_map/far/pallas_call | solution.py:396
  27.4 1.8 %collective-permute-start.8 = (bf16[3,256,128]{2,1,0:T(8,128)(2,1)S(1)}, bf16[3,256,128]{2,1,0:T(8,128)(2,1)S(1)}, u32[]{:S(2)}, u32[]{:S(2)}) collective-permute-start(bf16[3,256,128]{2,1,0:T(8,128)(2,1)S(1)} %get-tuple-element.60), channel_id=1, source_target_pairs={{0,4},{4,0},{8,12},{12,8},{16,20},{20,16},{24,28},{28,24},{1,5},{5... | collective-permute-start | bytes 589832 | tf_op jit(solution)/shard_map/ppermute | solution.py:281
  29.2 1.5 %collective-permute-start.6 = (bf16[768,128]{1,0:T(8,128)(2,1)S(1)}, bf16[768,128]{1,0:T(8,128)(2,1)S(1)}, u32[]{:S(2)}, u32[]{:S(2)}) collective-permute-start(bf16[768,128]{1,0:T(8,128)(2,1)S(1)} %get-tuple-element.49), channel_id=1, source_target_pairs={{0,2},{1,3},{2,0},{3,1},{4,6},{5,7},{6,4},{7,5},{8,10},{9,11},{10,... | collective-permute-start | bytes 589832 | tf_op jit(solution)/shard_map/ppermute | solution.py:281
  30.8 3.7 %collective-permute-done.8.got_ref = bf16[3,256,128]{2,1,0:T(8,128)(2,1)S(1)} collective-permute-done((bf16[3,256,128]{2,1,0:T(8,128)(2,1)S(1)}, bf16[3,256,128]{2,1,0:T(8,128)(2,1)S(1)}, u32[]{:S(2)}, u32[]{:S(2)}) %collective-permute-start.8) | collective-permute-done | bytes 196640 | tf_op jit(solution)/shard_map/ppermute | solution.py:281
  34.5 1.2 %patch.1 = (bf16[96,128]{1,0:T(8,128)(2,1)S(1)}, bf16[96,128]{1,0:T(8,128)(2,1)S(1)}, bf16[96,128]{1,0:T(8,128)(2,1)S(1)}, bf16[96,128]{1,0:T(8,128)(2,1)S(1)}) custom-call(s32[3,12]{1,0:T(4,128)S(1)} %copy-done.2, f32[2,3,128,128]{3,2,1,0:T(8,128)S(1)} %get-tuple-element.51.cur_ref, f32[2,3,128,128]{3,2,1,0:T(8,128)S(1)} %get-tuple-element.52.cur_top, ...), custom_call_target="tpu_custom_call" | custom-call | tf_op jit(solution)/shard_map/patch/pallas_call | solution.py:406
  35.7 1.8 %collective-permute-start.10 = (bf16[96,128]{1,0:T(8,128)(2,1)S(1)}, bf16[96,128]{1,0:T(8,128)(2,1)S(1)}, u32[]{:S(2)}, u32[]{:S(2)}) collective-permute-start(bf16[96,128]{1,0:T(8,128)(2,1)S(1)} %get-tuple-element.63), channel_id=1, source_target_pairs={{0,2},{1,3},{2,0},{3,1},{4,6},{5,7},{6,4},{7,5},{8,10},{9,11},{10,... | collective-permute-start | bytes 73736 | tf_op jit(solution)/shard_map/ppermute | solution.py:281
  37.5 0.4 collective-permute-start.9
  37.9 1.8 %collective-permute-done.7.x3 = bf16[768,128]{1,0:T(8,128)(2,1)S(1)} collective-permute-done((bf16[768,128]{1,0:T(8,128)(2,1)S(1)}, bf16[768,128]{1,0:T(8,128)(2,1)S(1)}, u32[]{:S(2)}, u32[]{:S(2)}) %collective-permute-start.7) | collective-permute-done | bytes 196640 | tf_op jit(solution)/shard_map/ppermute | solution.py:281
  39.7 1.0 %collective-permute-done.10.p2 = bf16[96,128]{1,0:T(8,128)(2,1)S(1)} collective-permute-done((bf16[96,128]{1,0:T(8,128)(2,1)S(1)}, bf16[96,128]{1,0:T(8,128)(2,1)S(1)}, u32[]{:S(2)}, u32[]{:S(2)}) %collective-permute-start.10) | collective-permute-done | bytes 24608 | tf_op jit(solution)/shard_map/ppermute | solution.py:281
  40.7 0.4 collective-permute-done.11.p3
  41.1 2.5 %project.1 = bf16[512,768]{1,0:T(8,128)(2,1)} custom-call(s32[3,12]{1,0:T(4,128)S(1)} %copy-done.2, bf16[768,128]{1,0:T(8,128)(2,1)S(1)} %get-tuple-element.44.x0, bf16[768,128]{1,0:T(8,128)(2,1)S(1)} %collective-permute-done.5.x1, bf16[768,128]{1,0:T(8,128)(2,1)S(1)} %collective-permute-done.6.x2, bf16[768,128]{1,0:T(8,128)(2,1)S(1)} %collective-permute-done.7.x3, ...), custom_call_target="tpu_custom_call" | custom-call | tf_op jit(solution)/shard_map/project/pallas_call | solution.py:416
  (13 shorter events, 0.0 us)
Async XLA Ops:
  2.0 17.3 %collective-permute-start = (bf16[3,512,128]{2,1,0:T(8,128)(2,1)S(1)}, bf16[3,512,128]{2,1,0:T(8,128)(2,1)S(1)}, u32[]{:S(2)}, u32[]{:S(2)}) collective-permute-start(bf16[3,512,128]{2,1,0:T(8,128)(2,1)S(1)} %get-tuple-element.37.own_ref), channel_id=1, source_target_pairs={{0,4},{4,0},{8,12},{12,8},{16,20},{20,16},{24,28},{28,24},{1,5},{5... | collective-permute-start | bytes 1179656 | tf_op jit(solution)/shard_map/ppermute | solution.py:281
  5.0 18.9 %collective-permute-start.2 = (bf16[2,3,128,128]{3,2,1,0:T(8,128)(2,1)S(1)}, bf16[2,3,128,128]{3,2,1,0:T(8,128)(2,1)S(1)}, u32[]{:S(2)}, u32[]{:S(2)}) collective-permute-start(bf16[2,3,128,128]{3,2,1,0:T(8,128)(2,1)S(1)} %get-tuple-element.54.kv0), channel_id=1, source_target_pairs={{0,8},{4,12},{8,0},{12,4},{16,24},{20,28},{24,16},{28,20},{1,9},{5... | collective-permute-start | bytes 589832 | tf_op jit(solution)/shard_map/ppermute | solution.py:281
  6.6 17.4 %collective-permute-start.3 = (bf16[2,3,128,128]{3,2,1,0:T(8,128)(2,1)S(1)}, bf16[2,3,128,128]{3,2,1,0:T(8,128)(2,1)S(1)}, u32[]{:S(2)}, u32[]{:S(2)}) collective-permute-start(bf16[2,3,128,128]{3,2,1,0:T(8,128)(2,1)S(1)} %get-tuple-element.54.kv0), channel_id=1, source_target_pairs={{0,16},{4,20},{8,24},{12,28},{16,0},{20,4},{24,8},{28,12},{1,17},{... | collective-permute-start | bytes 589832 | tf_op jit(solution)/shard_map/ppermute | solution.py:281
  9.2 14.8 %collective-permute-start.4 = (bf16[2,3,128,128]{3,2,1,0:T(8,128)(2,1)S(1)}, bf16[2,3,128,128]{3,2,1,0:T(8,128)(2,1)S(1)}, u32[]{:S(2)}, u32[]{:S(2)}) collective-permute-start(bf16[2,3,128,128]{3,2,1,0:T(8,128)(2,1)S(1)} %get-tuple-element.54.kv0), channel_id=1, source_target_pairs={{0,24},{4,28},{8,16},{12,20},{16,8},{20,12},{24,0},{28,4},{1,25},{... | collective-permute-start | bytes 589832 | tf_op jit(solution)/shard_map/ppermute | solution.py:281
  9.4 0.7 %copy-start.1 = (s32[3,12]{1,0:T(4,128)S(1)}, s32[3,12]{1,0:T(4,128)}, u32[]{:S(2)}) copy-start(s32[3,12]{1,0:T(4,128)} %off_ref.7) | copy-start | bytes 436
  11.4 7.9 %collective-permute-start.1 = (bf16[3,128,128]{2,1,0:T(8,128)(2,1)S(1)}, bf16[3,128,128]{2,1,0:T(8,128)(2,1)S(1)}, u32[]{:S(2)}, u32[]{:S(2)}) collective-permute-start(bf16[3,128,128]{2,1,0:T(8,128)(2,1)S(1)} %get-tuple-element.41.q_own), channel_id=1, source_target_pairs={{0,4},{4,0},{8,12},{12,8},{16,20},{20,16},{24,28},{28,24},{1,5},{5... | collective-permute-start | bytes 294920 | tf_op jit(solution)/shard_map/ppermute | solution.py:281
  19.3 15.1 %copy-start.2 = (s32[3,12]{1,0:T(4,128)S(1)}, s32[3,12]{1,0:T(4,128)}, u32[]{:S(2)}) copy-start(s32[3,12]{1,0:T(4,128)} %off_ref.7) | copy-start | bytes 436
  23.9 17.2 %copy-start = (bf16[768,768]{1,0:T(8,128)(2,1)S(1)}, bf16[768,768]{1,0:T(8,128)(2,1)}, u32[]{:S(2)}) copy-start(bf16[768,768]{1,0:T(8,128)(2,1)} %w_ref.1) | copy-start | bytes 3538948
  23.9 1.5 %collective-permute-start.5 = (bf16[768,128]{1,0:T(8,128)(2,1)S(1)}, bf16[768,128]{1,0:T(8,128)(2,1)S(1)}, u32[]{:S(2)}, u32[]{:S(2)}) collective-permute-start(bf16[768,128]{1,0:T(8,128)(2,1)S(1)} %get-tuple-element.47), channel_id=1, source_target_pairs={{0,1},{1,0},{2,3},{3,2},{4,5},{5,4},{6,7},{7,6},{8,9},{9,8},{10,11... | collective-permute-start | bytes 589832 | tf_op jit(solution)/shard_map/ppermute | solution.py:281
  27.4 7.0 %collective-permute-start.8 = (bf16[3,256,128]{2,1,0:T(8,128)(2,1)S(1)}, bf16[3,256,128]{2,1,0:T(8,128)(2,1)S(1)}, u32[]{:S(2)}, u32[]{:S(2)}) collective-permute-start(bf16[3,256,128]{2,1,0:T(8,128)(2,1)S(1)} %get-tuple-element.60), channel_id=1, source_target_pairs={{0,4},{4,0},{8,12},{12,8},{16,20},{20,16},{24,28},{28,24},{1,5},{5... | collective-permute-start | bytes 589832 | tf_op jit(solution)/shard_map/ppermute | solution.py:281
  29.2 8.7 %collective-permute-start.6 = (bf16[768,128]{1,0:T(8,128)(2,1)S(1)}, bf16[768,128]{1,0:T(8,128)(2,1)S(1)}, u32[]{:S(2)}, u32[]{:S(2)}) collective-permute-start(bf16[768,128]{1,0:T(8,128)(2,1)S(1)} %get-tuple-element.49), channel_id=1, source_target_pairs={{0,2},{1,3},{2,0},{3,1},{4,6},{5,7},{6,4},{7,5},{8,10},{9,11},{10,... | collective-permute-start | bytes 589832 | tf_op jit(solution)/shard_map/ppermute | solution.py:281
  30.8 8.9 %collective-permute-start.7 = (bf16[768,128]{1,0:T(8,128)(2,1)S(1)}, bf16[768,128]{1,0:T(8,128)(2,1)S(1)}, u32[]{:S(2)}, u32[]{:S(2)}) collective-permute-start(bf16[768,128]{1,0:T(8,128)(2,1)S(1)} %get-tuple-element.50), channel_id=1, source_target_pairs={{0,3},{1,2},{2,1},{3,0},{4,7},{5,6},{6,5},{7,4},{8,11},{9,10},{10,... | collective-permute-start | bytes 589832 | tf_op jit(solution)/shard_map/ppermute | solution.py:281
  35.7 5.0 %collective-permute-start.10 = (bf16[96,128]{1,0:T(8,128)(2,1)S(1)}, bf16[96,128]{1,0:T(8,128)(2,1)S(1)}, u32[]{:S(2)}, u32[]{:S(2)}) collective-permute-start(bf16[96,128]{1,0:T(8,128)(2,1)S(1)} %get-tuple-element.63), channel_id=1, source_target_pairs={{0,2},{1,3},{2,0},{3,1},{4,6},{5,7},{6,4},{7,5},{8,10},{9,11},{10,... | collective-permute-start | bytes 73736 | tf_op jit(solution)/shard_map/ppermute | solution.py:281
  37.5 3.6 %collective-permute-start.11 = (bf16[96,128]{1,0:T(8,128)(2,1)S(1)}, bf16[96,128]{1,0:T(8,128)(2,1)S(1)}, u32[]{:S(2)}, u32[]{:S(2)}) collective-permute-start(bf16[96,128]{1,0:T(8,128)(2,1)S(1)} %get-tuple-element.64), channel_id=1, source_target_pairs={{0,3},{1,2},{2,1},{3,0},{4,7},{5,6},{6,5},{7,4},{8,11},{9,10},{10,... | collective-permute-start | bytes 73736 | tf_op jit(solution)/shard_map/ppermute | solution.py:281
  37.5 3.6 %collective-permute-start.9 = (bf16[96,128]{1,0:T(8,128)(2,1)S(1)}, bf16[96,128]{1,0:T(8,128)(2,1)S(1)}, u32[]{:S(2)}, u32[]{:S(2)}) collective-permute-start(bf16[96,128]{1,0:T(8,128)(2,1)S(1)} %get-tuple-element.62), channel_id=1, source_target_pairs={{0,1},{1,0},{2,3},{3,2},{4,5},{5,4},{6,7},{7,6},{8,9},{9,8},{10,11... | collective-permute-start | bytes 73736 | tf_op jit(solution)/shard_map/ppermute | solution.py:281

commit v2 on v1

--- a/solution.py
+++ b/solution.py
@@ -15,7 +15,9 @@
 EXP2_SCALE = DH ** (-0.5) * math.log2(math.e)
 NT = (((1,), (1,)), ((), ()))
 NN = (((1,), (0,)), ((), ()))
+STATS = 16
 VMEM_BYTES = 24 << 20
+COVER = dict(select=6, query=4, local=25, far=1, pair=3, patch=5, arrange=4, project=6)
 BF16, F32 = jnp.bfloat16, jnp.float32
 
 
@@ -43,6 +45,15 @@
     row_max = jnp.max(scores, axis=1, keepdims=True)
     weights = jnp.exp2((scores - row_max) * EXP2_SCALE).astype(BF16)
     return row_max, weights
+
+
+def attend(items):
+    scores = items[0][0]()
+    for i, (_, values, sink) in enumerate(items):
+        ahead = items[i + 1][0]() if i + 1 < len(items) else None
+        row_max, weights = softmax_block(scores)
+        sink(row_max, values(weights))
+        scores = ahead
 
 
 def merge_rows(cur, cur_max, new, new_max):
@@ -89,13 +100,17 @@
     q_copy.wait()
 
 
-def query_kernel(dils, off_ref, q_ref, q1_ref, q23_ref, qt):
+def query_kernel(dils, off_hbm, q_ref, q1_ref, q23_ref, qt, off_ref, off_sem):
     heads = q_ref.shape[0] // DH
     tok = q_ref.shape[1]
+    copy = pltpu.make_async_copy(off_hbm, off_ref, off_sem)
+    copy.start()
     for h in range(heads):
         head = lax.axis_index("head") * heads + h
         query = q_ref[h * DH : (h + 1) * DH, :]
         qt[h] = stack_halves(jnp.zeros_like(query), query, h).T.astype(F32)
+        if h == 0:
+            copy.wait()
         picks = [pl.ds(off_ref[b, head], tok // d, stride=d) for b, d in enumerate(dils)]
         q1_ref[h] = qt[h, picks[0], :].astype(BF16)
         far_q = qt[h, picks[1], :]
@@ -104,102 +119,150 @@
         q23_ref[h] = far_q.astype(BF16)
 
 
-def local_kernel(q_ref, k_ref, v_ref, acc_ref, max_ref):
+def local_kernel(q_ref, k_ref, v_ref, acc_ref, max_ref, own_ref, core_ref, far_ref, qts):
+    heads = q_ref.shape[0] // DH
     tok = q_ref.shape[1]
-    for h in range(q_ref.shape[0] // DH):
+    width = tok // 4
+    half = width // 2
+    size = own_ref.shape[0]
+    me = lax.axis_index("head")
+    mains = (own_ref, core_ref, far_ref.at[:size, :], far_ref.at[size:, :])
+    items = []
+
+    def block(h, seg, keys, vals, s, part):
+        start = pl.multiple_of((me ^ s) * width + part * half, half)
+        at = pl.ds(start, half)
+
+        def sink(row_max, out):
+            acc_ref[h, at, :] = out
+            max_ref[h, at, :] = jnp.broadcast_to(row_max, out.shape)
+            if h == 1:
+                mains[s][part * half : (part + 1) * half, :] = pack_pair(acc_ref[0, at, :], out).astype(BF16)
+            elif h == 2 and part == 1:
+                first = acc_ref[2, pl.ds(start - half, half), :]
+                mains[s][width:, :] = pack_even(first, out).astype(BF16)
+
+        items.append((lambda: dot(qts[h, at, :], keys, NN), lambda weights: dot(weights, vals, NT), sink))
+
+    for h in range(heads):
         rows = slice(h * DH, (h + 1) * DH)
-        qt = q_ref[rows, :].T
-        for seg in range(tok // KEYS):
-            cols = slice(seg * KEYS, (seg + 1) * KEYS)
+        qts[h] = q_ref[rows, :].T
+        for pair in range(2):
+            cols = pl.ds(pl.multiple_of(((me // 2) ^ pair) * KEYS, KEYS), KEYS)
             keys = k_ref[rows, cols]
             vals = v_ref[rows, cols]
             vals = stack_halves(vals, jnp.ones_like(vals), h)
-            for blk in range(KEYS // QBLK):
-                at = seg * KEYS + blk * QBLK
-                row_max, weights = softmax_block(dot(qt[at : at + QBLK], keys, NN))
-                acc_ref[h, at : at + QBLK, :] = dot(weights, vals, NT)
-                max_ref[h, at : at + QBLK, :] = jnp.broadcast_to(row_max, (QBLK, LANES))
-
-
-def pair_kernel(dils, off_ref, q_ref, own_ref, other_ref, acc_in, max_in, m0, m1, m2, m3, cur_ref, top_ref, acc, top):
+            for s in (2 * pair, 2 * pair + 1):
+                for part in range(2):
+                    block(h, pair, keys, vals, s, part)
+    attend(items)
+
+
+def pair_kernel(dils, off_ref, q_ref, own_ref, other_ref, acc_in, max_in, p0, p1, p2, p3, cur_ref, top_ref, acc, top, merged):
     heads, n1, _ = q_ref.shape
     tok = acc.shape[1]
     me = lax.axis_index("head")
-    mains = (m0, m1, m2, m3)
-    width = tok // len(mains)
-    half = width // 2
-    for h in range(heads):
-        head = me * heads + h
+    patches = (p0, p1, p2, p3)
+    size = n1 // len(patches)
+    half = size // 2
+    items = []
+
+    def block(h, kv, vals, blk):
+        rows = pl.ds(off_ref[0, me * heads + h] + blk * QBLK * dils[0], QBLK, stride=dils[0])
+
+        def sink(row_max, out):
+            both, new = merge_rows(acc[h, rows, :], top[h, rows, :], out, row_max)
+            acc[h, rows, :] = new
+            top[h, rows, :] = both
+            merged[h, blk * QBLK : (blk + 1) * QBLK, :] = new
+            if (blk + 1) * QBLK == n1:
+                finish(h)
+
+        query = q_ref[h, blk * QBLK : (blk + 1) * QBLK]
+        items.append((lambda: dot(query, kv, NT), lambda weights: dot(weights, vals, NN), sink))
+
+    def finish(h):
+        for b in range(1, len(dils)):
+            pick = pl.ds(off_ref[b, me * heads + h], tok // dils[b], stride=dils[b])
+            cur_ref[b - 1, h] = acc[h, pick, :]
+            top_ref[b - 1, h] = top[h, pick, :]
+        for s, out in enumerate(patches):
+            start = pl.multiple_of((me ^ s) * size, size)
+            if h == 1:
+                rows = pl.ds(start, size)
+                out[:size, :] = pack_pair(merged[0, rows, :], merged[1, rows, :]).astype(BF16)
+            elif h == 2:
+                lo = merged[2, pl.ds(start, half), :]
+                hi = merged[2, pl.ds(start + half, half), :]
+                out[size : size + half, :] = pack_even(lo, hi).astype(BF16)
+
+    for h in range(heads):
         kv = jnp.concatenate([own_ref[h], other_ref[h]], 0)
         vals = jnp.where(in_values(kv.shape, h), kv, jnp.ones_like(kv))
         for blk in range(n1 // QBLK):
-            rows = pl.ds(off_ref[0, head] + blk * QBLK * dils[0], QBLK, stride=dils[0])
-            row_max, weights = softmax_block(dot(q_ref[h, blk * QBLK : (blk + 1) * QBLK], kv, NT))
-            out = dot(weights, vals, NN)
-            both, new = merge_rows(acc[h, rows, :], top[h, rows, :], out, row_max)
-            acc[h, rows, :] = new
-            top[h, rows, :] = both
-        for b in range(1, len(dils)):
-            pick = pl.ds(off_ref[b, head], tok // dils[b], stride=dils[b])
-            cur_ref[b - 1, h] = acc[h, pick, :]
-            top_ref[b - 1, h] = top[h, pick, :]
-        for s, out in enumerate(mains):
-            start = pl.multiple_of((me ^ s) * width, width)
-            if h == 1:
-                rows = pl.ds(start, width)
-                out[:width, :] = pack_pair(acc[0, rows, :], acc[1, rows, :]).astype(BF16)
-            elif h == 2:
-                lo = acc[2, pl.ds(start, half), :]
-                hi = acc[2, pl.ds(start + half, half), :]
-                out[width:, :] = pack_even(lo, hi).astype(BF16)
+            block(h, kv, vals, blk)
+    attend(items)
 
 
 def far_kernel(branches, q_own, q_other, kv0, kv1, kv2, kv3, part_ref, top_ref, send_ref):
     heads, n, _ = q_own.shape
-    for h in range(heads):
-        q_all = jnp.concatenate([q_own[h], q_other[h]], 0)
-        outs, tops = [], []
-        for b in range(branches):
-            kv = jnp.concatenate([r[b, h] for r in (kv0, kv1, kv2, kv3)], 0)
-            q_b = q_all if b == 0 else swap(q_all.astype(F32)).astype(BF16)
-            q_b = jnp.where(in_values(q_b.shape, h), jnp.zeros_like(q_b), q_b)
-            row_max, weights = softmax_block(dot(q_b, kv, NT))
-            out = dot(weights, jnp.where(in_values(kv.shape, h), kv, jnp.ones_like(kv)), NN)
+    a_lanes = [in_values((n, LANES), h) for h in range(2)]
+    items = []
+    held = {}
+
+    def block(h, b, query, kv, vals):
+        def sink(row_max, out):
             part_ref[b, h] = out[:n]
             top_ref[b, h] = jnp.broadcast_to(row_max[:n], (n, LANES))
-            outs.append(out[n:])
-            tops.append(row_max[n:])
-        a_lanes = in_values((n, LANES), h)
-        other, other_top = (swap(outs[1]), tops[1]) if branches == 2 else (outs[0], tops[0])
-        send_ref[h, :n, :] = jnp.where(a_lanes, outs[0], other).astype(BF16)
+            held[b] = out[n:], row_max[n:]
+            if b == branches - 1:
+                pack(h)
+
+        items.append((lambda: dot(query, kv, NT), lambda weights: dot(weights, vals, NN), sink))
+
+    def pack(h):
+        first, first_top = held[0]
+        other, other_top = held[branches - 1]
+        if branches == 2:
+            other = swap(other)
+        mine = a_lanes[h % 2]
+        send_ref[h, :n, :] = jnp.where(mine, first, other).astype(BF16)
         slot = lane_of((n, LANES)) % DH
-        stats = jnp.where(
-            slot >= 3, jnp.where(a_lanes, other, outs[0]), jnp.where(a_lanes, other_top, tops[0])
-        )
+        stats = jnp.where(slot >= 3, jnp.where(mine, other, first), jnp.where(mine, other_top, first_top))
         high = stats.astype(BF16).astype(F32)
         mid = (stats - high).astype(BF16).astype(F32)
         low = stats - high - mid
         coded = jnp.where(slot % 3 == 0, high, jnp.where(slot % 3 == 1, mid, low))
-        send_ref[h, n:, :] = coded.astype(BF16)
-
-
-def patch_kernel(branches, off_ref, cur_ref, cur_top, part_ref, part_top, got_ref, p0, p1, p2, p3, packed):
-    heads, two_n, _ = got_ref.shape
-    n = two_n // 2
+        coded = coded.T
+        send_ref[h, n : n + STATS, :] = coded[:STATS].astype(BF16)
+        send_ref[h, n + STATS :, :] = coded[DH : DH + STATS].astype(BF16)
+
+    for h in range(heads):
+        q_all = jnp.concatenate([q_own[h], q_other[h]], 0)
+        for b in range(branches):
+            kv = jnp.concatenate([r[b, h] for r in (kv0, kv1, kv2, kv3)], 0)
+            query = q_all if b == 0 else swap(q_all.astype(F32)).astype(BF16)
+            query = jnp.where(in_values(query.shape, h), jnp.zeros_like(query), query)
+            block(h, b, query, kv, jnp.where(in_values(kv.shape, h), kv, jnp.ones_like(kv)))
+    attend(items)
+
+
+def patch_kernel(branches, off_ref, cur_ref, cur_top, part_ref, part_top, got_ref, i0, i1, i2, i3, p0, p1, p2, p3, packed):
+    heads, n = cur_ref.shape[1:3]
     me = lax.axis_index("head")
     patches = (p0, p1, p2, p3)
     size = n // len(patches)
     spread = []
     for parity in range(2):
-        first = lax.broadcasted_iota(jnp.int32, (LANES, 4 * LANES), 0)
-        kind = lax.broadcasted_iota(jnp.int32, (LANES, 4 * LANES), 1) // LANES
-        base = jnp.where((kind // 2 == 0) == (parity == 0), DH, 0) + 3 * (kind % 2)
+        first = lax.broadcasted_iota(jnp.int32, (2 * STATS, 4 * LANES), 0)
+        kind = lax.broadcasted_iota(jnp.int32, (2 * STATS, 4 * LANES), 1) // LANES
+        base = jnp.where((kind // 2 == 0) == (parity == 0), STATS, 0) + 3 * (kind % 2)
         spread.append(jnp.where((first >= base) & (first < base + 3), 1.0, 0.0).astype(BF16))
     done = []
     for h in range(heads):
         a_lanes = in_values((n, LANES), h)
         got = got_ref[h, :n, :].astype(F32)
-        stats = dot(got_ref[h, n:, :], spread[h % 2], NN)
+        stats = dot(got_ref[h, n:, :], spread[h % 2], (((0,), (0,)), ((), ())))
         states = []
         for b in range(branches):
             got_max = stats[:, 2 * b * LANES : (2 * b + 1) * LANES]
@@ -221,20 +284,16 @@
     packed[branches] = pack_even(done[2][0], done[2][-1])
     for s, out in enumerate(patches):
         start = pl.multiple_of((me ^ s) * size, size)
+        base = out.shape[0] - (branches + 1) * size
         for i in range(branches + 1):
-            out[i * size : (i + 1) * size, :] = packed[i, pl.ds(start, size), :].astype(BF16)
-
-
-def project_kernel(branches, dil, off_ref, x0, x1, x2, x3, p0, p1, p2, p3, w_ref, out_hbm, pairs, lasts, out_ref, sems):
-    me = lax.axis_index("head")
-    width = out_ref.shape[0]
+            out[base + i * size : base + (i + 1) * size, :] = packed[i, pl.ds(start, size), :].astype(BF16)
+
+
+def arrange_kernel(x0, x1, x2, x3, pairs, lasts):
+    count = x0.shape[0]
+    width = pairs.shape[1]
     half = width // 2
-    size = width // dil
-    heads = 3
-    rows = heads * DH
-    sources = [me ^ s for s in range(4)]
-    xs, ps = (x0, x1, x2, x3), (p0, p1, p2, p3)
-    low = lane_of((size, LANES)) < DH
+    xs = (x0, x1, x2.at[:count, :], x3.at[count:, :])
     for s in range(4):
         pairs[s] = xs[s][:width, :].astype(F32)
     for t in range(2):
@@ -243,17 +302,43 @@
         lane = lane_of(a.shape)
         lasts[t, :half, :] = jnp.where(lane < DH, a, swap(b))
         lasts[t, half:, :] = jnp.where(lane < DH, swap(a), b)
+
+
+def project_kernel(dils, off_ref, pairs_in, lasts_in, p0, p1, p2, p3, w_ref, out_hbm, pairs, lasts, out_ref, sems):
+    me = lax.axis_index("head")
+    width = out_ref.shape[0]
+    branches = len(dils) - 1
+    near = width // dils[0]
+    size = width // dils[1]
+    heads = 3
+    rows = heads * DH
+    sources = [me ^ s for s in range(4)]
+    ps = (p0, p1, p2, p3)
+
+    def put(ref, index, branch, source, h, first, new, in_low):
+        dil = dils[branch]
+        at = pl.ds(off_ref[branch, sources[source] * heads + h] + first * dil, new.shape[0], stride=dil)
+        old = ref[index, at, :]
+        ref[index, at, :] = jnp.where((lane_of(new.shape) < DH) == in_low, new, old)
+
     for s in range(4):
+        in_low = s % 2 == 0
+        new = ps[s][:near, :].astype(F32)
+        for h in range(2):
+            put(pairs, s, 0, s, h, 0, new, h == 0)
+        new = ps[s][near : near + near // 2, :].astype(F32)
+        turned = swap(new)
+        put(lasts, s // 2, 0, s, 2, 0, new if in_low else turned, in_low)
+        put(lasts, s // 2, 0, s, 2, near // 2, turned if in_low else new, in_low)
+        base = near + near // 2
         for b in range(branches):
-            new = ps[s][b * size : (b + 1) * size, :].astype(F32)
+            new = ps[s][base + b * size : base + (b + 1) * size, :].astype(F32)
             for h in range(2):
-                at = pl.ds(off_ref[b + 1, sources[s] * heads + h], size, stride=dil)
-                pairs[s, at, :] = jnp.where(low == (h == 0), new, pairs[s, at, :])
-            new = ps[s][branches * size :, :].astype(F32)
+                put(pairs, s, b + 1, s, h, 0, new, h == 0)
+            new = ps[s][base + branches * size :, :].astype(F32)
             if b != s % 2:
                 new = swap(new)
-            at = pl.ds(off_ref[b + 1, sources[s] * heads + 2], size, stride=dil)
-            lasts[s // 2, at, :] = jnp.where(low == (s % 2 == 0), new, lasts[s // 2, at, :])
+            put(lasts, s // 2, b + 1, s, 2, 0, new, in_low)
 
     def w_rows(s, start, count):
         return w_ref[pl.ds(pl.multiple_of(sources[s] * rows + start, DH), count), :]
@@ -281,17 +366,13 @@
     return lax.ppermute(block, axis, [(i, i ^ apart) for i in range(count)])
 
 
-def call(kernel, name, outs, in_specs, scratch=(), queries=0, keys=0, aliases={}, space=pltpu.VMEM):
-    estimate = None
-    if queries:
-        estimate = pl.CostEstimate(
-            flops=queries * keys * 512, bytes_accessed=queries * 1024, transcendentals=queries * keys
-        )
+def call(kernel, name, outs, in_specs, scratch=(), aliases={}, spaces=None):
+    estimate = pl.CostEstimate(flops=int(COVER[name] * 1e9), bytes_accessed=1024, transcendentals=0)
     return pl.pallas_call(
         kernel,
         out_shape=tuple(jax.ShapeDtypeStruct(*o) for o in outs),
         in_specs=in_specs,
-        out_specs=(pl.BlockSpec(memory_space=space),) * len(outs),
+        out_specs=tuple(pl.BlockSpec(memory_space=m) for m in spaces or (pltpu.VMEM,) * len(outs)),
         input_output_aliases=aliases,
         scratch_shapes=scratch,
         compiler_params=pltpu.CompilerParams(vmem_limit_bytes=VMEM_BYTES),
@@ -328,6 +409,22 @@
 
     out_top, out = (jnp.stack(r, 0) for r in zip(*rows))
     return put(out, shaped), put(out_top, top.reshape(shaped.shape))
+
+
+def packed_mains(acc):
+    heads, tok, _ = acc.shape
+    width = tok // 4
+    me = lax.axis_index("head")
+    rows = []
+    for h in range(heads):
+        low, high = acc[h, :, :DH], acc[h, :, DH:]
+        rows.append(low / high if h % 2 == 0 else high / low)
+    blocks = []
+    for s in range(4):
+        mine = [lax.dynamic_slice_in_dim(r, (me ^ s) * width, width, 0) for r in rows]
+        last = jnp.concatenate([mine[2][: width // 2], mine[2][width // 2 :]], 1)
+        blocks.append(jnp.concatenate([jnp.concatenate(mine[:2], 1), last], 0).astype(BF16))
+    return blocks[0], blocks[1], jnp.concatenate(blocks[2:], 0)
 
 
 def local(queries, key_vectors, value_vectors, offsets, out_weight):
@@ -367,65 +464,81 @@
         functools.partial(query_kernel, dils),
         "query",
         [((heads, n1, LANES), BF16), ((heads, n2, LANES), BF16)],
-        [smem, whole],
-        [pltpu.VMEM((heads, tok, LANES), F32)],
-    )(offsets, q)
+        [hbm, whole],
+        [
+            pltpu.VMEM((heads, tok, LANES), F32),
+            pltpu.SMEM(offsets.shape, jnp.int32),
+            pltpu.SemaphoreType.DMA,
+        ],
+    )(stay[0], q)
     q23_other = partner(q23, "seq", 1)
 
-    acc, top = call(local_kernel, "local", [acc_shape] * 2, [whole] * 3, queries=heads * tok, keys=KEYS)(q, k, v)
+    q, q23 = lax.optimization_barrier((q, q23))
+    main = heads * width // 2
+    acc, top, m_own, m_core, m_far = call(
+        local_kernel,
+        "local",
+        [acc_shape] * 2 + [((main, LANES), BF16)] * 2 + [((2 * main, LANES), BF16)],
+        [whole] * 3,
+        [pltpu.VMEM((heads, tok, DH), BF16)],
+    )(q, k, v)
 
     if branches == 1:
         shape = (heads, DH, tok)
         my_offsets = lax.dynamic_slice_in_dim(offsets[2], lax.axis_index("head") * heads, heads, 0)
         parts = [a.reshape(shape) for a in (queries, key_vectors, value_vectors)]
         acc, top = spread_far(acc, top, *parts, far_rate, my_offsets)
-
-    acc, q23_other = lax.optimization_barrier((acc, q23_other))
-    *mains, cur, cur_top, _, _ = call(
-        functools.partial(pair_kernel, dils),
-        "pair",
-        [((heads * width // 2, LANES), BF16)] * 4 + [far_shape] * 2 + [acc_shape] * 2,
-        [smem] + [whole] * 5,
-        queries=heads * n1,
-        keys=KEYS,
-        aliases={4: 6, 5: 7},
-    )(offsets, q1, near, near_other, acc, top)
-    landed = [mains[0]] + [partner(mains[s], "head", s) for s in range(1, 4)]
-
-    fars, cur, landed[1] = lax.optimization_barrier((fars, cur, landed[1]))
+        m_own, m_core, m_far = packed_mains(acc)
+
+    m_far, q23_other = lax.optimization_barrier((m_far, q23_other))
+    y_in = partner(m_far, "head", 2)
+    core_in = partner(m_core, "head", 1)
+
+    patch_rows = n1 // 4 * 3 // 2 + (branches + 1) * n2 // 4
+    fars, acc = lax.optimization_barrier((fars, acc))
     part, part_top, send = call(
         functools.partial(far_kernel, branches),
         "far",
-        [far_shape] * 2 + [((heads, 2 * n2, LANES), BF16)],
+        [far_shape] * 2 + [((heads, n2 + 2 * STATS, LANES), BF16)],
         [whole] * 6,
-        queries=heads * n2 * 4,
-        keys=KEYS // 2,
     )(q23, q23_other, *fars)
+    acc, part = lax.optimization_barrier((acc, part))
+    *patches, cur, cur_top, _, _ = call(
+        functools.partial(pair_kernel, dils),
+        "pair",
+        [((patch_rows, LANES), BF16)] * 4 + [far_shape] * 2 + [acc_shape] * 2,
+        [smem] + [whole] * 5,
+        [pltpu.VMEM((heads, n1, LANES), F32)],
+        aliases={4: 6, 5: 7},
+    )(offsets, q1, near, near_other, acc, top)
     got = partner(send, "seq", 1)
+    cur, y_in = lax.optimization_barrier((cur, y_in))
+    y_core = partner(y_in, "head", 1)
 
     patches = call(
         functools.partial(patch_kernel, branches),
         "patch",
-        [(((branches + 1) * n2 // 4, LANES), BF16)] * 4,
-        [smem] + [whole] * 5,
+        [((patch_rows, LANES), BF16)] * 4,
+        [smem] + [whole] * 9,
         [pltpu.VMEM((branches + 1, n2, LANES), F32)],
-    )(offsets, cur, cur_top, part, part_top, got)
+        aliases={6: 0, 7: 1, 8: 2, 9: 3},
+    )(offsets, cur, cur_top, part, part_top, got, *patches)
     fixes = [patches[0]] + [partner(patches[s], "head", s) for s in range(1, 4)]
 
     out_shape = (width, out_weight.shape[1])
-    (out,) = call(
-        functools.partial(project_kernel, branches, dils[1]),
+    spread_shapes = [((4, width, LANES), F32), ((2, width, LANES), F32)]
+    pairs, lasts = call(arrange_kernel, "arrange", spread_shapes, [whole] * 4)(
+        m_own, core_in, y_in, y_core
+    )
+    out, _, _ = call(
+        functools.partial(project_kernel, dils),
         "project",
-        [(out_shape, BF16)],
-        [smem] + [whole] * 9,
-        [
-            pltpu.VMEM((4, width, LANES), F32),
-            pltpu.VMEM((2, width, LANES), F32),
-            pltpu.VMEM(out_shape, BF16),
-            pltpu.SemaphoreType.DMA((4,)),
-        ],
-        space=pltpu.HBM,
-    )(offsets, *landed, *fixes, out_weight)
+        [(out_shape, BF16)] + spread_shapes,
+        [smem] + [whole] * 7,
+        [pltpu.VMEM(out_shape, BF16), pltpu.SemaphoreType.DMA((4,))],
+        aliases={1: 1, 2: 2},
+        spaces=(pltpu.HBM, pltpu.VMEM, pltpu.VMEM),
+    )(offsets, pairs, lasts, *fixes, out_weight)
     return out
 
 

time: 43.9 us -> 41.1 us (0.936)
  Pallas kernels: 21.1 us -> 20 us
  local copies, waits for them, and re-layouts: 0.69 us -> 0.01 us
  waiting for transfers between devices: 8.3 us -> 7.64 us
    unnamed x6 -> x4, local copies, waits for them, and re-layouts: 0.69 us -> 0.01 us
    ppermute x12, waiting for transfers between devices: 8.3 us -> 7.64 us  [partner(): return lax.ppermute(block, axis, [(i, i ^ apart) for i in range(count)])]
    pallas_call x1, Pallas kernels: 2.04 us -> 1.42 us  [local(): call(functools.partial(far_kernel, branches), 'far', [far_shape] * 2 + [(...]
    pallas_call x4 -> x5, Pallas kernels: 15.7 us -> 15.3 us  [the longest x1 7.82 us: local(): call(local_kernel, 'local', [acc_shape] * 2 + [((main, LANES), BF16)] * 2...]
  transfers between devices with their start and end apart: 12 -> 12, of which waited for: 5 -> 4; matrix products, arithmetic and copies ran while one was open for 0% -> 0% of each run, Pallas kernels for 33% -> 38%
where the time goes in v2:
time: 41.1 us; the launch traced here: 41 us
  Pallas kernels  20 us (49%)
  starting transfers between devices  13.1 us (32%)
  waiting for transfers between devices  7.64 us (19%)
    ppermute x12, starting transfers between devices, partner(): return lax.ppermute(block, axis, [(i, i ^ apart) for i in range(count)])  13.1 us
    pallas_call x1, Pallas kernels, local(): call(local_kernel, 'local', [acc_shape] * 2 + [((main, LANES), BF16)] * 2...  7.82 us
    ppermute x12, waiting for transfers between devices, partner(): return lax.ppermute(block, axis, [(i, i ^ apart) for i in range(count)])  7.64 us
    pallas_call x1, Pallas kernels, local(): call(functools.partial(pair_kernel, dils), 'pair', [((patch_rows, LANES),...  3.58 us
    pallas_call x1, Pallas kernels, local(): call(functools.partial(project_kernel, dils), 'project', [(out_shape, BF1...  2.54 us
    pallas_call x1, Pallas kernels, local(): call(functools.partial(select_kernel, dils), 'select', [(queries.shape, B...  2.01 us
    pallas_call x1, Pallas kernels, local(): call(functools.partial(far_kernel, branches), 'far', [far_shape] * 2 + [(...  1.42 us
    pallas_call x1, Pallas kernels, local(): call(functools.partial(query_kernel, dils), 'query', [((heads, n1, LANES)...  1.31 us
  transfers between devices with their start and end apart: 12, of which 4 were waited for; matrix products, arithmetic and copies ran while one was open for 0% of the time, Pallas kernels for 38%

profile of v2, /device:TPU:0, one launch (start us, length us, event | category | flops | bytes accessed | tf_op | source)
XLA Modules:
  0.0 41.0 jit_solution(3902095879104338778)
XLA Ops:
  0.0 2.0 %select.1 = (bf16[192,2048]{1,0:T(8,128)(2,1)S(1)}, bf16[192,2048]{1,0:T(8,128)(2,1)S(1)}, bf16[192,2048]{1,0:T(8,128)(2,1)S(1)}, bf16[3,512,128]{2,1,0:T(8,128)(2,1)S(1)}, bf16[2,3,128,128]{3,2,1,0:T(8,128)(2,1)S(1)}) custom-call(s32[3,12]{1,0:T(4,128)} %off_ref.5, bf16[192,2048]{1,0:T(8,128)(2,1)} %q_hbm.1, bf16[192,2048]{1,0:T(8,128)(2,1)} %k_hbm.1, ...), custom_call_target="tpu_custom_call" | custom-call | flops 6000000000 | bytes 1024 | tf_op jit(solution)/shard_map/select/pallas_call | solution.py:448
  2.0 5.1 %collective-permute-start.4 = (bf16[2,3,128,128]{3,2,1,0:T(8,128)(2,1)S(1)}, bf16[2,3,128,128]{3,2,1,0:T(8,128)(2,1)S(1)}, u32[]{:S(2)}, u32[]{:S(2)}) collective-permute-start(bf16[2,3,128,128]{3,2,1,0:T(8,128)(2,1)S(1)} %get-tuple-element.61.kv0), channel_id=1, source_target_pairs={{0,24},{4,28},{8,16},{12,20},{16,8},{20,12},{24,0},{28,4},{1,25},{... | collective-permute-start | bytes 589832 | tf_op jit(solution)/shard_map/ppermute | solution.py:366
  7.1 0.6 %collective-permute-start.2 = (bf16[2,3,128,128]{3,2,1,0:T(8,128)(2,1)S(1)}, bf16[2,3,128,128]{3,2,1,0:T(8,128)(2,1)S(1)}, u32[]{:S(2)}, u32[]{:S(2)}) collective-permute-start(bf16[2,3,128,128]{3,2,1,0:T(8,128)(2,1)S(1)} %get-tuple-element.61.kv0), channel_id=1, source_target_pairs={{0,8},{4,12},{8,0},{12,4},{16,24},{20,28},{24,16},{28,20},{1,9},{5... | collective-permute-start | bytes 589832 | tf_op jit(solution)/shard_map/ppermute | solution.py:366
  7.8 1.6 %collective-permute-start.1 = (bf16[3,512,128]{2,1,0:T(8,128)(2,1)S(1)}, bf16[3,512,128]{2,1,0:T(8,128)(2,1)S(1)}, u32[]{:S(2)}, u32[]{:S(2)}) collective-permute-start(bf16[3,512,128]{2,1,0:T(8,128)(2,1)S(1)} %get-tuple-element.54.own_ref), channel_id=1, source_target_pairs={{0,4},{4,0},{8,12},{12,8},{16,20},{20,16},{24,28},{28,24},{1,5},{5... | collective-permute-start | bytes 1179656 | tf_op jit(solution)/shard_map/ppermute | solution.py:366
  9.4 1.3 %query.1 = (bf16[3,512,128]{2,1,0:T(8,128)(2,1)S(1)}, bf16[3,128,128]{2,1,0:T(8,128)(2,1)S(1)}) custom-call(s32[3,12]{1,0:T(4,128)} %off_ref.5, bf16[192,2048]{1,0:T(8,128)(2,1)S(1)} %get-tuple-element.48.q_ref), custom_call_target="tpu_custom_call" | custom-call | flops 4000000000 | bytes 1024 | tf_op jit(solution)/shard_map/query/pallas_call | solution.py:463
  10.7 0.5 %collective-permute-start.5 = (bf16[3,128,128]{2,1,0:T(8,128)(2,1)S(1)}, bf16[3,128,128]{2,1,0:T(8,128)(2,1)S(1)}, u32[]{:S(2)}, u32[]{:S(2)}) collective-permute-start(bf16[3,128,128]{2,1,0:T(8,128)(2,1)S(1)} %get-tuple-element.58.q_own), channel_id=1, source_target_pairs={{0,4},{4,0},{8,12},{12,8},{16,20},{20,16},{24,28},{28,24},{1,5},{5... | collective-permute-start | bytes 294920 | tf_op jit(solution)/shard_map/ppermute | solution.py:366
  11.2 7.8 %local.1 = (f32[3,2048,128]{2,1,0:T(8,128)S(1)}, f32[3,2048,128]{2,1,0:T(8,128)S(1)}, bf16[768,128]{1,0:T(8,128)(2,1)S(1)}, bf16[768,128]{1,0:T(8,128)(2,1)S(1)}, bf16[1536,128]{1,0:T(8,128)(2,1)S(1)}) custom-call(bf16[192,2048]{1,0:T(8,128)(2,1)S(1)} %get-tuple-element.48.q_ref, bf16[192,2048]{1,0:T(8,128)(2,1)S(1)} %get-tuple-element.49.k_ref, ...), custom_call_target="tpu_custom_call" | custom-call | flops 24999999488 | bytes 1024 | tf_op jit(solution)/shard_map/local/pallas_call | solution.py:478
  19.0 0.0 copy-start.1
  19.0 1.2 %collective-permute-done.5.q_other = bf16[3,128,128]{2,1,0:T(8,128)(2,1)S(1)} collective-permute-done((bf16[3,128,128]{2,1,0:T(8,128)(2,1)S(1)}, bf16[3,128,128]{2,1,0:T(8,128)(2,1)S(1)}, u32[]{:S(2)}, u32[]{:S(2)}) %collective-permute-start.5) | collective-permute-done | bytes 98336 | tf_op jit(solution)/shard_map/ppermute | solution.py:366
  20.2 1.5 %collective-permute-start.6 = (bf16[1536,128]{1,0:T(8,128)(2,1)S(1)}, bf16[1536,128]{1,0:T(8,128)(2,1)S(1)}, u32[]{:S(2)}, u32[]{:S(2)}) collective-permute-start(bf16[1536,128]{1,0:T(8,128)(2,1)S(1)} %get-tuple-element.69), channel_id=1, source_target_pairs={{0,2},{1,3},{2,0},{3,1},{4,6},{5,7},{6,4},{7,5},{8,10},{9,11},{10,... | collective-permute-start | bytes 1179656 | tf_op jit(solution)/shard_map/ppermute | solution.py:366
  21.7 2.1 %collective-permute-done.3.kv2 = bf16[2,3,128,128]{3,2,1,0:T(8,128)(2,1)S(1)} collective-permute-done((bf16[2,3,128,128]{3,2,1,0:T(8,128)(2,1)S(1)}, bf16[2,3,128,128]{3,2,1,0:T(8,128)(2,1)S(1)}, u32[]{:S(2)}, u32[]{:S(2)}) %collective-permute-start.3) | collective-permute-done | bytes 196640 | tf_op jit(solution)/shard_map/ppermute | solution.py:366
  23.8 1.4 %far.1 = (f32[2,3,128,128]{3,2,1,0:T(8,128)S(1)}, f32[2,3,128,128]{3,2,1,0:T(8,128)S(1)}, bf16[3,160,128]{2,1,0:T(8,128)(2,1)S(1)}) custom-call(bf16[3,128,128]{2,1,0:T(8,128)(2,1)S(1)} %get-tuple-element.58.q_own, bf16[3,128,128]{2,1,0:T(8,128)(2,1)S(1)} %collective-permute-done.5.q_other, bf16[2,3,128,128]{3,2,1,0:T(8,128)(2,1)S(1)} %get-tuple-element.61.kv0, ...), custom_call_target="tpu_custom_call" | custom-call | flops 1000000000 | bytes 1024 | tf_op jit(solution)/shard_map/far/pallas_call | solution.py:499
  25.2 1.6 %collective-permute-start.8 = (bf16[3,160,128]{2,1,0:T(8,128)(2,1)S(1)}, bf16[3,160,128]{2,1,0:T(8,128)(2,1)S(1)}, u32[]{:S(2)}, u32[]{:S(2)}) collective-permute-start(bf16[3,160,128]{2,1,0:T(8,128)(2,1)S(1)} %get-tuple-element.77), channel_id=1, source_target_pairs={{0,4},{4,0},{8,12},{12,8},{16,20},{20,16},{24,28},{28,24},{1,5},{5... | collective-permute-start | bytes 368648 | tf_op jit(solution)/shard_map/ppermute | solution.py:366
  26.8 0.0 collective-permute-done.1.other_ref
  26.8 3.6 %pair.1 = (bf16[288,128]{1,0:T(8,128)(2,1)S(1)}, bf16[288,128]{1,0:T(8,128)(2,1)S(1)}, bf16[288,128]{1,0:T(8,128)(2,1)S(1)}, bf16[288,128]{1,0:T(8,128)(2,1)S(1)...) custom-call(s32[3,12]{1,0:T(4,128)S(1)} %copy-done.1, ...), custom_call_target="tpu_custom_call", output_to_operand_aliasing={{6}: (4, {}), {7}: (5, {})} | custom-call | flops 3000000000 | bytes 1024 | tf_op jit(solution)/shard_map/pair/pallas_call | solution.py:506
  30.4 0.1 collective-permute-start.7
  30.5 1.2 %patch.1 = (bf16[288,128]{1,0:T(8,128)(2,1)S(1)}, bf16[288,128]{1,0:T(8,128)(2,1)S(1)}, bf16[288,128]{1,0:T(8,128)(2,1)S(1)}, bf16[288,128]{1,0:T(8,128)(2,1)S(1)}) custom-call(s32[3,12]{1,0:T(4,128)S(1)} %copy-done.1, f32[2,3,128,128]{3,2,1,0:T(8,128)S(1)} %get-tuple-element.73.cur_ref, ...), custom_call_target="tpu_custom_call", output_to_operand_aliasing={{0}: (6, {}), {1}: (7, {}), {2}: (8, {}), {3}: (9, {})} | custom-call | flops 5000000000 | bytes 1024 | tf_op jit(solution)/shard_map/patch/pallas_call | solution.py:518
  31.7 0.6 %collective-permute-start.9 = (bf16[288,128]{1,0:T(8,128)(2,1)S(1)}, bf16[288,128]{1,0:T(8,128)(2,1)S(1)}, u32[]{:S(2)}, u32[]{:S(2)}) collective-permute-start(bf16[288,128]{1,0:T(8,128)(2,1)S(1)} %get-tuple-element.83), channel_id=1, source_target_pairs={{0,1},{1,0},{2,3},{3,2},{4,5},{5,4},{6,7},{7,6},{8,9},{9,8},{10,11... | collective-permute-start | bytes 221192 | tf_op jit(solution)/shard_map/ppermute | solution.py:366
  32.2 1.5 %collective-permute-start.10 = (bf16[288,128]{1,0:T(8,128)(2,1)S(1)}, bf16[288,128]{1,0:T(8,128)(2,1)S(1)}, u32[]{:S(2)}, u32[]{:S(2)}) collective-permute-start(bf16[288,128]{1,0:T(8,128)(2,1)S(1)} %get-tuple-element.84), channel_id=1, source_target_pairs={{0,2},{1,3},{2,0},{3,1},{4,6},{5,7},{6,4},{7,5},{8,10},{9,11},{10,... | collective-permute-start | bytes 221192 | tf_op jit(solution)/shard_map/ppermute | solution.py:366
  33.8 0.0 copy-start
  33.8 0.2 arrange.1
  34.0 2.6 %collective-permute-done.10.p2 = bf16[288,128]{1,0:T(8,128)(2,1)S(1)} collective-permute-done((bf16[288,128]{1,0:T(8,128)(2,1)S(1)}, bf16[288,128]{1,0:T(8,128)(2,1)S(1)}, u32[]{:S(2)}, u32[]{:S(2)}) %collective-permute-start.10) | collective-permute-done | bytes 73760 | tf_op jit(solution)/shard_map/ppermute | solution.py:366
  36.6 1.7 %collective-permute-done.11.p3 = bf16[288,128]{1,0:T(8,128)(2,1)S(1)} collective-permute-done((bf16[288,128]{1,0:T(8,128)(2,1)S(1)}, bf16[288,128]{1,0:T(8,128)(2,1)S(1)}, u32[]{:S(2)}, u32[]{:S(2)}) %collective-permute-start.11) | collective-permute-done | bytes 73760 | tf_op jit(solution)/shard_map/ppermute | solution.py:366
  38.3 2.5 %project.1 = (bf16[512,768]{1,0:T(8,128)(2,1)}, f32[4,512,128]{2,1,0:T(8,128)S(1)}, f32[2,512,128]{2,1,0:T(8,128)S(1)}) custom-call(s32[3,12]{1,0:T(4,128)S(1)} %copy-done.1, f32[4,512,128]{2,1,0:T(8,128)S(1)} %get-tuple-element.71.pairs_in, f32[2,512,128]{2,1,0:T(8,128)S(1)} %get-tuple-element.72.lasts_in, ...), custom_call_target="tpu_custom_call", output_to_operand_aliasing={{1}: (1, {}), {2}: (2, {})} | custom-call | flops 6000000000 | bytes 1024 | tf_op jit(solution)/shard_map/project/pallas_call | solution.py:533
  (12 shorter events, 0.0 us)
Async XLA Ops:
  2.0 19.7 %collective-permute-start.4 = (bf16[2,3,128,128]{3,2,1,0:T(8,128)(2,1)S(1)}, bf16[2,3,128,128]{3,2,1,0:T(8,128)(2,1)S(1)}, u32[]{:S(2)}, u32[]{:S(2)}) collective-permute-start(bf16[2,3,128,128]{3,2,1,0:T(8,128)(2,1)S(1)} %get-tuple-element.61.kv0), channel_id=1, source_target_pairs={{0,24},{4,28},{8,16},{12,20},{16,8},{20,12},{24,0},{28,4},{1,25},{... | collective-permute-start | bytes 589832 | tf_op jit(solution)/shard_map/ppermute | solution.py:366
  7.1 16.7 %collective-permute-start.3 = (bf16[2,3,128,128]{3,2,1,0:T(8,128)(2,1)S(1)}, bf16[2,3,128,128]{3,2,1,0:T(8,128)(2,1)S(1)}, u32[]{:S(2)}, u32[]{:S(2)}) collective-permute-start(bf16[2,3,128,128]{3,2,1,0:T(8,128)(2,1)S(1)} %get-tuple-element.61.kv0), channel_id=1, source_target_pairs={{0,16},{4,20},{8,24},{12,28},{16,0},{20,4},{24,8},{28,12},{1,17},{... | collective-permute-start | bytes 589832 | tf_op jit(solution)/shard_map/ppermute | solution.py:366
  7.1 16.7 %collective-permute-start.2 = (bf16[2,3,128,128]{3,2,1,0:T(8,128)(2,1)S(1)}, bf16[2,3,128,128]{3,2,1,0:T(8,128)(2,1)S(1)}, u32[]{:S(2)}, u32[]{:S(2)}) collective-permute-start(bf16[2,3,128,128]{3,2,1,0:T(8,128)(2,1)S(1)} %get-tuple-element.61.kv0), channel_id=1, source_target_pairs={{0,8},{4,12},{8,0},{12,4},{16,24},{20,28},{24,16},{28,20},{1,9},{5... | collective-permute-start | bytes 589832 | tf_op jit(solution)/shard_map/ppermute | solution.py:366
  7.8 19.0 %collective-permute-start.1 = (bf16[3,512,128]{2,1,0:T(8,128)(2,1)S(1)}, bf16[3,512,128]{2,1,0:T(8,128)(2,1)S(1)}, u32[]{:S(2)}, u32[]{:S(2)}) collective-permute-start(bf16[3,512,128]{2,1,0:T(8,128)(2,1)S(1)} %get-tuple-element.54.own_ref), channel_id=1, source_target_pairs={{0,4},{4,0},{8,12},{12,8},{16,20},{20,16},{24,28},{28,24},{1,5},{5... | collective-permute-start | bytes 1179656 | tf_op jit(solution)/shard_map/ppermute | solution.py:366
  10.7 9.4 %collective-permute-start.5 = (bf16[3,128,128]{2,1,0:T(8,128)(2,1)S(1)}, bf16[3,128,128]{2,1,0:T(8,128)(2,1)S(1)}, u32[]{:S(2)}, u32[]{:S(2)}) collective-permute-start(bf16[3,128,128]{2,1,0:T(8,128)(2,1)S(1)} %get-tuple-element.58.q_own), channel_id=1, source_target_pairs={{0,4},{4,0},{8,12},{12,8},{16,20},{20,16},{24,28},{28,24},{1,5},{5... | collective-permute-start | bytes 294920 | tf_op jit(solution)/shard_map/ppermute | solution.py:366
  19.0 7.8 %copy-start.1 = (s32[3,12]{1,0:T(4,128)S(1)}, s32[3,12]{1,0:T(4,128)}, u32[]{:S(2)}) copy-start(s32[3,12]{1,0:T(4,128)} %off_ref.5) | copy-start | bytes 436
  20.2 10.2 %collective-permute-start.6 = (bf16[1536,128]{1,0:T(8,128)(2,1)S(1)}, bf16[1536,128]{1,0:T(8,128)(2,1)S(1)}, u32[]{:S(2)}, u32[]{:S(2)}) collective-permute-start(bf16[1536,128]{1,0:T(8,128)(2,1)S(1)} %get-tuple-element.69), channel_id=1, source_target_pairs={{0,2},{1,3},{2,0},{3,1},{4,6},{5,7},{6,4},{7,5},{8,10},{9,11},{10,... | collective-permute-start | bytes 1179656 | tf_op jit(solution)/shard_map/ppermute | solution.py:366
  21.7 12.1 %collective-permute-start = (bf16[768,128]{1,0:T(8,128)(2,1)S(1)}, bf16[768,128]{1,0:T(8,128)(2,1)S(1)}, u32[]{:S(2)}, u32[]{:S(2)}) collective-permute-start(bf16[768,128]{1,0:T(8,128)(2,1)S(1)} %get-tuple-element.52), channel_id=1, source_target_pairs={{0,1},{1,0},{2,3},{3,2},{4,5},{5,4},{6,7},{7,6},{8,9},{9,8},{10,11... | collective-permute-start | bytes 589832 | tf_op jit(solution)/shard_map/ppermute | solution.py:366
  25.2 5.2 %collective-permute-start.8 = (bf16[3,160,128]{2,1,0:T(8,128)(2,1)S(1)}, bf16[3,160,128]{2,1,0:T(8,128)(2,1)S(1)}, u32[]{:S(2)}, u32[]{:S(2)}) collective-permute-start(bf16[3,160,128]{2,1,0:T(8,128)(2,1)S(1)} %get-tuple-element.77), channel_id=1, source_target_pairs={{0,4},{4,0},{8,12},{12,8},{16,20},{20,16},{24,28},{28,24},{1,5},{5... | collective-permute-start | bytes 368648 | tf_op jit(solution)/shard_map/ppermute | solution.py:366
  30.4 3.4 %collective-permute-start.7 = (bf16[1536,128]{1,0:T(8,128)(2,1)S(1)}, bf16[1536,128]{1,0:T(8,128)(2,1)S(1)}, u32[]{:S(2)}, u32[]{:S(2)}) collective-permute-start(bf16[1536,128]{1,0:T(8,128)(2,1)S(1)} %collective-permute-done.6.x2), channel_id=1, source_target_pairs={{0,1},{1,0},{2,3},{3,2},{4,5},{5,4},{6,7},{7,6},{8,9},{9,8},{10,11... | collective-permute-start | bytes 1179656 | tf_op jit(solution)/shard_map/ppermute | solution.py:366
  31.7 2.3 %collective-permute-start.9 = (bf16[288,128]{1,0:T(8,128)(2,1)S(1)}, bf16[288,128]{1,0:T(8,128)(2,1)S(1)}, u32[]{:S(2)}, u32[]{:S(2)}) collective-permute-start(bf16[288,128]{1,0:T(8,128)(2,1)S(1)} %get-tuple-element.83), channel_id=1, source_target_pairs={{0,1},{1,0},{2,3},{3,2},{4,5},{5,4},{6,7},{7,6},{8,9},{9,8},{10,11... | collective-permute-start | bytes 221192 | tf_op jit(solution)/shard_map/ppermute | solution.py:366
  32.2 4.4 %collective-permute-start.10 = (bf16[288,128]{1,0:T(8,128)(2,1)S(1)}, bf16[288,128]{1,0:T(8,128)(2,1)S(1)}, u32[]{:S(2)}, u32[]{:S(2)}) collective-permute-start(bf16[288,128]{1,0:T(8,128)(2,1)S(1)} %get-tuple-element.84), channel_id=1, source_target_pairs={{0,2},{1,3},{2,0},{3,1},{4,6},{5,7},{6,4},{7,5},{8,10},{9,11},{10,... | collective-permute-start | bytes 221192 | tf_op jit(solution)/shard_map/ppermute | solution.py:366
  33.8 4.5 %collective-permute-start.11 = (bf16[288,128]{1,0:T(8,128)(2,1)S(1)}, bf16[288,128]{1,0:T(8,128)(2,1)S(1)}, u32[]{:S(2)}, u32[]{:S(2)}) collective-permute-start(bf16[288,128]{1,0:T(8,128)(2,1)S(1)} %get-tuple-element.85), channel_id=1, source_target_pairs={{0,3},{1,2},{2,1},{3,0},{4,7},{5,6},{6,5},{7,4},{8,11},{9,10},{10,... | collective-permute-start | bytes 221192 | tf_op jit(solution)/shard_map/ppermute | solution.py:366
  33.8 4.5 %copy-start = (bf16[768,768]{1,0:T(8,128)(2,1)S(1)}, bf16[768,768]{1,0:T(8,128)(2,1)}, u32[]{:S(2)}) copy-start(bf16[768,768]{1,0:T(8,128)(2,1)} %w_ref.1) | copy-start | bytes 3538948

commit v3 on v2

--- a/solution.py
+++ b/solution.py
@@ -158,7 +158,7 @@
     attend(items)
 
 
-def pair_kernel(dils, off_ref, q_ref, own_ref, other_ref, acc_in, max_in, p0, p1, p2, p3, cur_ref, top_ref, acc, top, merged):
+def pair_kernel(dils, off_ref, q_ref, own_ref, other_ref, acc_in, max_in, p0, p1, p2, p3, cur_ref, top_ref, acc, top):
     heads, n1, _ = q_ref.shape
     tok = acc.shape[1]
     me = lax.axis_index("head")
@@ -166,35 +166,32 @@
     size = n1 // len(patches)
     half = size // 2
     items = []
+    held = {}
+    odd = me % 2 == 1
 
     def block(h, kv, vals, blk):
-        rows = pl.ds(off_ref[0, me * heads + h] + blk * QBLK * dils[0], QBLK, stride=dils[0])
+        first = pl.multiple_of(((me // 2) ^ blk) * QBLK, QBLK)
+        rows = pl.ds(off_ref[0, me * heads + h] + first * dils[0], QBLK, stride=dils[0])
 
         def sink(row_max, out):
             both, new = merge_rows(acc[h, rows, :], top[h, rows, :], out, row_max)
             acc[h, rows, :] = new
             top[h, rows, :] = both
-            merged[h, blk * QBLK : (blk + 1) * QBLK, :] = new
-            if (blk + 1) * QBLK == n1:
-                finish(h)
-
-        query = q_ref[h, blk * QBLK : (blk + 1) * QBLK]
+            if h == 0:
+                held[blk] = new
+                return
+            if h == 1:
+                done = pack_pair(held[blk], new)
+                ends = [done[:size], done[size:]]
+                at = slice(0, size)
+            else:
+                ends = [pack_even(new[i : i + half], new[i + half : i + size]) for i in (0, size)]
+                at = slice(size, size + half)
+            patches[2 * blk][at, :] = jnp.where(odd, ends[1], ends[0]).astype(BF16)
+            patches[2 * blk + 1][at, :] = jnp.where(odd, ends[0], ends[1]).astype(BF16)
+
+        query = q_ref[h, pl.ds(first, QBLK), :]
         items.append((lambda: dot(query, kv, NT), lambda weights: dot(weights, vals, NN), sink))
-
-    def finish(h):
-        for b in range(1, len(dils)):
-            pick = pl.ds(off_ref[b, me * heads + h], tok // dils[b], stride=dils[b])
-            cur_ref[b - 1, h] = acc[h, pick, :]
-            top_ref[b - 1, h] = top[h, pick, :]
-        for s, out in enumerate(patches):
-            start = pl.multiple_of((me ^ s) * size, size)
-            if h == 1:
-                rows = pl.ds(start, size)
-                out[:size, :] = pack_pair(merged[0, rows, :], merged[1, rows, :]).astype(BF16)
-            elif h == 2:
-                lo = merged[2, pl.ds(start, half), :]
-                hi = merged[2, pl.ds(start + half, half), :]
-                out[size : size + half, :] = pack_even(lo, hi).astype(BF16)
 
     for h in range(heads):
         kv = jnp.concatenate([own_ref[h], other_ref[h]], 0)
@@ -202,6 +199,11 @@
         for blk in range(n1 // QBLK):
             block(h, kv, vals, blk)
     attend(items)
+    for h in range(heads):
+        for b in range(1, len(dils)):
+            pick = pl.ds(off_ref[b, me * heads + h], tok // dils[b], stride=dils[b])
+            cur_ref[b - 1, h] = acc[h, pick, :]
+            top_ref[b - 1, h] = top[h, pick, :]
 
 
 def far_kernel(branches, q_own, q_other, kv0, kv1, kv2, kv3, part_ref, top_ref, send_ref):
@@ -247,7 +249,7 @@
     attend(items)
 
 
-def patch_kernel(branches, off_ref, cur_ref, cur_top, part_ref, part_top, got_ref, i0, i1, i2, i3, p0, p1, p2, p3, packed):
+def patch_kernel(branches, off_ref, cur_ref, cur_top, part_ref, part_top, got_ref, p0, p1, p2, p3, packed):
     heads, n = cur_ref.shape[1:3]
     me = lax.axis_index("head")
     patches = (p0, p1, p2, p3)
@@ -284,16 +286,22 @@
     packed[branches] = pack_even(done[2][0], done[2][-1])
     for s, out in enumerate(patches):
         start = pl.multiple_of((me ^ s) * size, size)
-        base = out.shape[0] - (branches + 1) * size
         for i in range(branches + 1):
-            out[base + i * size : base + (i + 1) * size, :] = packed[i, pl.ds(start, size), :].astype(BF16)
-
-
-def arrange_kernel(x0, x1, x2, x3, pairs, lasts):
+            out[i * size : (i + 1) * size, :] = packed[i, pl.ds(start, size), :].astype(BF16)
+
+
+def put_rows(off_ref, dil, branch, head, first, ref, index, new, in_low):
+    at = pl.ds(off_ref[branch, head] + first * dil, new.shape[0], stride=dil)
+    ref[index, at, :] = jnp.where((lane_of(new.shape) < DH) == in_low, new, ref[index, at, :])
+
+
+def arrange_kernel(dils, off_ref, x0, x1, x2, x3, p0, p1, p2, p3, pairs, lasts):
+    me = lax.axis_index("head")
     count = x0.shape[0]
     width = pairs.shape[1]
     half = width // 2
-    xs = (x0, x1, x2.at[:count, :], x3.at[count:, :])
+    near = width // dils[0]
+    xs, ps = (x0, x1, x2.at[:count, :], x3.at[count:, :]), (p0, p1, p2, p3)
     for s in range(4):
         pairs[s] = xs[s][:width, :].astype(F32)
     for t in range(2):
@@ -302,63 +310,54 @@
         lane = lane_of(a.shape)
         lasts[t, :half, :] = jnp.where(lane < DH, a, swap(b))
         lasts[t, half:, :] = jnp.where(lane < DH, swap(a), b)
-
-
-def project_kernel(dils, off_ref, pairs_in, lasts_in, p0, p1, p2, p3, w_ref, out_hbm, pairs, lasts, out_ref, sems):
+    for s in range(4):
+        in_low = s % 2 == 0
+        put = functools.partial(put_rows, off_ref, dils[0], 0)
+        head = (me ^ s) * 3
+        new = ps[s][:near, :].astype(F32)
+        for h in range(2):
+            put(head + h, 0, pairs, s, new, h == 0)
+        new = ps[s][near:, :].astype(F32)
+        turned = swap(new)
+        put(head + 2, 0, lasts, s // 2, new if in_low else turned, in_low)
+        put(head + 2, near // 2, lasts, s // 2, turned if in_low else new, in_low)
+
+
+def project_kernel(dils, off_ref, pairs_in, lasts_in, p0, p1, p2, p3, w_ref, out_hbm, pairs, lasts, out_ref, sem):
     me = lax.axis_index("head")
     width = out_ref.shape[0]
     branches = len(dils) - 1
-    near = width // dils[0]
     size = width // dils[1]
-    heads = 3
-    rows = heads * DH
+    rows = 3 * DH
     sources = [me ^ s for s in range(4)]
     ps = (p0, p1, p2, p3)
-
-    def put(ref, index, branch, source, h, first, new, in_low):
-        dil = dils[branch]
-        at = pl.ds(off_ref[branch, sources[source] * heads + h] + first * dil, new.shape[0], stride=dil)
-        old = ref[index, at, :]
-        ref[index, at, :] = jnp.where((lane_of(new.shape) < DH) == in_low, new, old)
-
     for s in range(4):
         in_low = s % 2 == 0
-        new = ps[s][:near, :].astype(F32)
-        for h in range(2):
-            put(pairs, s, 0, s, h, 0, new, h == 0)
-        new = ps[s][near : near + near // 2, :].astype(F32)
-        turned = swap(new)
-        put(lasts, s // 2, 0, s, 2, 0, new if in_low else turned, in_low)
-        put(lasts, s // 2, 0, s, 2, near // 2, turned if in_low else new, in_low)
-        base = near + near // 2
+        head = sources[s] * 3
         for b in range(branches):
-            new = ps[s][base + b * size : base + (b + 1) * size, :].astype(F32)
+            put = functools.partial(put_rows, off_ref, dils[b + 1], b + 1)
+            new = ps[s][b * size : (b + 1) * size, :].astype(F32)
             for h in range(2):
-                put(pairs, s, b + 1, s, h, 0, new, h == 0)
-            new = ps[s][base + branches * size :, :].astype(F32)
+                put(head + h, 0, pairs, s, new, h == 0)
+            new = ps[s][branches * size :, :].astype(F32)
             if b != s % 2:
                 new = swap(new)
-            put(lasts, s // 2, b + 1, s, 2, 0, new, in_low)
+            put(head + 2, 0, lasts, s // 2, new, in_low)
 
     def w_rows(s, start, count):
         return w_ref[pl.ds(pl.multiple_of(sources[s] * rows + start, DH), count), :]
 
     ws = [jnp.concatenate([w_rows(2 * t, 0, LANES), w_rows(2 * t + 1, 0, LANES)], 0) for t in range(2)]
     ws.append(jnp.concatenate([w_rows(s, LANES, DH) for s in range(4)], 0))
-    copies = []
-    step = width // 4
-    for c in range(4):
-        at = slice(c * step, (c + 1) * step)
-        total = None
-        for t in range(3):
-            halves = (pairs[2 * t, at], pairs[2 * t + 1, at]) if t < 2 else (lasts[0, at], lasts[1, at])
-            part = dot(jnp.concatenate(halves, 1).astype(BF16), ws[t], NN)
-            total = part if total is None else total + part
-        out_ref[at, :] = total.astype(BF16)
-        copies.append(pltpu.make_async_copy(out_ref.at[pl.ds(c * step, step), :], out_hbm.at[pl.ds(c * step, step), :], sems.at[c]))
-        copies[-1].start()
-    for copy in copies:
-        copy.wait()
+    total = None
+    for t in range(3):
+        halves = (pairs[2 * t], pairs[2 * t + 1]) if t < 2 else (lasts[0], lasts[1])
+        part = dot(jnp.concatenate(halves, 1).astype(BF16), ws[t], NN)
+        total = part if total is None else total + part
+    out_ref[...] = total.astype(BF16)
+    copy = pltpu.make_async_copy(out_ref, out_hbm, sem)
+    copy.start()
+    copy.wait()
 
 
 def partner(block, axis, apart):
@@ -458,7 +457,6 @@
         ],
     )(*stay)
     fars = [far] + [partner(far, "seq", apart) for apart in (2, 4, 6)]
-    near_other = partner(near, "seq", 1)
 
     q1, q23 = call(
         functools.partial(query_kernel, dils),
@@ -472,6 +470,7 @@
         ],
     )(stay[0], q)
     q23_other = partner(q23, "seq", 1)
+    near_other = partner(near, "seq", 1)
 
     q, q23 = lax.optimization_barrier((q, q23))
     main = heads * width // 2
@@ -494,48 +493,47 @@
     y_in = partner(m_far, "head", 2)
     core_in = partner(m_core, "head", 1)
 
-    patch_rows = n1 // 4 * 3 // 2 + (branches + 1) * n2 // 4
-    fars, acc = lax.optimization_barrier((fars, acc))
+    acc, near_other = lax.optimization_barrier((acc, near_other))
+    *early, cur, cur_top, _, _ = call(
+        functools.partial(pair_kernel, dils),
+        "pair",
+        [((n1 * 3 // 8, LANES), BF16)] * 4 + [far_shape] * 2 + [acc_shape] * 2,
+        [smem] + [whole] * 5,
+        aliases={4: 6, 5: 7},
+    )(offsets, q1, near, near_other, acc, top)
+    early = [early[0]] + [partner(early[s], "head", s) for s in range(1, 4)]
+
+    fars, cur = lax.optimization_barrier((fars, cur))
     part, part_top, send = call(
         functools.partial(far_kernel, branches),
         "far",
         [far_shape] * 2 + [((heads, n2 + 2 * STATS, LANES), BF16)],
         [whole] * 6,
     )(q23, q23_other, *fars)
-    acc, part = lax.optimization_barrier((acc, part))
-    *patches, cur, cur_top, _, _ = call(
-        functools.partial(pair_kernel, dils),
-        "pair",
-        [((patch_rows, LANES), BF16)] * 4 + [far_shape] * 2 + [acc_shape] * 2,
-        [smem] + [whole] * 5,
-        [pltpu.VMEM((heads, n1, LANES), F32)],
-        aliases={4: 6, 5: 7},
-    )(offsets, q1, near, near_other, acc, top)
     got = partner(send, "seq", 1)
-    cur, y_in = lax.optimization_barrier((cur, y_in))
+    y_in, part = lax.optimization_barrier((y_in, part))
     y_core = partner(y_in, "head", 1)
 
     patches = call(
         functools.partial(patch_kernel, branches),
         "patch",
-        [((patch_rows, LANES), BF16)] * 4,
-        [smem] + [whole] * 9,
+        [(((branches + 1) * n2 // 4, LANES), BF16)] * 4,
+        [smem] + [whole] * 5,
         [pltpu.VMEM((branches + 1, n2, LANES), F32)],
-        aliases={6: 0, 7: 1, 8: 2, 9: 3},
-    )(offsets, cur, cur_top, part, part_top, got, *patches)
+    )(offsets, cur, cur_top, part, part_top, got)
     fixes = [patches[0]] + [partner(patches[s], "head", s) for s in range(1, 4)]
 
     out_shape = (width, out_weight.shape[1])
     spread_shapes = [((4, width, LANES), F32), ((2, width, LANES), F32)]
-    pairs, lasts = call(arrange_kernel, "arrange", spread_shapes, [whole] * 4)(
-        m_own, core_in, y_in, y_core
-    )
+    pairs, lasts = call(
+        functools.partial(arrange_kernel, dils), "arrange", spread_shapes, [smem] + [whole] * 8
+    )(offsets, m_own, core_in, y_in, y_core, *early)
     out, _, _ = call(
         functools.partial(project_kernel, dils),
         "project",
         [(out_shape, BF16)] + spread_shapes,
         [smem] + [whole] * 7,
-        [pltpu.VMEM(out_shape, BF16), pltpu.SemaphoreType.DMA((4,))],
+        [pltpu.VMEM(out_shape, BF16), pltpu.SemaphoreType.DMA],
         aliases={1: 1, 2: 2},
         spaces=(pltpu.HBM, pltpu.VMEM, pltpu.VMEM),
     )(offsets, pairs, lasts, *fixes, out_weight)

time: 41.1 us -> 40.2 us (0.978)
  waiting for transfers between devices: 7.64 us -> 4.3 us
  starting transfers between devices: 13.1 us -> 14.8 us
  Pallas kernels: 20 us -> 20.7 us
    ppermute x12 -> x15, waiting for transfers between devices: 7.64 us -> 4.3 us  [partner(): return lax.ppermute(block, axis, [(i, i ^ apart) for i in range(count)])]
    ppermute x12 -> x15, starting transfers between devices: 13.1 us -> 14.8 us  [partner(): return lax.ppermute(block, axis, [(i, i ^ apart) for i in range(count)])]
    pallas_call x3, Pallas kernels: 4.91 us -> 5.53 us  [the longest x1 3.51 us: local(): call(functools.partial(pair_kernel, dils), 'pair', [((n1 * 3 // 8, LANES)...]
  transfers between devices with their start and end apart: 12 -> 15, of which waited for: 4 -> 4; matrix products, arithmetic and copies ran while one was open for 0% -> 0% of each run, Pallas kernels for 38% -> 40%
where the time goes in v3:
time: 40.2 us; the launch traced here: 40 us
  Pallas kernels  20.7 us (51%)
  starting transfers between devices  14.8 us (37%)
  waiting for transfers between devices  4.3 us (11%)
    ppermute x15, starting transfers between devices, partner(): return lax.ppermute(block, axis, [(i, i ^ apart) for i in range(count)])  14.8 us
    pallas_call x1, Pallas kernels, local(): call(local_kernel, 'local', [acc_shape] * 2 + [((main, LANES), BF16)] * 2...  7.86 us
    ppermute x15, waiting for transfers between devices, partner(): return lax.ppermute(block, axis, [(i, i ^ apart) for i in range(count)])  4.3 us
    pallas_call x1, Pallas kernels, local(): call(functools.partial(pair_kernel, dils), 'pair', [((n1 * 3 // 8, LANES)...  3.51 us
    pallas_call x1, Pallas kernels, local(): call(functools.partial(project_kernel, dils), 'project', [(out_shape, BF1...  2.52 us
    pallas_call x1, Pallas kernels, local(): call(functools.partial(select_kernel, dils), 'select', [(queries.shape, B...  2.01 us
    pallas_call x1, Pallas kernels, local(): call(functools.partial(far_kernel, branches), 'far', [far_shape] * 2 + [(...  1.43 us
    pallas_call x1, Pallas kernels, local(): call(functools.partial(query_kernel, dils), 'query', [((heads, n1, LANES)...  1.33 us
  transfers between devices with their start and end apart: 15, of which 4 were waited for; matrix products, arithmetic and copies ran while one was open for 0% of the time, Pallas kernels for 40%

profile of v3, /device:TPU:0, one launch (start us, length us, event | category | flops | bytes accessed | tf_op | source)
XLA Modules:
  0.0 40.0 jit_solution(11556733422836996876)
XLA Ops:
  0.0 2.0 %select.1 = (bf16[192,2048]{1,0:T(8,128)(2,1)S(1)}, bf16[192,2048]{1,0:T(8,128)(2,1)S(1)}, bf16[192,2048]{1,0:T(8,128)(2,1)S(1)}, bf16[3,512,128]{2,1,0:T(8,128)(2,1)S(1)}, bf16[2,3,128,128]{3,2,1,0:T(8,128)(2,1)S(1)}) custom-call(s32[3,12]{1,0:T(4,128)} %off_ref.7, bf16[192,2048]{1,0:T(8,128)(2,1)} %q_hbm.1, bf16[192,2048]{1,0:T(8,128)(2,1)} %k_hbm.1, ...), custom_call_target="tpu_custom_call" | custom-call | flops 6000000000 | bytes 1024 | tf_op jit(solution)/shard_map/select/pallas_call | solution.py:447
  2.0 3.1 %collective-permute-start.3 = (bf16[2,3,128,128]{3,2,1,0:T(8,128)(2,1)S(1)}, bf16[2,3,128,128]{3,2,1,0:T(8,128)(2,1)S(1)}, u32[]{:S(2)}, u32[]{:S(2)}) collective-permute-start(bf16[2,3,128,128]{3,2,1,0:T(8,128)(2,1)S(1)} %get-tuple-element.65.kv0), channel_id=1, source_target_pairs={{0,8},{4,12},{8,0},{12,4},{16,24},{20,28},{24,16},{28,20},{1,9},{5... | collective-permute-start | bytes 589832 | tf_op jit(solution)/shard_map/ppermute | solution.py:365
  5.1 2.6 %collective-permute-start.4 = (bf16[2,3,128,128]{3,2,1,0:T(8,128)(2,1)S(1)}, bf16[2,3,128,128]{3,2,1,0:T(8,128)(2,1)S(1)}, u32[]{:S(2)}, u32[]{:S(2)}) collective-permute-start(bf16[2,3,128,128]{3,2,1,0:T(8,128)(2,1)S(1)} %get-tuple-element.65.kv0), channel_id=1, source_target_pairs={{0,16},{4,20},{8,24},{12,28},{16,0},{20,4},{24,8},{28,12},{1,17},{... | collective-permute-start | bytes 589832 | tf_op jit(solution)/shard_map/ppermute | solution.py:365
  7.7 1.7 %collective-permute-start.6 = (bf16[3,512,128]{2,1,0:T(8,128)(2,1)S(1)}, bf16[3,512,128]{2,1,0:T(8,128)(2,1)S(1)}, u32[]{:S(2)}, u32[]{:S(2)}) collective-permute-start(bf16[3,512,128]{2,1,0:T(8,128)(2,1)S(1)} %get-tuple-element.59.own_ref), channel_id=1, source_target_pairs={{0,4},{4,0},{8,12},{12,8},{16,20},{20,16},{24,28},{28,24},{1,5},{5... | collective-permute-start | bytes 1179656 | tf_op jit(solution)/shard_map/ppermute | solution.py:365
  9.4 1.3 %query.1 = (bf16[3,512,128]{2,1,0:T(8,128)(2,1)S(1)}, bf16[3,128,128]{2,1,0:T(8,128)(2,1)S(1)}) custom-call(s32[3,12]{1,0:T(4,128)} %off_ref.7, bf16[192,2048]{1,0:T(8,128)(2,1)S(1)} %get-tuple-element.48.q_ref), custom_call_target="tpu_custom_call" | custom-call | flops 4000000000 | bytes 1024 | tf_op jit(solution)/shard_map/query/pallas_call | solution.py:461
  10.7 0.4 collective-permute-start.1
  11.1 7.9 %local.1 = (f32[3,2048,128]{2,1,0:T(8,128)S(1)}, f32[3,2048,128]{2,1,0:T(8,128)S(1)}, bf16[768,128]{1,0:T(8,128)(2,1)S(1)}, bf16[768,128]{1,0:T(8,128)(2,1)S(1)}, bf16[1536,128]{1,0:T(8,128)(2,1)S(1)}) custom-call(bf16[192,2048]{1,0:T(8,128)(2,1)S(1)} %get-tuple-element.48.q_ref, bf16[192,2048]{1,0:T(8,128)(2,1)S(1)} %get-tuple-element.49.k_ref, ...), custom_call_target="tpu_custom_call" | custom-call | flops 24999999488 | bytes 1024 | tf_op jit(solution)/shard_map/local/pallas_call | solution.py:477
  19.0 1.1 %collective-permute-done.1.q_other = bf16[3,128,128]{2,1,0:T(8,128)(2,1)S(1)} collective-permute-done((bf16[3,128,128]{2,1,0:T(8,128)(2,1)S(1)}, bf16[3,128,128]{2,1,0:T(8,128)(2,1)S(1)}, u32[]{:S(2)}, u32[]{:S(2)}) %collective-permute-start.1) | collective-permute-done | bytes 98336 | tf_op jit(solution)/shard_map/ppermute | solution.py:365
  20.1 1.5 %collective-permute-start.2 = (bf16[1536,128]{1,0:T(8,128)(2,1)S(1)}, bf16[1536,128]{1,0:T(8,128)(2,1)S(1)}, u32[]{:S(2)}, u32[]{:S(2)}) collective-permute-start(bf16[1536,128]{1,0:T(8,128)(2,1)S(1)} %get-tuple-element.54), channel_id=1, source_target_pairs={{0,2},{1,3},{2,0},{3,1},{4,6},{5,7},{6,4},{7,5},{8,10},{9,11},{10,... | collective-permute-start | bytes 1179656 | tf_op jit(solution)/shard_map/ppermute | solution.py:365
  21.6 3.5 %pair.1 = (bf16[192,128]{1,0:T(8,128)(2,1)S(1)}, bf16[192,128]{1,0:T(8,128)(2,1)S(1)}, bf16[192,128]{1,0:T(8,128)(2,1)S(1)}, bf16[192,128]{1,0:T(8,128)(2,1)S(1)...) custom-call(s32[3,12]{1,0:T(4,128)S(1)} %copy-done.1, ...), custom_call_target="tpu_custom_call", output_to_operand_aliasing={{6}: (4, {}), {7}: (5, {})} | custom-call | flops 3000000000 | bytes 1024 | tf_op jit(solution)/shard_map/pair/pallas_call | solution.py:497
  25.2 1.4 %far.1 = (f32[2,3,128,128]{3,2,1,0:T(8,128)S(1)}, f32[2,3,128,128]{3,2,1,0:T(8,128)S(1)}, bf16[3,160,128]{2,1,0:T(8,128)(2,1)S(1)}) custom-call(bf16[3,128,128]{2,1,0:T(8,128)(2,1)S(1)} %get-tuple-element.55.q_own, bf16[3,128,128]{2,1,0:T(8,128)(2,1)S(1)} %collective-permute-done.1.q_other, bf16[2,3,128,128]{3,2,1,0:T(8,128)(2,1)S(1)} %get-tuple-element.65.kv0, ...), custom_call_target="tpu_custom_call" | custom-call | flops 1000000000 | bytes 1024 | tf_op jit(solution)/shard_map/far/pallas_call | solution.py:507
  26.6 1.6 %collective-permute-start.11 = (bf16[3,160,128]{2,1,0:T(8,128)(2,1)S(1)}, bf16[3,160,128]{2,1,0:T(8,128)(2,1)S(1)}, u32[]{:S(2)}, u32[]{:S(2)}) collective-permute-start(bf16[3,160,128]{2,1,0:T(8,128)(2,1)S(1)} %get-tuple-element.81), channel_id=1, source_target_pairs={{0,4},{4,0},{8,12},{12,8},{16,20},{20,16},{24,28},{28,24},{1,5},{5... | collective-permute-start | bytes 368648 | tf_op jit(solution)/shard_map/ppermute | solution.py:365
  28.2 0.6 %collective-permute-start.10 = (bf16[192,128]{1,0:T(8,128)(2,1)S(1)}, bf16[192,128]{1,0:T(8,128)(2,1)S(1)}, u32[]{:S(2)}, u32[]{:S(2)}) collective-permute-start(bf16[192,128]{1,0:T(8,128)(2,1)S(1)} %get-tuple-element.74), channel_id=1, source_target_pairs={{0,3},{1,2},{2,1},{3,0},{4,7},{5,6},{6,5},{7,4},{8,11},{9,10},{10,... | collective-permute-start | bytes 147464 | tf_op jit(solution)/shard_map/ppermute | solution.py:365
  28.8 0.0 collective-permute-start.8
  28.8 0.7 %collective-permute-done.2.x2 = bf16[1536,128]{1,0:T(8,128)(2,1)S(1)} collective-permute-done((bf16[1536,128]{1,0:T(8,128)(2,1)S(1)}, bf16[1536,128]{1,0:T(8,128)(2,1)S(1)}, u32[]{:S(2)}, u32[]{:S(2)}) %collective-permute-start.2) | collective-permute-done | bytes 393248 | tf_op jit(solution)/shard_map/ppermute | solution.py:365
  29.5 1.3 %collective-permute-start.9 = (bf16[192,128]{1,0:T(8,128)(2,1)S(1)}, bf16[192,128]{1,0:T(8,128)(2,1)S(1)}, u32[]{:S(2)}, u32[]{:S(2)}) collective-permute-start(bf16[192,128]{1,0:T(8,128)(2,1)S(1)} %get-tuple-element.73), channel_id=1, source_target_pairs={{0,2},{1,3},{2,0},{3,1},{4,6},{5,7},{6,4},{7,5},{8,10},{9,11},{10,... | collective-permute-start | bytes 147464 | tf_op jit(solution)/shard_map/ppermute | solution.py:365
  30.8 0.8 %collective-permute-done.11.got_ref = bf16[3,160,128]{2,1,0:T(8,128)(2,1)S(1)} collective-permute-done((bf16[3,160,128]{2,1,0:T(8,128)(2,1)S(1)}, bf16[3,160,128]{2,1,0:T(8,128)(2,1)S(1)}, u32[]{:S(2)}, u32[]{:S(2)}) %collective-permute-start.11) | collective-permute-done | bytes 122912 | tf_op jit(solution)/shard_map/ppermute | solution.py:365
  31.6 1.2 %patch.1 = (bf16[96,128]{1,0:T(8,128)(2,1)S(1)}, bf16[96,128]{1,0:T(8,128)(2,1)S(1)}, bf16[96,128]{1,0:T(8,128)(2,1)S(1)}, bf16[96,128]{1,0:T(8,128)(2,1)S(1)}) custom-call(s32[3,12]{1,0:T(4,128)S(1)} %copy-done.1, f32[2,3,128,128]{3,2,1,0:T(8,128)S(1)} %get-tuple-element.77.cur_ref, f32[2,3,128,128]{3,2,1,0:T(8,128)S(1)} %get-tuple-element.78.cur_top, ...), custom_call_target="tpu_custom_call" | custom-call | flops 5000000000 | bytes 1024 | tf_op jit(solution)/shard_map/patch/pallas_call | solution.py:517
  32.7 0.6 %collective-permute-start.12 = (bf16[96,128]{1,0:T(8,128)(2,1)S(1)}, bf16[96,128]{1,0:T(8,128)(2,1)S(1)}, u32[]{:S(2)}, u32[]{:S(2)}) collective-permute-start(bf16[96,128]{1,0:T(8,128)(2,1)S(1)} %get-tuple-element.83), channel_id=1, source_target_pairs={{0,1},{1,0},{2,3},{3,2},{4,5},{5,4},{6,7},{7,6},{8,9},{9,8},{10,11... | collective-permute-start | bytes 73736 | tf_op jit(solution)/shard_map/ppermute | solution.py:365
  33.3 0.5 %collective-permute-start.13 = (bf16[96,128]{1,0:T(8,128)(2,1)S(1)}, bf16[96,128]{1,0:T(8,128)(2,1)S(1)}, u32[]{:S(2)}, u32[]{:S(2)}) collective-permute-start(bf16[96,128]{1,0:T(8,128)(2,1)S(1)} %get-tuple-element.84), channel_id=1, source_target_pairs={{0,2},{1,3},{2,0},{3,1},{4,6},{5,7},{6,4},{7,5},{8,10},{9,11},{10,... | collective-permute-start | bytes 73736 | tf_op jit(solution)/shard_map/ppermute | solution.py:365
  33.8 0.9 %collective-permute-start.14 = (bf16[96,128]{1,0:T(8,128)(2,1)S(1)}, bf16[96,128]{1,0:T(8,128)(2,1)S(1)}, u32[]{:S(2)}, u32[]{:S(2)}) collective-permute-start(bf16[96,128]{1,0:T(8,128)(2,1)S(1)} %get-tuple-element.85), channel_id=1, source_target_pairs={{0,3},{1,2},{2,1},{3,0},{4,7},{5,6},{6,5},{7,4},{8,11},{9,10},{10,... | collective-permute-start | bytes 73736 | tf_op jit(solution)/shard_map/ppermute | solution.py:365
  34.8 0.9 %arrange.1 = (f32[4,512,128]{2,1,0:T(8,128)S(1)}, f32[2,512,128]{2,1,0:T(8,128)S(1)}) custom-call(s32[3,12]{1,0:T(4,128)S(1)} %copy-done.1, bf16[768,128]{1,0:T(8,128)(2,1)S(1)} %get-tuple-element.51.x0, bf16[768,128]{1,0:T(8,128)(2,1)S(1)} %collective-permute-done.x1, bf16[1536,128]{1,0:T(8,128)(2,1)S(1)} %collective-permute-done.2.x2, ...), custom_call_target="tpu_custom_call" | custom-call | flops 4000000000 | bytes 1024 | tf_op jit(solution)/shard_map/arrange/pallas_call | solution.py:528
  35.6 1.7 %collective-permute-done.13.p2 = bf16[96,128]{1,0:T(8,128)(2,1)S(1)} collective-permute-done((bf16[96,128]{1,0:T(8,128)(2,1)S(1)}, bf16[96,128]{1,0:T(8,128)(2,1)S(1)}, u32[]{:S(2)}, u32[]{:S(2)}) %collective-permute-start.13) | collective-permute-done | bytes 24608 | tf_op jit(solution)/shard_map/ppermute | solution.py:365
  37.4 2.5 %project.1 = (bf16[512,768]{1,0:T(8,128)(2,1)}, f32[4,512,128]{2,1,0:T(8,128)S(1)}, f32[2,512,128]{2,1,0:T(8,128)S(1)}) custom-call(s32[3,12]{1,0:T(4,128)S(1)} %copy-done.1, f32[4,512,128]{2,1,0:T(8,128)S(1)} %get-tuple-element.75.pairs_in, f32[2,512,128]{2,1,0:T(8,128)S(1)} %get-tuple-element.76.lasts_in, ...), custom_call_target="tpu_custom_call", output_to_operand_aliasing={{1}: (1, {}), {2}: (2, {})} | custom-call | flops 6000000000 | bytes 1024 | tf_op jit(solution)/shard_map/project/pallas_call | solution.py:531
  (18 shorter events, 0.0 us)
Async XLA Ops:
  2.0 23.1 %collective-permute-start.3 = (bf16[2,3,128,128]{3,2,1,0:T(8,128)(2,1)S(1)}, bf16[2,3,128,128]{3,2,1,0:T(8,128)(2,1)S(1)}, u32[]{:S(2)}, u32[]{:S(2)}) collective-permute-start(bf16[2,3,128,128]{3,2,1,0:T(8,128)(2,1)S(1)} %get-tuple-element.65.kv0), channel_id=1, source_target_pairs={{0,8},{4,12},{8,0},{12,4},{16,24},{20,28},{24,16},{28,20},{1,9},{5... | collective-permute-start | bytes 589832 | tf_op jit(solution)/shard_map/ppermute | solution.py:365
  5.1 20.1 %collective-permute-start.4 = (bf16[2,3,128,128]{3,2,1,0:T(8,128)(2,1)S(1)}, bf16[2,3,128,128]{3,2,1,0:T(8,128)(2,1)S(1)}, u32[]{:S(2)}, u32[]{:S(2)}) collective-permute-start(bf16[2,3,128,128]{3,2,1,0:T(8,128)(2,1)S(1)} %get-tuple-element.65.kv0), channel_id=1, source_target_pairs={{0,16},{4,20},{8,24},{12,28},{16,0},{20,4},{24,8},{28,12},{1,17},{... | collective-permute-start | bytes 589832 | tf_op jit(solution)/shard_map/ppermute | solution.py:365
  7.7 17.5 %collective-permute-start.5 = (bf16[2,3,128,128]{3,2,1,0:T(8,128)(2,1)S(1)}, bf16[2,3,128,128]{3,2,1,0:T(8,128)(2,1)S(1)}, u32[]{:S(2)}, u32[]{:S(2)}) collective-permute-start(bf16[2,3,128,128]{3,2,1,0:T(8,128)(2,1)S(1)} %get-tuple-element.65.kv0), channel_id=1, source_target_pairs={{0,24},{4,28},{8,16},{12,20},{16,8},{20,12},{24,0},{28,4},{1,25},{... | collective-permute-start | bytes 589832 | tf_op jit(solution)/shard_map/ppermute | solution.py:365
  7.7 13.9 %collective-permute-start.6 = (bf16[3,512,128]{2,1,0:T(8,128)(2,1)S(1)}, bf16[3,512,128]{2,1,0:T(8,128)(2,1)S(1)}, u32[]{:S(2)}, u32[]{:S(2)}) collective-permute-start(bf16[3,512,128]{2,1,0:T(8,128)(2,1)S(1)} %get-tuple-element.59.own_ref), channel_id=1, source_target_pairs={{0,4},{4,0},{8,12},{12,8},{16,20},{20,16},{24,28},{28,24},{1,5},{5... | collective-permute-start | bytes 1179656 | tf_op jit(solution)/shard_map/ppermute | solution.py:365
  10.7 9.4 %collective-permute-start.1 = (bf16[3,128,128]{2,1,0:T(8,128)(2,1)S(1)}, bf16[3,128,128]{2,1,0:T(8,128)(2,1)S(1)}, u32[]{:S(2)}, u32[]{:S(2)}) collective-permute-start(bf16[3,128,128]{2,1,0:T(8,128)(2,1)S(1)} %get-tuple-element.55.q_own), channel_id=1, source_target_pairs={{0,4},{4,0},{8,12},{12,8},{16,20},{20,16},{24,28},{28,24},{1,5},{5... | collective-permute-start | bytes 294920 | tf_op jit(solution)/shard_map/ppermute | solution.py:365
  11.1 10.5 %copy-start.1 = (s32[3,12]{1,0:T(4,128)S(1)}, s32[3,12]{1,0:T(4,128)}, u32[]{:S(2)}) copy-start(s32[3,12]{1,0:T(4,128)} %off_ref.7) | copy-start | bytes 436
  20.1 9.4 %collective-permute-start.2 = (bf16[1536,128]{1,0:T(8,128)(2,1)S(1)}, bf16[1536,128]{1,0:T(8,128)(2,1)S(1)}, u32[]{:S(2)}, u32[]{:S(2)}) collective-permute-start(bf16[1536,128]{1,0:T(8,128)(2,1)S(1)} %get-tuple-element.54), channel_id=1, source_target_pairs={{0,2},{1,3},{2,0},{3,1},{4,6},{5,7},{6,4},{7,5},{8,10},{9,11},{10,... | collective-permute-start | bytes 1179656 | tf_op jit(solution)/shard_map/ppermute | solution.py:365
  26.6 4.9 %collective-permute-start.11 = (bf16[3,160,128]{2,1,0:T(8,128)(2,1)S(1)}, bf16[3,160,128]{2,1,0:T(8,128)(2,1)S(1)}, u32[]{:S(2)}, u32[]{:S(2)}) collective-permute-start(bf16[3,160,128]{2,1,0:T(8,128)(2,1)S(1)} %get-tuple-element.81), channel_id=1, source_target_pairs={{0,4},{4,0},{8,12},{12,8},{16,20},{20,16},{24,28},{28,24},{1,5},{5... | collective-permute-start | bytes 368648 | tf_op jit(solution)/shard_map/ppermute | solution.py:365
  28.2 4.6 %collective-permute-start = (bf16[768,128]{1,0:T(8,128)(2,1)S(1)}, bf16[768,128]{1,0:T(8,128)(2,1)S(1)}, u32[]{:S(2)}, u32[]{:S(2)}) collective-permute-start(bf16[768,128]{1,0:T(8,128)(2,1)S(1)} %get-tuple-element.52), channel_id=1, source_target_pairs={{0,1},{1,0},{2,3},{3,2},{4,5},{5,4},{6,7},{7,6},{8,9},{9,8},{10,11... | collective-permute-start | bytes 589832 | tf_op jit(solution)/shard_map/ppermute | solution.py:365
  28.2 5.1 %collective-permute-start.10 = (bf16[192,128]{1,0:T(8,128)(2,1)S(1)}, bf16[192,128]{1,0:T(8,128)(2,1)S(1)}, u32[]{:S(2)}, u32[]{:S(2)}) collective-permute-start(bf16[192,128]{1,0:T(8,128)(2,1)S(1)} %get-tuple-element.74), channel_id=1, source_target_pairs={{0,3},{1,2},{2,1},{3,0},{4,7},{5,6},{6,5},{7,4},{8,11},{9,10},{10,... | collective-permute-start | bytes 147464 | tf_op jit(solution)/shard_map/ppermute | solution.py:365
  28.8 5.0 %collective-permute-start.8 = (bf16[192,128]{1,0:T(8,128)(2,1)S(1)}, bf16[192,128]{1,0:T(8,128)(2,1)S(1)}, u32[]{:S(2)}, u32[]{:S(2)}) collective-permute-start(bf16[192,128]{1,0:T(8,128)(2,1)S(1)} %get-tuple-element.72), channel_id=1, source_target_pairs={{0,1},{1,0},{2,3},{3,2},{4,5},{5,4},{6,7},{7,6},{8,9},{9,8},{10,11... | collective-permute-start | bytes 147464 | tf_op jit(solution)/shard_map/ppermute | solution.py:365
  29.5 5.3 %collective-permute-start.9 = (bf16[192,128]{1,0:T(8,128)(2,1)S(1)}, bf16[192,128]{1,0:T(8,128)(2,1)S(1)}, u32[]{:S(2)}, u32[]{:S(2)}) collective-permute-start(bf16[192,128]{1,0:T(8,128)(2,1)S(1)} %get-tuple-element.73), channel_id=1, source_target_pairs={{0,2},{1,3},{2,0},{3,1},{4,6},{5,7},{6,4},{7,5},{8,10},{9,11},{10,... | collective-permute-start | bytes 147464 | tf_op jit(solution)/shard_map/ppermute | solution.py:365
  31.6 3.2 %collective-permute-start.7 = (bf16[1536,128]{1,0:T(8,128)(2,1)S(1)}, bf16[1536,128]{1,0:T(8,128)(2,1)S(1)}, u32[]{:S(2)}, u32[]{:S(2)}) collective-permute-start(bf16[1536,128]{1,0:T(8,128)(2,1)S(1)} %collective-permute-done.2.x2), channel_id=1, source_target_pairs={{0,1},{1,0},{2,3},{3,2},{4,5},{5,4},{6,7},{7,6},{8,9},{9,8},{10,11... | collective-permute-start | bytes 1179656 | tf_op jit(solution)/shard_map/ppermute | solution.py:365
  32.7 2.9 %collective-permute-start.12 = (bf16[96,128]{1,0:T(8,128)(2,1)S(1)}, bf16[96,128]{1,0:T(8,128)(2,1)S(1)}, u32[]{:S(2)}, u32[]{:S(2)}) collective-permute-start(bf16[96,128]{1,0:T(8,128)(2,1)S(1)} %get-tuple-element.83), channel_id=1, source_target_pairs={{0,1},{1,0},{2,3},{3,2},{4,5},{5,4},{6,7},{7,6},{8,9},{9,8},{10,11... | collective-permute-start | bytes 73736 | tf_op jit(solution)/shard_map/ppermute | solution.py:365
  33.3 4.0 %collective-permute-start.13 = (bf16[96,128]{1,0:T(8,128)(2,1)S(1)}, bf16[96,128]{1,0:T(8,128)(2,1)S(1)}, u32[]{:S(2)}, u32[]{:S(2)}) collective-permute-start(bf16[96,128]{1,0:T(8,128)(2,1)S(1)} %get-tuple-element.84), channel_id=1, source_target_pairs={{0,2},{1,3},{2,0},{3,1},{4,6},{5,7},{6,4},{7,5},{8,10},{9,11},{10,... | collective-permute-start | bytes 73736 | tf_op jit(solution)/shard_map/ppermute | solution.py:365
  33.8 3.5 %collective-permute-start.14 = (bf16[96,128]{1,0:T(8,128)(2,1)S(1)}, bf16[96,128]{1,0:T(8,128)(2,1)S(1)}, u32[]{:S(2)}, u32[]{:S(2)}) collective-permute-start(bf16[96,128]{1,0:T(8,128)(2,1)S(1)} %get-tuple-element.85), channel_id=1, source_target_pairs={{0,3},{1,2},{2,1},{3,0},{4,7},{5,6},{6,5},{7,4},{8,11},{9,10},{10,... | collective-permute-start | bytes 73736 | tf_op jit(solution)/shard_map/ppermute | solution.py:365
  34.8 2.6 %copy-start = (bf16[768,768]{1,0:T(8,128)(2,1)S(1)}, bf16[768,768]{1,0:T(8,128)(2,1)}, u32[]{:S(2)}) copy-start(bf16[768,768]{1,0:T(8,128)(2,1)} %w_ref.1) | copy-start | bytes 3538948

commit v4 on v3

--- a/solution.py
+++ b/solution.py
@@ -489,7 +489,6 @@
         acc, top = spread_far(acc, top, *parts, far_rate, my_offsets)
         m_own, m_core, m_far = packed_mains(acc)
 
-    m_far, q23_other = lax.optimization_barrier((m_far, q23_other))
     y_in = partner(m_far, "head", 2)
     core_in = partner(m_core, "head", 1)
 
@@ -511,7 +510,6 @@
         [whole] * 6,
     )(q23, q23_other, *fars)
     got = partner(send, "seq", 1)
-    y_in, part = lax.optimization_barrier((y_in, part))
     y_core = partner(y_in, "head", 1)
 
     patches = call(

time: 40.2 us -> 39.1 us (0.973)
  waiting for transfers between devices: 4.3 us -> 3.58 us
    ppermute x15, waiting for transfers between devices: 4.3 us -> 3.58 us  [partner(): return lax.ppermute(block, axis, [(i, i ^ apart) for i in range(count)])]
  transfers between devices with their start and end apart: 15 -> 15, of which waited for: 4 -> 4; matrix products, arithmetic and copies ran while one was open for 0% -> 0% of each run, Pallas kernels for 40% -> 41%
where the time goes in v4:
time: 39.1 us; the launch traced here: 39 us
  Pallas kernels  20.6 us (53%)
  starting transfers between devices  14.5 us (37%)
  waiting for transfers between devices  3.58 us (9%)
    ppermute x15, starting transfers between devices, partner(): return lax.ppermute(block, axis, [(i, i ^ apart) for i in range(count)])  14.5 us
    pallas_call x1, Pallas kernels, local(): call(local_kernel, 'local', [acc_shape] * 2 + [((main, LANES), BF16)] * 2...  7.86 us
    ppermute x15, waiting for transfers between devices, partner(): return lax.ppermute(block, axis, [(i, i ^ apart) for i in range(count)])  3.58 us
    pallas_call x1, Pallas kernels, local(): call(functools.partial(pair_kernel, dils), 'pair', [((n1 * 3 // 8, LANES)...  3.5 us
    pallas_call x1, Pallas kernels, local(): call(functools.partial(project_kernel, dils), 'project', [(out_shape, BF1...  2.51 us
    pallas_call x1, Pallas kernels, local(): call(functools.partial(select_kernel, dils), 'select', [(queries.shape, B...  2.01 us
    pallas_call x1, Pallas kernels, local(): call(functools.partial(far_kernel, branches), 'far', [far_shape] * 2 + [(...  1.43 us
    pallas_call x1, Pallas kernels, local(): call(functools.partial(query_kernel, dils), 'query', [((heads, n1, LANES)...  1.31 us
  transfers between devices with their start and end apart: 15, of which 4 were waited for; matrix products, arithmetic and copies ran while one was open for 0% of the time, Pallas kernels for 41%

profile of v4, /device:TPU:0, one launch (start us, length us, event | category | flops | bytes accessed | tf_op | source)
XLA Modules:
  0.0 39.0 jit_solution(4084658282721222220)
XLA Ops:
  0.0 2.0 %select.1 = (bf16[192,2048]{1,0:T(8,128)(2,1)S(1)}, bf16[192,2048]{1,0:T(8,128)(2,1)S(1)}, bf16[192,2048]{1,0:T(8,128)(2,1)S(1)}, bf16[3,512,128]{2,1,0:T(8,128)(2,1)S(1)}, bf16[2,3,128,128]{3,2,1,0:T(8,128)(2,1)S(1)}) custom-call(s32[3,12]{1,0:T(4,128)} %off_ref.7, bf16[192,2048]{1,0:T(8,128)(2,1)} %q_hbm.1, bf16[192,2048]{1,0:T(8,128)(2,1)} %k_hbm.1, ...), custom_call_target="tpu_custom_call" | custom-call | flops 6000000000 | bytes 1024 | tf_op jit(solution)/shard_map/select/pallas_call | solution.py:447
  2.0 3.1 %collective-permute-start.7 = (bf16[2,3,128,128]{3,2,1,0:T(8,128)(2,1)S(1)}, bf16[2,3,128,128]{3,2,1,0:T(8,128)(2,1)S(1)}, u32[]{:S(2)}, u32[]{:S(2)}) collective-permute-start(bf16[2,3,128,128]{3,2,1,0:T(8,128)(2,1)S(1)} %get-tuple-element.67.kv0), channel_id=1, source_target_pairs={{0,8},{4,12},{8,0},{12,4},{16,24},{20,28},{24,16},{28,20},{1,9},{5... | collective-permute-start | bytes 589832 | tf_op jit(solution)/shard_map/ppermute | solution.py:365
  5.1 2.6 %collective-permute-start.8 = (bf16[2,3,128,128]{3,2,1,0:T(8,128)(2,1)S(1)}, bf16[2,3,128,128]{3,2,1,0:T(8,128)(2,1)S(1)}, u32[]{:S(2)}, u32[]{:S(2)}) collective-permute-start(bf16[2,3,128,128]{3,2,1,0:T(8,128)(2,1)S(1)} %get-tuple-element.67.kv0), channel_id=1, source_target_pairs={{0,16},{4,20},{8,24},{12,28},{16,0},{20,4},{24,8},{28,12},{1,17},{... | collective-permute-start | bytes 589832 | tf_op jit(solution)/shard_map/ppermute | solution.py:365
  7.7 1.7 %collective-permute-start.3 = (bf16[3,512,128]{2,1,0:T(8,128)(2,1)S(1)}, bf16[3,512,128]{2,1,0:T(8,128)(2,1)S(1)}, u32[]{:S(2)}, u32[]{:S(2)}) collective-permute-start(bf16[3,512,128]{2,1,0:T(8,128)(2,1)S(1)} %get-tuple-element.51.own_ref), channel_id=1, source_target_pairs={{0,4},{4,0},{8,12},{12,8},{16,20},{20,16},{24,28},{28,24},{1,5},{5... | collective-permute-start | bytes 1179656 | tf_op jit(solution)/shard_map/ppermute | solution.py:365
  9.4 1.3 %query.1 = (bf16[3,512,128]{2,1,0:T(8,128)(2,1)S(1)}, bf16[3,128,128]{2,1,0:T(8,128)(2,1)S(1)}) custom-call(s32[3,12]{1,0:T(4,128)} %off_ref.7, bf16[192,2048]{1,0:T(8,128)(2,1)S(1)} %get-tuple-element.44.q_ref), custom_call_target="tpu_custom_call" | custom-call | flops 4000000000 | bytes 1024 | tf_op jit(solution)/shard_map/query/pallas_call | solution.py:461
  10.7 0.4 collective-permute-start.10
  11.1 7.9 %local.1 = (f32[3,2048,128]{2,1,0:T(8,128)S(1)}, f32[3,2048,128]{2,1,0:T(8,128)S(1)}, bf16[768,128]{1,0:T(8,128)(2,1)S(1)}, bf16[768,128]{1,0:T(8,128)(2,1)S(1)}, bf16[1536,128]{1,0:T(8,128)(2,1)S(1)}) custom-call(bf16[192,2048]{1,0:T(8,128)(2,1)S(1)} %get-tuple-element.44.q_ref, bf16[192,2048]{1,0:T(8,128)(2,1)S(1)} %get-tuple-element.45.k_ref, ...), custom_call_target="tpu_custom_call" | custom-call | flops 24999999488 | bytes 1024 | tf_op jit(solution)/shard_map/local/pallas_call | solution.py:477
  19.0 0.1 collective-permute-done.3.other_ref
  19.0 1.7 %collective-permute-start.1 = (bf16[1536,128]{1,0:T(8,128)(2,1)S(1)}, bf16[1536,128]{1,0:T(8,128)(2,1)S(1)}, u32[]{:S(2)}, u32[]{:S(2)}) collective-permute-start(bf16[1536,128]{1,0:T(8,128)(2,1)S(1)} %get-tuple-element.49), channel_id=1, source_target_pairs={{0,2},{1,3},{2,0},{3,1},{4,6},{5,7},{6,4},{7,5},{8,10},{9,11},{10,... | collective-permute-start | bytes 1179656 | tf_op jit(solution)/shard_map/ppermute | solution.py:365
  20.8 3.5 %pair.1 = (bf16[192,128]{1,0:T(8,128)(2,1)S(1)}, bf16[192,128]{1,0:T(8,128)(2,1)S(1)}, bf16[192,128]{1,0:T(8,128)(2,1)S(1)}, bf16[192,128]{1,0:T(8,128)(2,1)S(1)...) custom-call(s32[3,12]{1,0:T(4,128)S(1)} %copy-done.1, ...), custom_call_target="tpu_custom_call", output_to_operand_aliasing={{6}: (4, {}), {7}: (5, {})} | custom-call | flops 3000000000 | bytes 1024 | tf_op jit(solution)/shard_map/pair/pallas_call | solution.py:496
  24.3 1.4 %far.1 = (f32[2,3,128,128]{3,2,1,0:T(8,128)S(1)}, f32[2,3,128,128]{3,2,1,0:T(8,128)S(1)}, bf16[3,160,128]{2,1,0:T(8,128)(2,1)S(1)}) custom-call(bf16[3,128,128]{2,1,0:T(8,128)(2,1)S(1)} %get-tuple-element.66.q_own, bf16[3,128,128]{2,1,0:T(8,128)(2,1)S(1)} %collective-permute-done.10.q_other, bf16[2,3,128,128]{3,2,1,0:T(8,128)(2,1)S(1)} %get-tuple-element.67.kv0, ...), custom_call_target="tpu_custom_call" | custom-call | flops 1000000000 | bytes 1024 | tf_op jit(solution)/shard_map/far/pallas_call | solution.py:506
  25.8 1.6 %collective-permute-start.11 = (bf16[3,160,128]{2,1,0:T(8,128)(2,1)S(1)}, bf16[3,160,128]{2,1,0:T(8,128)(2,1)S(1)}, u32[]{:S(2)}, u32[]{:S(2)}) collective-permute-start(bf16[3,160,128]{2,1,0:T(8,128)(2,1)S(1)} %get-tuple-element.73), channel_id=1, source_target_pairs={{0,4},{4,0},{8,12},{12,8},{16,20},{20,16},{24,28},{28,24},{1,5},{5... | collective-permute-start | bytes 368648 | tf_op jit(solution)/shard_map/ppermute | solution.py:365
  27.3 0.5 %collective-permute-start.4 = (bf16[192,128]{1,0:T(8,128)(2,1)S(1)}, bf16[192,128]{1,0:T(8,128)(2,1)S(1)}, u32[]{:S(2)}, u32[]{:S(2)}) collective-permute-start(bf16[192,128]{1,0:T(8,128)(2,1)S(1)} %get-tuple-element.57), channel_id=1, source_target_pairs={{0,1},{1,0},{2,3},{3,2},{4,5},{5,4},{6,7},{7,6},{8,9},{9,8},{10,11... | collective-permute-start | bytes 147464 | tf_op jit(solution)/shard_map/ppermute | solution.py:365
  27.8 0.5 %collective-permute-start.5 = (bf16[192,128]{1,0:T(8,128)(2,1)S(1)}, bf16[192,128]{1,0:T(8,128)(2,1)S(1)}, u32[]{:S(2)}, u32[]{:S(2)}) collective-permute-start(bf16[192,128]{1,0:T(8,128)(2,1)S(1)} %get-tuple-element.58), channel_id=1, source_target_pairs={{0,2},{1,3},{2,0},{3,1},{4,6},{5,7},{6,4},{7,5},{8,10},{9,11},{10,... | collective-permute-start | bytes 147464 | tf_op jit(solution)/shard_map/ppermute | solution.py:365
  28.3 0.5 %collective-permute-done.1.x2 = bf16[1536,128]{1,0:T(8,128)(2,1)S(1)} collective-permute-done((bf16[1536,128]{1,0:T(8,128)(2,1)S(1)}, bf16[1536,128]{1,0:T(8,128)(2,1)S(1)}, u32[]{:S(2)}, u32[]{:S(2)}) %collective-permute-start.1) | collective-permute-done | bytes 393248 | tf_op jit(solution)/shard_map/ppermute | solution.py:365
  28.8 0.4 %collective-permute-start.6 = (bf16[192,128]{1,0:T(8,128)(2,1)S(1)}, bf16[192,128]{1,0:T(8,128)(2,1)S(1)}, u32[]{:S(2)}, u32[]{:S(2)}) collective-permute-start(bf16[192,128]{1,0:T(8,128)(2,1)S(1)} %get-tuple-element.59), channel_id=1, source_target_pairs={{0,3},{1,2},{2,1},{3,0},{4,7},{5,6},{6,5},{7,4},{8,11},{9,10},{10,... | collective-permute-start | bytes 147464 | tf_op jit(solution)/shard_map/ppermute | solution.py:365
  29.2 1.5 %collective-permute-done.11.got_ref = bf16[3,160,128]{2,1,0:T(8,128)(2,1)S(1)} collective-permute-done((bf16[3,160,128]{2,1,0:T(8,128)(2,1)S(1)}, bf16[3,160,128]{2,1,0:T(8,128)(2,1)S(1)}, u32[]{:S(2)}, u32[]{:S(2)}) %collective-permute-start.11) | collective-permute-done | bytes 122912 | tf_op jit(solution)/shard_map/ppermute | solution.py:365
  30.7 1.2 %patch.1 = (bf16[96,128]{1,0:T(8,128)(2,1)S(1)}, bf16[96,128]{1,0:T(8,128)(2,1)S(1)}, bf16[96,128]{1,0:T(8,128)(2,1)S(1)}, bf16[96,128]{1,0:T(8,128)(2,1)S(1)}) custom-call(s32[3,12]{1,0:T(4,128)S(1)} %copy-done.1, f32[2,3,128,128]{3,2,1,0:T(8,128)S(1)} %get-tuple-element.64.cur_ref, f32[2,3,128,128]{3,2,1,0:T(8,128)S(1)} %get-tuple-element.65.cur_top, ...), custom_call_target="tpu_custom_call" | custom-call | flops 5000000000 | bytes 1024 | tf_op jit(solution)/shard_map/patch/pallas_call | solution.py:515
  31.9 0.6 %collective-permute-start.12 = (bf16[96,128]{1,0:T(8,128)(2,1)S(1)}, bf16[96,128]{1,0:T(8,128)(2,1)S(1)}, u32[]{:S(2)}, u32[]{:S(2)}) collective-permute-start(bf16[96,128]{1,0:T(8,128)(2,1)S(1)} %get-tuple-element.75), channel_id=1, source_target_pairs={{0,1},{1,0},{2,3},{3,2},{4,5},{5,4},{6,7},{7,6},{8,9},{9,8},{10,11... | collective-permute-start | bytes 73736 | tf_op jit(solution)/shard_map/ppermute | solution.py:365
  32.5 0.3 collective-permute-start.13
  32.8 1.2 %collective-permute-start.14 = (bf16[96,128]{1,0:T(8,128)(2,1)S(1)}, bf16[96,128]{1,0:T(8,128)(2,1)S(1)}, u32[]{:S(2)}, u32[]{:S(2)}) collective-permute-start(bf16[96,128]{1,0:T(8,128)(2,1)S(1)} %get-tuple-element.77), channel_id=1, source_target_pairs={{0,3},{1,2},{2,1},{3,0},{4,7},{5,6},{6,5},{7,4},{8,11},{9,10},{10,... | collective-permute-start | bytes 73736 | tf_op jit(solution)/shard_map/ppermute | solution.py:365
  33.9 0.9 %arrange.1 = (f32[4,512,128]{2,1,0:T(8,128)S(1)}, f32[2,512,128]{2,1,0:T(8,128)S(1)}) custom-call(s32[3,12]{1,0:T(4,128)S(1)} %copy-done.1, bf16[768,128]{1,0:T(8,128)(2,1)S(1)} %get-tuple-element.47.x0, bf16[768,128]{1,0:T(8,128)(2,1)S(1)} %collective-permute-done.x1, bf16[1536,128]{1,0:T(8,128)(2,1)S(1)} %collective-permute-done.1.x2, ...), custom_call_target="tpu_custom_call" | custom-call | flops 4000000000 | bytes 1024 | tf_op jit(solution)/shard_map/arrange/pallas_call | solution.py:526
  34.8 1.5 %collective-permute-done.13.p2 = bf16[96,128]{1,0:T(8,128)(2,1)S(1)} collective-permute-done((bf16[96,128]{1,0:T(8,128)(2,1)S(1)}, bf16[96,128]{1,0:T(8,128)(2,1)S(1)}, u32[]{:S(2)}, u32[]{:S(2)}) %collective-permute-start.13) | collective-permute-done | bytes 24608 | tf_op jit(solution)/shard_map/ppermute | solution.py:365
  36.3 2.5 %project.1 = (bf16[512,768]{1,0:T(8,128)(2,1)}, f32[4,512,128]{2,1,0:T(8,128)S(1)}, f32[2,512,128]{2,1,0:T(8,128)S(1)}) custom-call(s32[3,12]{1,0:T(4,128)S(1)} %copy-done.1, f32[4,512,128]{2,1,0:T(8,128)S(1)} %get-tuple-element.60.pairs_in, f32[2,512,128]{2,1,0:T(8,128)S(1)} %get-tuple-element.61.lasts_in, ...), custom_call_target="tpu_custom_call", output_to_operand_aliasing={{1}: (1, {}), {2}: (2, {})} | custom-call | flops 6000000000 | bytes 1024 | tf_op jit(solution)/shard_map/project/pallas_call | solution.py:529
  (18 shorter events, 0.0 us)
Async XLA Ops:
  2.0 22.3 %collective-permute-start.7 = (bf16[2,3,128,128]{3,2,1,0:T(8,128)(2,1)S(1)}, bf16[2,3,128,128]{3,2,1,0:T(8,128)(2,1)S(1)}, u32[]{:S(2)}, u32[]{:S(2)}) collective-permute-start(bf16[2,3,128,128]{3,2,1,0:T(8,128)(2,1)S(1)} %get-tuple-element.67.kv0), channel_id=1, source_target_pairs={{0,8},{4,12},{8,0},{12,4},{16,24},{20,28},{24,16},{28,20},{1,9},{5... | collective-permute-start | bytes 589832 | tf_op jit(solution)/shard_map/ppermute | solution.py:365
  5.1 19.2 %collective-permute-start.8 = (bf16[2,3,128,128]{3,2,1,0:T(8,128)(2,1)S(1)}, bf16[2,3,128,128]{3,2,1,0:T(8,128)(2,1)S(1)}, u32[]{:S(2)}, u32[]{:S(2)}) collective-permute-start(bf16[2,3,128,128]{3,2,1,0:T(8,128)(2,1)S(1)} %get-tuple-element.67.kv0), channel_id=1, source_target_pairs={{0,16},{4,20},{8,24},{12,28},{16,0},{20,4},{24,8},{28,12},{1,17},{... | collective-permute-start | bytes 589832 | tf_op jit(solution)/shard_map/ppermute | solution.py:365
  7.7 16.6 %collective-permute-start.9 = (bf16[2,3,128,128]{3,2,1,0:T(8,128)(2,1)S(1)}, bf16[2,3,128,128]{3,2,1,0:T(8,128)(2,1)S(1)}, u32[]{:S(2)}, u32[]{:S(2)}) collective-permute-start(bf16[2,3,128,128]{3,2,1,0:T(8,128)(2,1)S(1)} %get-tuple-element.67.kv0), channel_id=1, source_target_pairs={{0,24},{4,28},{8,16},{12,20},{16,8},{20,12},{24,0},{28,4},{1,25},{... | collective-permute-start | bytes 589832 | tf_op jit(solution)/shard_map/ppermute | solution.py:365
  7.7 11.3 %collective-permute-start.3 = (bf16[3,512,128]{2,1,0:T(8,128)(2,1)S(1)}, bf16[3,512,128]{2,1,0:T(8,128)(2,1)S(1)}, u32[]{:S(2)}, u32[]{:S(2)}) collective-permute-start(bf16[3,512,128]{2,1,0:T(8,128)(2,1)S(1)} %get-tuple-element.51.own_ref), channel_id=1, source_target_pairs={{0,4},{4,0},{8,12},{12,8},{16,20},{20,16},{24,28},{28,24},{1,5},{5... | collective-permute-start | bytes 1179656 | tf_op jit(solution)/shard_map/ppermute | solution.py:365
  10.7 13.6 %collective-permute-start.10 = (bf16[3,128,128]{2,1,0:T(8,128)(2,1)S(1)}, bf16[3,128,128]{2,1,0:T(8,128)(2,1)S(1)}, u32[]{:S(2)}, u32[]{:S(2)}) collective-permute-start(bf16[3,128,128]{2,1,0:T(8,128)(2,1)S(1)} %get-tuple-element.66.q_own), channel_id=1, source_target_pairs={{0,4},{4,0},{8,12},{12,8},{16,20},{20,16},{24,28},{28,24},{1,5},{5... | collective-permute-start | bytes 294920 | tf_op jit(solution)/shard_map/ppermute | solution.py:365
  11.1 9.7 %copy-start.1 = (s32[3,12]{1,0:T(4,128)S(1)}, s32[3,12]{1,0:T(4,128)}, u32[]{:S(2)}) copy-start(s32[3,12]{1,0:T(4,128)} %off_ref.7) | copy-start | bytes 436
  19.0 9.8 %collective-permute-start.1 = (bf16[1536,128]{1,0:T(8,128)(2,1)S(1)}, bf16[1536,128]{1,0:T(8,128)(2,1)S(1)}, u32[]{:S(2)}, u32[]{:S(2)}) collective-permute-start(bf16[1536,128]{1,0:T(8,128)(2,1)S(1)} %get-tuple-element.49), channel_id=1, source_target_pairs={{0,2},{1,3},{2,0},{3,1},{4,6},{5,7},{6,4},{7,5},{8,10},{9,11},{10,... | collective-permute-start | bytes 1179656 | tf_op jit(solution)/shard_map/ppermute | solution.py:365
  25.8 4.9 %collective-permute-start.11 = (bf16[3,160,128]{2,1,0:T(8,128)(2,1)S(1)}, bf16[3,160,128]{2,1,0:T(8,128)(2,1)S(1)}, u32[]{:S(2)}, u32[]{:S(2)}) collective-permute-start(bf16[3,160,128]{2,1,0:T(8,128)(2,1)S(1)} %get-tuple-element.73), channel_id=1, source_target_pairs={{0,4},{4,0},{8,12},{12,8},{16,20},{20,16},{24,28},{28,24},{1,5},{5... | collective-permute-start | bytes 368648 | tf_op jit(solution)/shard_map/ppermute | solution.py:365
  27.3 4.6 %collective-permute-start = (bf16[768,128]{1,0:T(8,128)(2,1)S(1)}, bf16[768,128]{1,0:T(8,128)(2,1)S(1)}, u32[]{:S(2)}, u32[]{:S(2)}) collective-permute-start(bf16[768,128]{1,0:T(8,128)(2,1)S(1)} %get-tuple-element.48), channel_id=1, source_target_pairs={{0,1},{1,0},{2,3},{3,2},{4,5},{5,4},{6,7},{7,6},{8,9},{9,8},{10,11... | collective-permute-start | bytes 589832 | tf_op jit(solution)/shard_map/ppermute | solution.py:365
  27.3 5.1 %collective-permute-start.4 = (bf16[192,128]{1,0:T(8,128)(2,1)S(1)}, bf16[192,128]{1,0:T(8,128)(2,1)S(1)}, u32[]{:S(2)}, u32[]{:S(2)}) collective-permute-start(bf16[192,128]{1,0:T(8,128)(2,1)S(1)} %get-tuple-element.57), channel_id=1, source_target_pairs={{0,1},{1,0},{2,3},{3,2},{4,5},{5,4},{6,7},{7,6},{8,9},{9,8},{10,11... | collective-permute-start | bytes 147464 | tf_op jit(solution)/shard_map/ppermute | solution.py:365
  27.8 4.9 %collective-permute-start.5 = (bf16[192,128]{1,0:T(8,128)(2,1)S(1)}, bf16[192,128]{1,0:T(8,128)(2,1)S(1)}, u32[]{:S(2)}, u32[]{:S(2)}) collective-permute-start(bf16[192,128]{1,0:T(8,128)(2,1)S(1)} %get-tuple-element.58), channel_id=1, source_target_pairs={{0,2},{1,3},{2,0},{3,1},{4,6},{5,7},{6,4},{7,5},{8,10},{9,11},{10,... | collective-permute-start | bytes 147464 | tf_op jit(solution)/shard_map/ppermute | solution.py:365
  28.8 5.1 %collective-permute-start.6 = (bf16[192,128]{1,0:T(8,128)(2,1)S(1)}, bf16[192,128]{1,0:T(8,128)(2,1)S(1)}, u32[]{:S(2)}, u32[]{:S(2)}) collective-permute-start(bf16[192,128]{1,0:T(8,128)(2,1)S(1)} %get-tuple-element.59), channel_id=1, source_target_pairs={{0,3},{1,2},{2,1},{3,0},{4,7},{5,6},{6,5},{7,4},{8,11},{9,10},{10,... | collective-permute-start | bytes 147464 | tf_op jit(solution)/shard_map/ppermute | solution.py:365
  30.7 3.2 %collective-permute-start.2 = (bf16[1536,128]{1,0:T(8,128)(2,1)S(1)}, bf16[1536,128]{1,0:T(8,128)(2,1)S(1)}, u32[]{:S(2)}, u32[]{:S(2)}) collective-permute-start(bf16[1536,128]{1,0:T(8,128)(2,1)S(1)} %collective-permute-done.1.x2), channel_id=1, source_target_pairs={{0,1},{1,0},{2,3},{3,2},{4,5},{5,4},{6,7},{7,6},{8,9},{9,8},{10,11... | collective-permute-start | bytes 1179656 | tf_op jit(solution)/shard_map/ppermute | solution.py:365
  31.9 2.9 %collective-permute-start.12 = (bf16[96,128]{1,0:T(8,128)(2,1)S(1)}, bf16[96,128]{1,0:T(8,128)(2,1)S(1)}, u32[]{:S(2)}, u32[]{:S(2)}) collective-permute-start(bf16[96,128]{1,0:T(8,128)(2,1)S(1)} %get-tuple-element.75), channel_id=1, source_target_pairs={{0,1},{1,0},{2,3},{3,2},{4,5},{5,4},{6,7},{7,6},{8,9},{9,8},{10,11... | collective-permute-start | bytes 73736 | tf_op jit(solution)/shard_map/ppermute | solution.py:365
  32.5 3.8 %collective-permute-start.13 = (bf16[96,128]{1,0:T(8,128)(2,1)S(1)}, bf16[96,128]{1,0:T(8,128)(2,1)S(1)}, u32[]{:S(2)}, u32[]{:S(2)}) collective-permute-start(bf16[96,128]{1,0:T(8,128)(2,1)S(1)} %get-tuple-element.76), channel_id=1, source_target_pairs={{0,2},{1,3},{2,0},{3,1},{4,6},{5,7},{6,4},{7,5},{8,10},{9,11},{10,... | collective-permute-start | bytes 73736 | tf_op jit(solution)/shard_map/ppermute | solution.py:365
  32.8 3.5 %collective-permute-start.14 = (bf16[96,128]{1,0:T(8,128)(2,1)S(1)}, bf16[96,128]{1,0:T(8,128)(2,1)S(1)}, u32[]{:S(2)}, u32[]{:S(2)}) collective-permute-start(bf16[96,128]{1,0:T(8,128)(2,1)S(1)} %get-tuple-element.77), channel_id=1, source_target_pairs={{0,3},{1,2},{2,1},{3,0},{4,7},{5,6},{6,5},{7,4},{8,11},{9,10},{10,... | collective-permute-start | bytes 73736 | tf_op jit(solution)/shard_map/ppermute | solution.py:365
  33.9 2.4 %copy-start = (bf16[768,768]{1,0:T(8,128)(2,1)S(1)}, bf16[768,768]{1,0:T(8,128)(2,1)}, u32[]{:S(2)}) copy-start(bf16[768,768]{1,0:T(8,128)(2,1)} %w_ref.1) | copy-start | bytes 3538948

commit v5 on v4

--- a/solution.py
+++ b/solution.py
@@ -349,15 +349,22 @@
 
     ws = [jnp.concatenate([w_rows(2 * t, 0, LANES), w_rows(2 * t + 1, 0, LANES)], 0) for t in range(2)]
     ws.append(jnp.concatenate([w_rows(s, LANES, DH) for s in range(4)], 0))
-    total = None
-    for t in range(3):
-        halves = (pairs[2 * t], pairs[2 * t + 1]) if t < 2 else (lasts[0], lasts[1])
-        part = dot(jnp.concatenate(halves, 1).astype(BF16), ws[t], NN)
-        total = part if total is None else total + part
-    out_ref[...] = total.astype(BF16)
-    copy = pltpu.make_async_copy(out_ref, out_hbm, sem)
-    copy.start()
-    copy.wait()
+    xs = [jnp.concatenate([pairs[0], pairs[1]], 1), jnp.concatenate([pairs[2], pairs[3]], 1)]
+    xs = [x.astype(BF16) for x in xs + [jnp.concatenate([lasts[0], lasts[1]], 1)]]
+    step = out_ref.shape[1] // 3
+    copies = []
+    for c in range(3):
+        cols = slice(c * step, (c + 1) * step)
+        total = None
+        for x, w in zip(xs, ws):
+            part = dot(x, w[:, cols], NN)
+            total = part if total is None else total + part
+        out_ref[:, cols] = total.astype(BF16)
+        at = pl.ds(c * step, step)
+        copies.append(pltpu.make_async_copy(out_ref.at[:, at], out_hbm.at[:, at], sem.at[c]))
+        copies[-1].start()
+    for copy in copies:
+        copy.wait()
 
 
 def partner(block, axis, apart):
@@ -456,7 +463,7 @@
             pltpu.SemaphoreType.DMA,
         ],
     )(*stay)
-    fars = [far] + [partner(far, "seq", apart) for apart in (2, 4, 6)]
+    fars = [far] + [partner(far, "seq", apart) for apart in (4, 6, 2)]
 
     q1, q23 = call(
         functools.partial(query_kernel, dils),
@@ -531,7 +538,7 @@
         "project",
         [(out_shape, BF16)] + spread_shapes,
         [smem] + [whole] * 7,
-        [pltpu.VMEM(out_shape, BF16), pltpu.SemaphoreType.DMA],
+        [pltpu.VMEM(out_shape, BF16), pltpu.SemaphoreType.DMA((3,))],
         aliases={1: 1, 2: 2},
         spaces=(pltpu.HBM, pltpu.VMEM, pltpu.VMEM),
     )(offsets, pairs, lasts, *fixes, out_weight)

time: 39.1 us -> 39.1 us (level)
  starting transfers between devices: 14.5 us -> 14.1 us
    ppermute x15, starting transfers between devices: 14.5 us -> 14.1 us  [partner(): return lax.ppermute(block, axis, [(i, i ^ apart) for i in range(count)])]
where the time goes in v5:
time: 39.1 us; the launch traced here: 38.9 us
  Pallas kernels  20.6 us (53%)
  starting transfers between devices  14.1 us (36%)
  waiting for transfers between devices  3.96 us (10%)
    ppermute x15, starting transfers between devices, partner(): return lax.ppermute(block, axis, [(i, i ^ apart) for i in range(count)])  14.1 us
    pallas_call x1, Pallas kernels, local(): call(local_kernel, 'local', [acc_shape] * 2 + [((main, LANES), BF16)] * 2...  7.85 us
    ppermute x15, waiting for transfers between devices, partner(): return lax.ppermute(block, axis, [(i, i ^ apart) for i in range(count)])  3.96 us
    pallas_call x1, Pallas kernels, local(): call(functools.partial(pair_kernel, dils), 'pair', [((n1 * 3 // 8, LANES)...  3.5 us
    pallas_call x1, Pallas kernels, local(): call(functools.partial(project_kernel, dils), 'project', [(out_shape, BF1...  2.45 us
    pallas_call x1, Pallas kernels, local(): call(functools.partial(select_kernel, dils), 'select', [(queries.shape, B...  2.01 us
    pallas_call x1, Pallas kernels, local(): call(functools.partial(far_kernel, branches), 'far', [far_shape] * 2 + [(...  1.43 us
    pallas_call x1, Pallas kernels, local(): call(functools.partial(query_kernel, dils), 'query', [((heads, n1, LANES)...  1.33 us
  transfers between devices with their start and end apart: 15, of which 4 were waited for; matrix products, arithmetic and copies ran while one was open for 0% of the time, Pallas kernels for 41%

profile of v5, /device:TPU:0, one launch (start us, length us, event | category | flops | bytes accessed | tf_op | source)
XLA Modules:
  0.0 38.9 jit_solution(14012120285777087400)
XLA Ops:
  0.0 2.0 %select.1 = (bf16[192,2048]{1,0:T(8,128)(2,1)S(1)}, bf16[192,2048]{1,0:T(8,128)(2,1)S(1)}, bf16[192,2048]{1,0:T(8,128)(2,1)S(1)}, bf16[3,512,128]{2,1,0:T(8,128)(2,1)S(1)}, bf16[2,3,128,128]{3,2,1,0:T(8,128)(2,1)S(1)}) custom-call(s32[3,12]{1,0:T(4,128)} %off_ref.7, bf16[192,2048]{1,0:T(8,128)(2,1)} %q_hbm.1, bf16[192,2048]{1,0:T(8,128)(2,1)} %k_hbm.1, ...), custom_call_target="tpu_custom_call" | custom-call | flops 6000000000 | bytes 1024 | tf_op jit(solution)/shard_map/select/pallas_call | solution.py:454
  2.0 4.1 %collective-permute-start.7 = (bf16[2,3,128,128]{3,2,1,0:T(8,128)(2,1)S(1)}, bf16[2,3,128,128]{3,2,1,0:T(8,128)(2,1)S(1)}, u32[]{:S(2)}, u32[]{:S(2)}) collective-permute-start(bf16[2,3,128,128]{3,2,1,0:T(8,128)(2,1)S(1)} %get-tuple-element.67.kv0), channel_id=1, source_target_pairs={{0,16},{4,20},{8,24},{12,28},{16,0},{20,4},{24,8},{28,12},{1,17},{... | collective-permute-start | bytes 589832 | tf_op jit(solution)/shard_map/ppermute | solution.py:372
  6.1 1.3 %collective-permute-start.8 = (bf16[2,3,128,128]{3,2,1,0:T(8,128)(2,1)S(1)}, bf16[2,3,128,128]{3,2,1,0:T(8,128)(2,1)S(1)}, u32[]{:S(2)}, u32[]{:S(2)}) collective-permute-start(bf16[2,3,128,128]{3,2,1,0:T(8,128)(2,1)S(1)} %get-tuple-element.67.kv0), channel_id=1, source_target_pairs={{0,24},{4,28},{8,16},{12,20},{16,8},{20,12},{24,0},{28,4},{1,25},{... | collective-permute-start | bytes 589832 | tf_op jit(solution)/shard_map/ppermute | solution.py:372
  7.5 0.2 collective-permute-start.9
  7.7 1.5 %collective-permute-start.3 = (bf16[3,512,128]{2,1,0:T(8,128)(2,1)S(1)}, bf16[3,512,128]{2,1,0:T(8,128)(2,1)S(1)}, u32[]{:S(2)}, u32[]{:S(2)}) collective-permute-start(bf16[3,512,128]{2,1,0:T(8,128)(2,1)S(1)} %get-tuple-element.51.own_ref), channel_id=1, source_target_pairs={{0,4},{4,0},{8,12},{12,8},{16,20},{20,16},{24,28},{28,24},{1,5},{5... | collective-permute-start | bytes 1179656 | tf_op jit(solution)/shard_map/ppermute | solution.py:372
  9.2 1.3 %query.1 = (bf16[3,512,128]{2,1,0:T(8,128)(2,1)S(1)}, bf16[3,128,128]{2,1,0:T(8,128)(2,1)S(1)}) custom-call(s32[3,12]{1,0:T(4,128)} %off_ref.7, bf16[192,2048]{1,0:T(8,128)(2,1)S(1)} %get-tuple-element.44.q_ref), custom_call_target="tpu_custom_call" | custom-call | flops 4000000000 | bytes 1024 | tf_op jit(solution)/shard_map/query/pallas_call | solution.py:468
  10.5 0.6 %collective-permute-start.10 = (bf16[3,128,128]{2,1,0:T(8,128)(2,1)S(1)}, bf16[3,128,128]{2,1,0:T(8,128)(2,1)S(1)}, u32[]{:S(2)}, u32[]{:S(2)}) collective-permute-start(bf16[3,128,128]{2,1,0:T(8,128)(2,1)S(1)} %get-tuple-element.66.q_own), channel_id=1, source_target_pairs={{0,4},{4,0},{8,12},{12,8},{16,20},{20,16},{24,28},{28,24},{1,5},{5... | collective-permute-start | bytes 294920 | tf_op jit(solution)/shard_map/ppermute | solution.py:372
  11.1 7.9 %local.1 = (f32[3,2048,128]{2,1,0:T(8,128)S(1)}, f32[3,2048,128]{2,1,0:T(8,128)S(1)}, bf16[768,128]{1,0:T(8,128)(2,1)S(1)}, bf16[768,128]{1,0:T(8,128)(2,1)S(1)}, bf16[1536,128]{1,0:T(8,128)(2,1)S(1)}) custom-call(bf16[192,2048]{1,0:T(8,128)(2,1)S(1)} %get-tuple-element.44.q_ref, bf16[192,2048]{1,0:T(8,128)(2,1)S(1)} %get-tuple-element.45.k_ref, ...), custom_call_target="tpu_custom_call" | custom-call | flops 24999999488 | bytes 1024 | tf_op jit(solution)/shard_map/local/pallas_call | solution.py:484
  19.0 1.5 %collective-permute-start.1 = (bf16[1536,128]{1,0:T(8,128)(2,1)S(1)}, bf16[1536,128]{1,0:T(8,128)(2,1)S(1)}, u32[]{:S(2)}, u32[]{:S(2)}) collective-permute-start(bf16[1536,128]{1,0:T(8,128)(2,1)S(1)} %get-tuple-element.49), channel_id=1, source_target_pairs={{0,2},{1,3},{2,0},{3,1},{4,6},{5,7},{6,4},{7,5},{8,10},{9,11},{10,... | collective-permute-start | bytes 1179656 | tf_op jit(solution)/shard_map/ppermute | solution.py:372
  20.6 3.5 %pair.1 = (bf16[192,128]{1,0:T(8,128)(2,1)S(1)}, bf16[192,128]{1,0:T(8,128)(2,1)S(1)}, bf16[192,128]{1,0:T(8,128)(2,1)S(1)}, bf16[192,128]{1,0:T(8,128)(2,1)S(1)...) custom-call(s32[3,12]{1,0:T(4,128)S(1)} %copy-done.1, ...), custom_call_target="tpu_custom_call", output_to_operand_aliasing={{6}: (4, {}), {7}: (5, {})} | custom-call | flops 3000000000 | bytes 1024 | tf_op jit(solution)/shard_map/pair/pallas_call | solution.py:503
  24.1 1.4 %far.1 = (f32[2,3,128,128]{3,2,1,0:T(8,128)S(1)}, f32[2,3,128,128]{3,2,1,0:T(8,128)S(1)}, bf16[3,160,128]{2,1,0:T(8,128)(2,1)S(1)}) custom-call(bf16[3,128,128]{2,1,0:T(8,128)(2,1)S(1)} %get-tuple-element.66.q_own, bf16[3,128,128]{2,1,0:T(8,128)(2,1)S(1)} %collective-permute-done.10.q_other, bf16[2,3,128,128]{3,2,1,0:T(8,128)(2,1)S(1)} %get-tuple-element.67.kv0, ...), custom_call_target="tpu_custom_call" | custom-call | flops 1000000000 | bytes 1024 | tf_op jit(solution)/shard_map/far/pallas_call | solution.py:513
  25.6 1.6 %collective-permute-start.11 = (bf16[3,160,128]{2,1,0:T(8,128)(2,1)S(1)}, bf16[3,160,128]{2,1,0:T(8,128)(2,1)S(1)}, u32[]{:S(2)}, u32[]{:S(2)}) collective-permute-start(bf16[3,160,128]{2,1,0:T(8,128)(2,1)S(1)} %get-tuple-element.73), channel_id=1, source_target_pairs={{0,4},{4,0},{8,12},{12,8},{16,20},{20,16},{24,28},{28,24},{1,5},{5... | collective-permute-start | bytes 368648 | tf_op jit(solution)/shard_map/ppermute | solution.py:372
  27.1 0.5 %collective-permute-start.4 = (bf16[192,128]{1,0:T(8,128)(2,1)S(1)}, bf16[192,128]{1,0:T(8,128)(2,1)S(1)}, u32[]{:S(2)}, u32[]{:S(2)}) collective-permute-start(bf16[192,128]{1,0:T(8,128)(2,1)S(1)} %get-tuple-element.57), channel_id=1, source_target_pairs={{0,1},{1,0},{2,3},{3,2},{4,5},{5,4},{6,7},{7,6},{8,9},{9,8},{10,11... | collective-permute-start | bytes 147464 | tf_op jit(solution)/shard_map/ppermute | solution.py:372
  27.6 0.5 %collective-permute-start.5 = (bf16[192,128]{1,0:T(8,128)(2,1)S(1)}, bf16[192,128]{1,0:T(8,128)(2,1)S(1)}, u32[]{:S(2)}, u32[]{:S(2)}) collective-permute-start(bf16[192,128]{1,0:T(8,128)(2,1)S(1)} %get-tuple-element.58), channel_id=1, source_target_pairs={{0,2},{1,3},{2,0},{3,1},{4,6},{5,7},{6,4},{7,5},{8,10},{9,11},{10,... | collective-permute-start | bytes 147464 | tf_op jit(solution)/shard_map/ppermute | solution.py:372
  28.2 0.7 %collective-permute-done.1.x2 = bf16[1536,128]{1,0:T(8,128)(2,1)S(1)} collective-permute-done((bf16[1536,128]{1,0:T(8,128)(2,1)S(1)}, bf16[1536,128]{1,0:T(8,128)(2,1)S(1)}, u32[]{:S(2)}, u32[]{:S(2)}) %collective-permute-start.1) | collective-permute-done | bytes 393248 | tf_op jit(solution)/shard_map/ppermute | solution.py:372
  28.8 0.2 collective-permute-start.6
  29.0 1.5 %collective-permute-done.11.got_ref = bf16[3,160,128]{2,1,0:T(8,128)(2,1)S(1)} collective-permute-done((bf16[3,160,128]{2,1,0:T(8,128)(2,1)S(1)}, bf16[3,160,128]{2,1,0:T(8,128)(2,1)S(1)}, u32[]{:S(2)}, u32[]{:S(2)}) %collective-permute-start.11) | collective-permute-done | bytes 122912 | tf_op jit(solution)/shard_map/ppermute | solution.py:372
  30.5 1.2 %patch.1 = (bf16[96,128]{1,0:T(8,128)(2,1)S(1)}, bf16[96,128]{1,0:T(8,128)(2,1)S(1)}, bf16[96,128]{1,0:T(8,128)(2,1)S(1)}, bf16[96,128]{1,0:T(8,128)(2,1)S(1)}) custom-call(s32[3,12]{1,0:T(4,128)S(1)} %copy-done.1, f32[2,3,128,128]{3,2,1,0:T(8,128)S(1)} %get-tuple-element.64.cur_ref, f32[2,3,128,128]{3,2,1,0:T(8,128)S(1)} %get-tuple-element.65.cur_top, ...), custom_call_target="tpu_custom_call" | custom-call | flops 5000000000 | bytes 1024 | tf_op jit(solution)/shard_map/patch/pallas_call | solution.py:522
  31.7 0.6 %collective-permute-start.12 = (bf16[96,128]{1,0:T(8,128)(2,1)S(1)}, bf16[96,128]{1,0:T(8,128)(2,1)S(1)}, u32[]{:S(2)}, u32[]{:S(2)}) collective-permute-start(bf16[96,128]{1,0:T(8,128)(2,1)S(1)} %get-tuple-element.75), channel_id=1, source_target_pairs={{0,1},{1,0},{2,3},{3,2},{4,5},{5,4},{6,7},{7,6},{8,9},{9,8},{10,11... | collective-permute-start | bytes 73736 | tf_op jit(solution)/shard_map/ppermute | solution.py:372
  32.3 0.5 %collective-permute-start.13 = (bf16[96,128]{1,0:T(8,128)(2,1)S(1)}, bf16[96,128]{1,0:T(8,128)(2,1)S(1)}, u32[]{:S(2)}, u32[]{:S(2)}) collective-permute-start(bf16[96,128]{1,0:T(8,128)(2,1)S(1)} %get-tuple-element.76), channel_id=1, source_target_pairs={{0,2},{1,3},{2,0},{3,1},{4,6},{5,7},{6,4},{7,5},{8,10},{9,11},{10,... | collective-permute-start | bytes 73736 | tf_op jit(solution)/shard_map/ppermute | solution.py:372
  32.8 0.9 %collective-permute-start.14 = (bf16[96,128]{1,0:T(8,128)(2,1)S(1)}, bf16[96,128]{1,0:T(8,128)(2,1)S(1)}, u32[]{:S(2)}, u32[]{:S(2)}) collective-permute-start(bf16[96,128]{1,0:T(8,128)(2,1)S(1)} %get-tuple-element.77), channel_id=1, source_target_pairs={{0,3},{1,2},{2,1},{3,0},{4,7},{5,6},{6,5},{7,4},{8,11},{9,10},{10,... | collective-permute-start | bytes 73736 | tf_op jit(solution)/shard_map/ppermute | solution.py:372
  33.7 0.9 %arrange.1 = (f32[4,512,128]{2,1,0:T(8,128)S(1)}, f32[2,512,128]{2,1,0:T(8,128)S(1)}) custom-call(s32[3,12]{1,0:T(4,128)S(1)} %copy-done.1, bf16[768,128]{1,0:T(8,128)(2,1)S(1)} %get-tuple-element.47.x0, bf16[768,128]{1,0:T(8,128)(2,1)S(1)} %collective-permute-done.x1, bf16[1536,128]{1,0:T(8,128)(2,1)S(1)} %collective-permute-done.1.x2, ...), custom_call_target="tpu_custom_call" | custom-call | flops 4000000000 | bytes 1024 | tf_op jit(solution)/shard_map/arrange/pallas_call | solution.py:533
  34.6 1.7 %collective-permute-done.13.p2 = bf16[96,128]{1,0:T(8,128)(2,1)S(1)} collective-permute-done((bf16[96,128]{1,0:T(8,128)(2,1)S(1)}, bf16[96,128]{1,0:T(8,128)(2,1)S(1)}, u32[]{:S(2)}, u32[]{:S(2)}) %collective-permute-start.13) | collective-permute-done | bytes 24608 | tf_op jit(solution)/shard_map/ppermute | solution.py:372
  36.3 2.5 %project.1 = (bf16[512,768]{1,0:T(8,128)(2,1)}, f32[4,512,128]{2,1,0:T(8,128)S(1)}, f32[2,512,128]{2,1,0:T(8,128)S(1)}) custom-call(s32[3,12]{1,0:T(4,128)S(1)} %copy-done.1, f32[4,512,128]{2,1,0:T(8,128)S(1)} %get-tuple-element.60.pairs_in, f32[2,512,128]{2,1,0:T(8,128)S(1)} %get-tuple-element.61.lasts_in, ...), custom_call_target="tpu_custom_call", output_to_operand_aliasing={{1}: (1, {}), {2}: (2, {})} | custom-call | flops 6000000000 | bytes 1024 | tf_op jit(solution)/shard_map/project/pallas_call | solution.py:536
  (18 shorter events, 0.1 us)
Async XLA Ops:
  2.0 22.1 %collective-permute-start.7 = (bf16[2,3,128,128]{3,2,1,0:T(8,128)(2,1)S(1)}, bf16[2,3,128,128]{3,2,1,0:T(8,128)(2,1)S(1)}, u32[]{:S(2)}, u32[]{:S(2)}) collective-permute-start(bf16[2,3,128,128]{3,2,1,0:T(8,128)(2,1)S(1)} %get-tuple-element.67.kv0), channel_id=1, source_target_pairs={{0,16},{4,20},{8,24},{12,28},{16,0},{20,4},{24,8},{28,12},{1,17},{... | collective-permute-start | bytes 589832 | tf_op jit(solution)/shard_map/ppermute | solution.py:372
  6.1 18.0 %collective-permute-start.8 = (bf16[2,3,128,128]{3,2,1,0:T(8,128)(2,1)S(1)}, bf16[2,3,128,128]{3,2,1,0:T(8,128)(2,1)S(1)}, u32[]{:S(2)}, u32[]{:S(2)}) collective-permute-start(bf16[2,3,128,128]{3,2,1,0:T(8,128)(2,1)S(1)} %get-tuple-element.67.kv0), channel_id=1, source_target_pairs={{0,24},{4,28},{8,16},{12,20},{16,8},{20,12},{24,0},{28,4},{1,25},{... | collective-permute-start | bytes 589832 | tf_op jit(solution)/shard_map/ppermute | solution.py:372
  7.5 16.7 %collective-permute-start.9 = (bf16[2,3,128,128]{3,2,1,0:T(8,128)(2,1)S(1)}, bf16[2,3,128,128]{3,2,1,0:T(8,128)(2,1)S(1)}, u32[]{:S(2)}, u32[]{:S(2)}) collective-permute-start(bf16[2,3,128,128]{3,2,1,0:T(8,128)(2,1)S(1)} %get-tuple-element.67.kv0), channel_id=1, source_target_pairs={{0,8},{4,12},{8,0},{12,4},{16,24},{20,28},{24,16},{28,20},{1,9},{5... | collective-permute-start | bytes 589832 | tf_op jit(solution)/shard_map/ppermute | solution.py:372
  7.7 11.3 %collective-permute-start.3 = (bf16[3,512,128]{2,1,0:T(8,128)(2,1)S(1)}, bf16[3,512,128]{2,1,0:T(8,128)(2,1)S(1)}, u32[]{:S(2)}, u32[]{:S(2)}) collective-permute-start(bf16[3,512,128]{2,1,0:T(8,128)(2,1)S(1)} %get-tuple-element.51.own_ref), channel_id=1, source_target_pairs={{0,4},{4,0},{8,12},{12,8},{16,20},{20,16},{24,28},{28,24},{1,5},{5... | collective-permute-start | bytes 1179656 | tf_op jit(solution)/shard_map/ppermute | solution.py:372
  10.5 13.6 %collective-permute-start.10 = (bf16[3,128,128]{2,1,0:T(8,128)(2,1)S(1)}, bf16[3,128,128]{2,1,0:T(8,128)(2,1)S(1)}, u32[]{:S(2)}, u32[]{:S(2)}) collective-permute-start(bf16[3,128,128]{2,1,0:T(8,128)(2,1)S(1)} %get-tuple-element.66.q_own), channel_id=1, source_target_pairs={{0,4},{4,0},{8,12},{12,8},{16,20},{20,16},{24,28},{28,24},{1,5},{5... | collective-permute-start | bytes 294920 | tf_op jit(solution)/shard_map/ppermute | solution.py:372
  11.1 9.5 %copy-start.1 = (s32[3,12]{1,0:T(4,128)S(1)}, s32[3,12]{1,0:T(4,128)}, u32[]{:S(2)}) copy-start(s32[3,12]{1,0:T(4,128)} %off_ref.7) | copy-start | bytes 436
  19.0 9.8 %collective-permute-start.1 = (bf16[1536,128]{1,0:T(8,128)(2,1)S(1)}, bf16[1536,128]{1,0:T(8,128)(2,1)S(1)}, u32[]{:S(2)}, u32[]{:S(2)}) collective-permute-start(bf16[1536,128]{1,0:T(8,128)(2,1)S(1)} %get-tuple-element.49), channel_id=1, source_target_pairs={{0,2},{1,3},{2,0},{3,1},{4,6},{5,7},{6,4},{7,5},{8,10},{9,11},{10,... | collective-permute-start | bytes 1179656 | tf_op jit(solution)/shard_map/ppermute | solution.py:372
  25.6 4.9 %collective-permute-start.11 = (bf16[3,160,128]{2,1,0:T(8,128)(2,1)S(1)}, bf16[3,160,128]{2,1,0:T(8,128)(2,1)S(1)}, u32[]{:S(2)}, u32[]{:S(2)}) collective-permute-start(bf16[3,160,128]{2,1,0:T(8,128)(2,1)S(1)} %get-tuple-element.73), channel_id=1, source_target_pairs={{0,4},{4,0},{8,12},{12,8},{16,20},{20,16},{24,28},{28,24},{1,5},{5... | collective-permute-start | bytes 368648 | tf_op jit(solution)/shard_map/ppermute | solution.py:372
  27.1 4.6 %collective-permute-start = (bf16[768,128]{1,0:T(8,128)(2,1)S(1)}, bf16[768,128]{1,0:T(8,128)(2,1)S(1)}, u32[]{:S(2)}, u32[]{:S(2)}) collective-permute-start(bf16[768,128]{1,0:T(8,128)(2,1)S(1)} %get-tuple-element.48), channel_id=1, source_target_pairs={{0,1},{1,0},{2,3},{3,2},{4,5},{5,4},{6,7},{7,6},{8,9},{9,8},{10,11... | collective-permute-start | bytes 589832 | tf_op jit(solution)/shard_map/ppermute | solution.py:372
  27.1 5.1 %collective-permute-start.4 = (bf16[192,128]{1,0:T(8,128)(2,1)S(1)}, bf16[192,128]{1,0:T(8,128)(2,1)S(1)}, u32[]{:S(2)}, u32[]{:S(2)}) collective-permute-start(bf16[192,128]{1,0:T(8,128)(2,1)S(1)} %get-tuple-element.57), channel_id=1, source_target_pairs={{0,1},{1,0},{2,3},{3,2},{4,5},{5,4},{6,7},{7,6},{8,9},{9,8},{10,11... | collective-permute-start | bytes 147464 | tf_op jit(solution)/shard_map/ppermute | solution.py:372
  27.6 5.1 %collective-permute-start.5 = (bf16[192,128]{1,0:T(8,128)(2,1)S(1)}, bf16[192,128]{1,0:T(8,128)(2,1)S(1)}, u32[]{:S(2)}, u32[]{:S(2)}) collective-permute-start(bf16[192,128]{1,0:T(8,128)(2,1)S(1)} %get-tuple-element.58), channel_id=1, source_target_pairs={{0,2},{1,3},{2,0},{3,1},{4,6},{5,7},{6,4},{7,5},{8,10},{9,11},{10,... | collective-permute-start | bytes 147464 | tf_op jit(solution)/shard_map/ppermute | solution.py:372
  28.8 4.9 %collective-permute-start.6 = (bf16[192,128]{1,0:T(8,128)(2,1)S(1)}, bf16[192,128]{1,0:T(8,128)(2,1)S(1)}, u32[]{:S(2)}, u32[]{:S(2)}) collective-permute-start(bf16[192,128]{1,0:T(8,128)(2,1)S(1)} %get-tuple-element.59), channel_id=1, source_target_pairs={{0,3},{1,2},{2,1},{3,0},{4,7},{5,6},{6,5},{7,4},{8,11},{9,10},{10,... | collective-permute-start | bytes 147464 | tf_op jit(solution)/shard_map/ppermute | solution.py:372
  30.5 3.2 %collective-permute-start.2 = (bf16[1536,128]{1,0:T(8,128)(2,1)S(1)}, bf16[1536,128]{1,0:T(8,128)(2,1)S(1)}, u32[]{:S(2)}, u32[]{:S(2)}) collective-permute-start(bf16[1536,128]{1,0:T(8,128)(2,1)S(1)} %collective-permute-done.1.x2), channel_id=1, source_target_pairs={{0,1},{1,0},{2,3},{3,2},{4,5},{5,4},{6,7},{7,6},{8,9},{9,8},{10,11... | collective-permute-start | bytes 1179656 | tf_op jit(solution)/shard_map/ppermute | solution.py:372
  31.7 2.9 %collective-permute-start.12 = (bf16[96,128]{1,0:T(8,128)(2,1)S(1)}, bf16[96,128]{1,0:T(8,128)(2,1)S(1)}, u32[]{:S(2)}, u32[]{:S(2)}) collective-permute-start(bf16[96,128]{1,0:T(8,128)(2,1)S(1)} %get-tuple-element.75), channel_id=1, source_target_pairs={{0,1},{1,0},{2,3},{3,2},{4,5},{5,4},{6,7},{7,6},{8,9},{9,8},{10,11... | collective-permute-start | bytes 73736 | tf_op jit(solution)/shard_map/ppermute | solution.py:372
  32.3 4.0 %collective-permute-start.13 = (bf16[96,128]{1,0:T(8,128)(2,1)S(1)}, bf16[96,128]{1,0:T(8,128)(2,1)S(1)}, u32[]{:S(2)}, u32[]{:S(2)}) collective-permute-start(bf16[96,128]{1,0:T(8,128)(2,1)S(1)} %get-tuple-element.76), channel_id=1, source_target_pairs={{0,2},{1,3},{2,0},{3,1},{4,6},{5,7},{6,4},{7,5},{8,10},{9,11},{10,... | collective-permute-start | bytes 73736 | tf_op jit(solution)/shard_map/ppermute | solution.py:372
  32.8 3.5 %collective-permute-start.14 = (bf16[96,128]{1,0:T(8,128)(2,1)S(1)}, bf16[96,128]{1,0:T(8,128)(2,1)S(1)}, u32[]{:S(2)}, u32[]{:S(2)}) collective-permute-start(bf16[96,128]{1,0:T(8,128)(2,1)S(1)} %get-tuple-element.77), channel_id=1, source_target_pairs={{0,3},{1,2},{2,1},{3,0},{4,7},{5,6},{6,5},{7,4},{8,11},{9,10},{10,... | collective-permute-start | bytes 73736 | tf_op jit(solution)/shard_map/ppermute | solution.py:372
  33.7 2.6 %copy-start = (bf16[768,768]{1,0:T(8,128)(2,1)S(1)}, bf16[768,768]{1,0:T(8,128)(2,1)}, u32[]{:S(2)}) copy-start(bf16[768,768]{1,0:T(8,128)(2,1)} %w_ref.1) | copy-start | bytes 3538948

commit v6 on v5

--- a/solution.py
+++ b/solution.py
@@ -65,12 +65,12 @@
 
 def pack_pair(even, odd):
     low = lane_of(even.shape) < DH
-    return jnp.where(low, even, odd) / swap(jnp.where(low, odd, even))
+    return jnp.where(low, even, odd) * pl.reciprocal(swap(jnp.where(low, odd, even)))
 
 
 def pack_even(first, second):
     low = lane_of(first.shape) < DH
-    return jnp.where(low, first, swap(second)) / jnp.where(low, swap(first), second)
+    return jnp.where(low, first, swap(second)) * pl.reciprocal(jnp.where(low, swap(first), second))
 
 
 def select_kernel(dils, off_hbm, q_hbm, k_hbm, v_hbm, q_ref, k_ref, v_ref, near_ref, far_ref, kvt, off_ref, sems, off_sem):

time: 39.1 us -> 39.1 us (level)
  no operation moved by 1% of the time
where the time goes in v6:
time: 39.1 us; the launch traced here: 38.9 us
  Pallas kernels  20.6 us (53%)
  starting transfers between devices  14.1 us (36%)
  waiting for transfers between devices  3.97 us (10%)
    ppermute x15, starting transfers between devices, partner(): return lax.ppermute(block, axis, [(i, i ^ apart) for i in range(count)])  14.1 us
    pallas_call x1, Pallas kernels, local(): call(local_kernel, 'local', [acc_shape] * 2 + [((main, LANES), BF16)] * 2...  7.86 us
    ppermute x15, waiting for transfers between devices, partner(): return lax.ppermute(block, axis, [(i, i ^ apart) for i in range(count)])  3.97 us
    pallas_call x1, Pallas kernels, local(): call(functools.partial(pair_kernel, dils), 'pair', [((n1 * 3 // 8, LANES)...  3.51 us
    pallas_call x1, Pallas kernels, local(): call(functools.partial(project_kernel, dils), 'project', [(out_shape, BF1...  2.46 us
    pallas_call x1, Pallas kernels, local(): call(functools.partial(select_kernel, dils), 'select', [(queries.shape, B...  2.01 us
    pallas_call x1, Pallas kernels, local(): call(functools.partial(far_kernel, branches), 'far', [far_shape] * 2 + [(...  1.43 us
    pallas_call x1, Pallas kernels, local(): call(functools.partial(query_kernel, dils), 'query', [((heads, n1, LANES)...  1.31 us
  transfers between devices with their start and end apart: 15, of which 4 were waited for; matrix products, arithmetic and copies ran while one was open for 0% of the time, Pallas kernels for 41%

profile of v6, /device:TPU:0, one launch (start us, length us, event | category | flops | bytes accessed | tf_op | source)
XLA Modules:
  0.0 38.9 jit_solution(14012120285777087400)
XLA Ops:
  0.0 2.0 %select.1 = (bf16[192,2048]{1,0:T(8,128)(2,1)S(1)}, bf16[192,2048]{1,0:T(8,128)(2,1)S(1)}, bf16[192,2048]{1,0:T(8,128)(2,1)S(1)}, bf16[3,512,128]{2,1,0:T(8,128)(2,1)S(1)}, bf16[2,3,128,128]{3,2,1,0:T(8,128)(2,1)S(1)}) custom-call(s32[3,12]{1,0:T(4,128)} %off_ref.7, bf16[192,2048]{1,0:T(8,128)(2,1)} %q_hbm.1, bf16[192,2048]{1,0:T(8,128)(2,1)} %k_hbm.1, ...), custom_call_target="tpu_custom_call" | custom-call | flops 6000000000 | bytes 1024 | tf_op jit(solution)/shard_map/select/pallas_call | solution.py:454
  2.0 4.1 %collective-permute-start.7 = (bf16[2,3,128,128]{3,2,1,0:T(8,128)(2,1)S(1)}, bf16[2,3,128,128]{3,2,1,0:T(8,128)(2,1)S(1)}, u32[]{:S(2)}, u32[]{:S(2)}) collective-permute-start(bf16[2,3,128,128]{3,2,1,0:T(8,128)(2,1)S(1)} %get-tuple-element.67.kv0), channel_id=1, source_target_pairs={{0,16},{4,20},{8,24},{12,28},{16,0},{20,4},{24,8},{28,12},{1,17},{... | collective-permute-start | bytes 589832 | tf_op jit(solution)/shard_map/ppermute | solution.py:372
  6.1 1.3 %collective-permute-start.8 = (bf16[2,3,128,128]{3,2,1,0:T(8,128)(2,1)S(1)}, bf16[2,3,128,128]{3,2,1,0:T(8,128)(2,1)S(1)}, u32[]{:S(2)}, u32[]{:S(2)}) collective-permute-start(bf16[2,3,128,128]{3,2,1,0:T(8,128)(2,1)S(1)} %get-tuple-element.67.kv0), channel_id=1, source_target_pairs={{0,24},{4,28},{8,16},{12,20},{16,8},{20,12},{24,0},{28,4},{1,25},{... | collective-permute-start | bytes 589832 | tf_op jit(solution)/shard_map/ppermute | solution.py:372
  7.5 0.2 collective-permute-start.9
  7.7 1.5 %collective-permute-start.3 = (bf16[3,512,128]{2,1,0:T(8,128)(2,1)S(1)}, bf16[3,512,128]{2,1,0:T(8,128)(2,1)S(1)}, u32[]{:S(2)}, u32[]{:S(2)}) collective-permute-start(bf16[3,512,128]{2,1,0:T(8,128)(2,1)S(1)} %get-tuple-element.51.own_ref), channel_id=1, source_target_pairs={{0,4},{4,0},{8,12},{12,8},{16,20},{20,16},{24,28},{28,24},{1,5},{5... | collective-permute-start | bytes 1179656 | tf_op jit(solution)/shard_map/ppermute | solution.py:372
  9.2 1.3 %query.1 = (bf16[3,512,128]{2,1,0:T(8,128)(2,1)S(1)}, bf16[3,128,128]{2,1,0:T(8,128)(2,1)S(1)}) custom-call(s32[3,12]{1,0:T(4,128)} %off_ref.7, bf16[192,2048]{1,0:T(8,128)(2,1)S(1)} %get-tuple-element.44.q_ref), custom_call_target="tpu_custom_call" | custom-call | flops 4000000000 | bytes 1024 | tf_op jit(solution)/shard_map/query/pallas_call | solution.py:468
  10.5 0.6 %collective-permute-start.10 = (bf16[3,128,128]{2,1,0:T(8,128)(2,1)S(1)}, bf16[3,128,128]{2,1,0:T(8,128)(2,1)S(1)}, u32[]{:S(2)}, u32[]{:S(2)}) collective-permute-start(bf16[3,128,128]{2,1,0:T(8,128)(2,1)S(1)} %get-tuple-element.66.q_own), channel_id=1, source_target_pairs={{0,4},{4,0},{8,12},{12,8},{16,20},{20,16},{24,28},{28,24},{1,5},{5... | collective-permute-start | bytes 294920 | tf_op jit(solution)/shard_map/ppermute | solution.py:372
  11.1 7.9 %local.1 = (f32[3,2048,128]{2,1,0:T(8,128)S(1)}, f32[3,2048,128]{2,1,0:T(8,128)S(1)}, bf16[768,128]{1,0:T(8,128)(2,1)S(1)}, bf16[768,128]{1,0:T(8,128)(2,1)S(1)}, bf16[1536,128]{1,0:T(8,128)(2,1)S(1)}) custom-call(bf16[192,2048]{1,0:T(8,128)(2,1)S(1)} %get-tuple-element.44.q_ref, bf16[192,2048]{1,0:T(8,128)(2,1)S(1)} %get-tuple-element.45.k_ref, ...), custom_call_target="tpu_custom_call" | custom-call | flops 24999999488 | bytes 1024 | tf_op jit(solution)/shard_map/local/pallas_call | solution.py:484
  19.0 1.5 %collective-permute-start.1 = (bf16[1536,128]{1,0:T(8,128)(2,1)S(1)}, bf16[1536,128]{1,0:T(8,128)(2,1)S(1)}, u32[]{:S(2)}, u32[]{:S(2)}) collective-permute-start(bf16[1536,128]{1,0:T(8,128)(2,1)S(1)} %get-tuple-element.49), channel_id=1, source_target_pairs={{0,2},{1,3},{2,0},{3,1},{4,6},{5,7},{6,4},{7,5},{8,10},{9,11},{10,... | collective-permute-start | bytes 1179656 | tf_op jit(solution)/shard_map/ppermute | solution.py:372
  20.6 3.5 %pair.1 = (bf16[192,128]{1,0:T(8,128)(2,1)S(1)}, bf16[192,128]{1,0:T(8,128)(2,1)S(1)}, bf16[192,128]{1,0:T(8,128)(2,1)S(1)}, bf16[192,128]{1,0:T(8,128)(2,1)S(1)...) custom-call(s32[3,12]{1,0:T(4,128)S(1)} %copy-done.1, ...), custom_call_target="tpu_custom_call", output_to_operand_aliasing={{6}: (4, {}), {7}: (5, {})} | custom-call | flops 3000000000 | bytes 1024 | tf_op jit(solution)/shard_map/pair/pallas_call | solution.py:503
  24.1 1.4 %far.1 = (f32[2,3,128,128]{3,2,1,0:T(8,128)S(1)}, f32[2,3,128,128]{3,2,1,0:T(8,128)S(1)}, bf16[3,160,128]{2,1,0:T(8,128)(2,1)S(1)}) custom-call(bf16[3,128,128]{2,1,0:T(8,128)(2,1)S(1)} %get-tuple-element.66.q_own, bf16[3,128,128]{2,1,0:T(8,128)(2,1)S(1)} %collective-permute-done.10.q_other, bf16[2,3,128,128]{3,2,1,0:T(8,128)(2,1)S(1)} %get-tuple-element.67.kv0, ...), custom_call_target="tpu_custom_call" | custom-call | flops 1000000000 | bytes 1024 | tf_op jit(solution)/shard_map/far/pallas_call | solution.py:513
  25.6 1.6 %collective-permute-start.11 = (bf16[3,160,128]{2,1,0:T(8,128)(2,1)S(1)}, bf16[3,160,128]{2,1,0:T(8,128)(2,1)S(1)}, u32[]{:S(2)}, u32[]{:S(2)}) collective-permute-start(bf16[3,160,128]{2,1,0:T(8,128)(2,1)S(1)} %get-tuple-element.73), channel_id=1, source_target_pairs={{0,4},{4,0},{8,12},{12,8},{16,20},{20,16},{24,28},{28,24},{1,5},{5... | collective-permute-start | bytes 368648 | tf_op jit(solution)/shard_map/ppermute | solution.py:372
  27.1 0.5 %collective-permute-start.4 = (bf16[192,128]{1,0:T(8,128)(2,1)S(1)}, bf16[192,128]{1,0:T(8,128)(2,1)S(1)}, u32[]{:S(2)}, u32[]{:S(2)}) collective-permute-start(bf16[192,128]{1,0:T(8,128)(2,1)S(1)} %get-tuple-element.57), channel_id=1, source_target_pairs={{0,1},{1,0},{2,3},{3,2},{4,5},{5,4},{6,7},{7,6},{8,9},{9,8},{10,11... | collective-permute-start | bytes 147464 | tf_op jit(solution)/shard_map/ppermute | solution.py:372
  27.6 0.5 %collective-permute-start.5 = (bf16[192,128]{1,0:T(8,128)(2,1)S(1)}, bf16[192,128]{1,0:T(8,128)(2,1)S(1)}, u32[]{:S(2)}, u32[]{:S(2)}) collective-permute-start(bf16[192,128]{1,0:T(8,128)(2,1)S(1)} %get-tuple-element.58), channel_id=1, source_target_pairs={{0,2},{1,3},{2,0},{3,1},{4,6},{5,7},{6,4},{7,5},{8,10},{9,11},{10,... | collective-permute-start | bytes 147464 | tf_op jit(solution)/shard_map/ppermute | solution.py:372
  28.1 0.6 %collective-permute-done.1.x2 = bf16[1536,128]{1,0:T(8,128)(2,1)S(1)} collective-permute-done((bf16[1536,128]{1,0:T(8,128)(2,1)S(1)}, bf16[1536,128]{1,0:T(8,128)(2,1)S(1)}, u32[]{:S(2)}, u32[]{:S(2)}) %collective-permute-start.1) | collective-permute-done | bytes 393248 | tf_op jit(solution)/shard_map/ppermute | solution.py:372
  28.8 0.2 collective-permute-start.6
  29.0 1.5 %collective-permute-done.11.got_ref = bf16[3,160,128]{2,1,0:T(8,128)(2,1)S(1)} collective-permute-done((bf16[3,160,128]{2,1,0:T(8,128)(2,1)S(1)}, bf16[3,160,128]{2,1,0:T(8,128)(2,1)S(1)}, u32[]{:S(2)}, u32[]{:S(2)}) %collective-permute-start.11) | collective-permute-done | bytes 122912 | tf_op jit(solution)/shard_map/ppermute | solution.py:372
  30.5 1.2 %patch.1 = (bf16[96,128]{1,0:T(8,128)(2,1)S(1)}, bf16[96,128]{1,0:T(8,128)(2,1)S(1)}, bf16[96,128]{1,0:T(8,128)(2,1)S(1)}, bf16[96,128]{1,0:T(8,128)(2,1)S(1)}) custom-call(s32[3,12]{1,0:T(4,128)S(1)} %copy-done.1, f32[2,3,128,128]{3,2,1,0:T(8,128)S(1)} %get-tuple-element.64.cur_ref, f32[2,3,128,128]{3,2,1,0:T(8,128)S(1)} %get-tuple-element.65.cur_top, ...), custom_call_target="tpu_custom_call" | custom-call | flops 5000000000 | bytes 1024 | tf_op jit(solution)/shard_map/patch/pallas_call | solution.py:522
  31.7 0.6 %collective-permute-start.12 = (bf16[96,128]{1,0:T(8,128)(2,1)S(1)}, bf16[96,128]{1,0:T(8,128)(2,1)S(1)}, u32[]{:S(2)}, u32[]{:S(2)}) collective-permute-start(bf16[96,128]{1,0:T(8,128)(2,1)S(1)} %get-tuple-element.75), channel_id=1, source_target_pairs={{0,1},{1,0},{2,3},{3,2},{4,5},{5,4},{6,7},{7,6},{8,9},{9,8},{10,11... | collective-permute-start | bytes 73736 | tf_op jit(solution)/shard_map/ppermute | solution.py:372
  32.3 0.5 %collective-permute-start.13 = (bf16[96,128]{1,0:T(8,128)(2,1)S(1)}, bf16[96,128]{1,0:T(8,128)(2,1)S(1)}, u32[]{:S(2)}, u32[]{:S(2)}) collective-permute-start(bf16[96,128]{1,0:T(8,128)(2,1)S(1)} %get-tuple-element.76), channel_id=1, source_target_pairs={{0,2},{1,3},{2,0},{3,1},{4,6},{5,7},{6,4},{7,5},{8,10},{9,11},{10,... | collective-permute-start | bytes 73736 | tf_op jit(solution)/shard_map/ppermute | solution.py:372
  32.8 0.9 %collective-permute-start.14 = (bf16[96,128]{1,0:T(8,128)(2,1)S(1)}, bf16[96,128]{1,0:T(8,128)(2,1)S(1)}, u32[]{:S(2)}, u32[]{:S(2)}) collective-permute-start(bf16[96,128]{1,0:T(8,128)(2,1)S(1)} %get-tuple-element.77), channel_id=1, source_target_pairs={{0,3},{1,2},{2,1},{3,0},{4,7},{5,6},{6,5},{7,4},{8,11},{9,10},{10,... | collective-permute-start | bytes 73736 | tf_op jit(solution)/shard_map/ppermute | solution.py:372
  33.7 0.9 %arrange.1 = (f32[4,512,128]{2,1,0:T(8,128)S(1)}, f32[2,512,128]{2,1,0:T(8,128)S(1)}) custom-call(s32[3,12]{1,0:T(4,128)S(1)} %copy-done.1, bf16[768,128]{1,0:T(8,128)(2,1)S(1)} %get-tuple-element.47.x0, bf16[768,128]{1,0:T(8,128)(2,1)S(1)} %collective-permute-done.x1, bf16[1536,128]{1,0:T(8,128)(2,1)S(1)} %collective-permute-done.1.x2, ...), custom_call_target="tpu_custom_call" | custom-call | flops 4000000000 | bytes 1024 | tf_op jit(solution)/shard_map/arrange/pallas_call | solution.py:533
  34.6 1.7 %collective-permute-done.13.p2 = bf16[96,128]{1,0:T(8,128)(2,1)S(1)} collective-permute-done((bf16[96,128]{1,0:T(8,128)(2,1)S(1)}, bf16[96,128]{1,0:T(8,128)(2,1)S(1)}, u32[]{:S(2)}, u32[]{:S(2)}) %collective-permute-start.13) | collective-permute-done | bytes 24608 | tf_op jit(solution)/shard_map/ppermute | solution.py:372
  36.3 2.5 %project.1 = (bf16[512,768]{1,0:T(8,128)(2,1)}, f32[4,512,128]{2,1,0:T(8,128)S(1)}, f32[2,512,128]{2,1,0:T(8,128)S(1)}) custom-call(s32[3,12]{1,0:T(4,128)S(1)} %copy-done.1, f32[4,512,128]{2,1,0:T(8,128)S(1)} %get-tuple-element.60.pairs_in, f32[2,512,128]{2,1,0:T(8,128)S(1)} %get-tuple-element.61.lasts_in, ...), custom_call_target="tpu_custom_call", output_to_operand_aliasing={{1}: (1, {}), {2}: (2, {})} | custom-call | flops 6000000000 | bytes 1024 | tf_op jit(solution)/shard_map/project/pallas_call | solution.py:536
  (18 shorter events, 0.1 us)
Async XLA Ops:
  2.0 22.1 %collective-permute-start.7 = (bf16[2,3,128,128]{3,2,1,0:T(8,128)(2,1)S(1)}, bf16[2,3,128,128]{3,2,1,0:T(8,128)(2,1)S(1)}, u32[]{:S(2)}, u32[]{:S(2)}) collective-permute-start(bf16[2,3,128,128]{3,2,1,0:T(8,128)(2,1)S(1)} %get-tuple-element.67.kv0), channel_id=1, source_target_pairs={{0,16},{4,20},{8,24},{12,28},{16,0},{20,4},{24,8},{28,12},{1,17},{... | collective-permute-start | bytes 589832 | tf_op jit(solution)/shard_map/ppermute | solution.py:372
  6.1 18.0 %collective-permute-start.8 = (bf16[2,3,128,128]{3,2,1,0:T(8,128)(2,1)S(1)}, bf16[2,3,128,128]{3,2,1,0:T(8,128)(2,1)S(1)}, u32[]{:S(2)}, u32[]{:S(2)}) collective-permute-start(bf16[2,3,128,128]{3,2,1,0:T(8,128)(2,1)S(1)} %get-tuple-element.67.kv0), channel_id=1, source_target_pairs={{0,24},{4,28},{8,16},{12,20},{16,8},{20,12},{24,0},{28,4},{1,25},{... | collective-permute-start | bytes 589832 | tf_op jit(solution)/shard_map/ppermute | solution.py:372
  7.5 16.6 %collective-permute-start.9 = (bf16[2,3,128,128]{3,2,1,0:T(8,128)(2,1)S(1)}, bf16[2,3,128,128]{3,2,1,0:T(8,128)(2,1)S(1)}, u32[]{:S(2)}, u32[]{:S(2)}) collective-permute-start(bf16[2,3,128,128]{3,2,1,0:T(8,128)(2,1)S(1)} %get-tuple-element.67.kv0), channel_id=1, source_target_pairs={{0,8},{4,12},{8,0},{12,4},{16,24},{20,28},{24,16},{28,20},{1,9},{5... | collective-permute-start | bytes 589832 | tf_op jit(solution)/shard_map/ppermute | solution.py:372
  7.7 11.3 %collective-permute-start.3 = (bf16[3,512,128]{2,1,0:T(8,128)(2,1)S(1)}, bf16[3,512,128]{2,1,0:T(8,128)(2,1)S(1)}, u32[]{:S(2)}, u32[]{:S(2)}) collective-permute-start(bf16[3,512,128]{2,1,0:T(8,128)(2,1)S(1)} %get-tuple-element.51.own_ref), channel_id=1, source_target_pairs={{0,4},{4,0},{8,12},{12,8},{16,20},{20,16},{24,28},{28,24},{1,5},{5... | collective-permute-start | bytes 1179656 | tf_op jit(solution)/shard_map/ppermute | solution.py:372
  10.5 13.6 %collective-permute-start.10 = (bf16[3,128,128]{2,1,0:T(8,128)(2,1)S(1)}, bf16[3,128,128]{2,1,0:T(8,128)(2,1)S(1)}, u32[]{:S(2)}, u32[]{:S(2)}) collective-permute-start(bf16[3,128,128]{2,1,0:T(8,128)(2,1)S(1)} %get-tuple-element.66.q_own), channel_id=1, source_target_pairs={{0,4},{4,0},{8,12},{12,8},{16,20},{20,16},{24,28},{28,24},{1,5},{5... | collective-permute-start | bytes 294920 | tf_op jit(solution)/shard_map/ppermute | solution.py:372
  11.1 9.5 %copy-start.1 = (s32[3,12]{1,0:T(4,128)S(1)}, s32[3,12]{1,0:T(4,128)}, u32[]{:S(2)}) copy-start(s32[3,12]{1,0:T(4,128)} %off_ref.7) | copy-start | bytes 436
  19.0 9.7 %collective-permute-start.1 = (bf16[1536,128]{1,0:T(8,128)(2,1)S(1)}, bf16[1536,128]{1,0:T(8,128)(2,1)S(1)}, u32[]{:S(2)}, u32[]{:S(2)}) collective-permute-start(bf16[1536,128]{1,0:T(8,128)(2,1)S(1)} %get-tuple-element.49), channel_id=1, source_target_pairs={{0,2},{1,3},{2,0},{3,1},{4,6},{5,7},{6,4},{7,5},{8,10},{9,11},{10,... | collective-permute-start | bytes 1179656 | tf_op jit(solution)/shard_map/ppermute | solution.py:372
  25.6 4.9 %collective-permute-start.11 = (bf16[3,160,128]{2,1,0:T(8,128)(2,1)S(1)}, bf16[3,160,128]{2,1,0:T(8,128)(2,1)S(1)}, u32[]{:S(2)}, u32[]{:S(2)}) collective-permute-start(bf16[3,160,128]{2,1,0:T(8,128)(2,1)S(1)} %get-tuple-element.73), channel_id=1, source_target_pairs={{0,4},{4,0},{8,12},{12,8},{16,20},{20,16},{24,28},{28,24},{1,5},{5... | collective-permute-start | bytes 368648 | tf_op jit(solution)/shard_map/ppermute | solution.py:372
  27.1 4.6 %collective-permute-start = (bf16[768,128]{1,0:T(8,128)(2,1)S(1)}, bf16[768,128]{1,0:T(8,128)(2,1)S(1)}, u32[]{:S(2)}, u32[]{:S(2)}) collective-permute-start(bf16[768,128]{1,0:T(8,128)(2,1)S(1)} %get-tuple-element.48), channel_id=1, source_target_pairs={{0,1},{1,0},{2,3},{3,2},{4,5},{5,4},{6,7},{7,6},{8,9},{9,8},{10,11... | collective-permute-start | bytes 589832 | tf_op jit(solution)/shard_map/ppermute | solution.py:372
  27.1 5.1 %collective-permute-start.4 = (bf16[192,128]{1,0:T(8,128)(2,1)S(1)}, bf16[192,128]{1,0:T(8,128)(2,1)S(1)}, u32[]{:S(2)}, u32[]{:S(2)}) collective-permute-start(bf16[192,128]{1,0:T(8,128)(2,1)S(1)} %get-tuple-element.57), channel_id=1, source_target_pairs={{0,1},{1,0},{2,3},{3,2},{4,5},{5,4},{6,7},{7,6},{8,9},{9,8},{10,11... | collective-permute-start | bytes 147464 | tf_op jit(solution)/shard_map/ppermute | solution.py:372
  27.6 5.1 %collective-permute-start.5 = (bf16[192,128]{1,0:T(8,128)(2,1)S(1)}, bf16[192,128]{1,0:T(8,128)(2,1)S(1)}, u32[]{:S(2)}, u32[]{:S(2)}) collective-permute-start(bf16[192,128]{1,0:T(8,128)(2,1)S(1)} %get-tuple-element.58), channel_id=1, source_target_pairs={{0,2},{1,3},{2,0},{3,1},{4,6},{5,7},{6,4},{7,5},{8,10},{9,11},{10,... | collective-permute-start | bytes 147464 | tf_op jit(solution)/shard_map/ppermute | solution.py:372
  28.8 4.9 %collective-permute-start.6 = (bf16[192,128]{1,0:T(8,128)(2,1)S(1)}, bf16[192,128]{1,0:T(8,128)(2,1)S(1)}, u32[]{:S(2)}, u32[]{:S(2)}) collective-permute-start(bf16[192,128]{1,0:T(8,128)(2,1)S(1)} %get-tuple-element.59), channel_id=1, source_target_pairs={{0,3},{1,2},{2,1},{3,0},{4,7},{5,6},{6,5},{7,4},{8,11},{9,10},{10,... | collective-permute-start | bytes 147464 | tf_op jit(solution)/shard_map/ppermute | solution.py:372
  30.5 3.2 %collective-permute-start.2 = (bf16[1536,128]{1,0:T(8,128)(2,1)S(1)}, bf16[1536,128]{1,0:T(8,128)(2,1)S(1)}, u32[]{:S(2)}, u32[]{:S(2)}) collective-permute-start(bf16[1536,128]{1,0:T(8,128)(2,1)S(1)} %collective-permute-done.1.x2), channel_id=1, source_target_pairs={{0,1},{1,0},{2,3},{3,2},{4,5},{5,4},{6,7},{7,6},{8,9},{9,8},{10,11... | collective-permute-start | bytes 1179656 | tf_op jit(solution)/shard_map/ppermute | solution.py:372
  31.7 2.9 %collective-permute-start.12 = (bf16[96,128]{1,0:T(8,128)(2,1)S(1)}, bf16[96,128]{1,0:T(8,128)(2,1)S(1)}, u32[]{:S(2)}, u32[]{:S(2)}) collective-permute-start(bf16[96,128]{1,0:T(8,128)(2,1)S(1)} %get-tuple-element.75), channel_id=1, source_target_pairs={{0,1},{1,0},{2,3},{3,2},{4,5},{5,4},{6,7},{7,6},{8,9},{9,8},{10,11... | collective-permute-start | bytes 73736 | tf_op jit(solution)/shard_map/ppermute | solution.py:372
  32.3 4.0 %collective-permute-start.13 = (bf16[96,128]{1,0:T(8,128)(2,1)S(1)}, bf16[96,128]{1,0:T(8,128)(2,1)S(1)}, u32[]{:S(2)}, u32[]{:S(2)}) collective-permute-start(bf16[96,128]{1,0:T(8,128)(2,1)S(1)} %get-tuple-element.76), channel_id=1, source_target_pairs={{0,2},{1,3},{2,0},{3,1},{4,6},{5,7},{6,4},{7,5},{8,10},{9,11},{10,... | collective-permute-start | bytes 73736 | tf_op jit(solution)/shard_map/ppermute | solution.py:372
  32.8 3.5 %collective-permute-start.14 = (bf16[96,128]{1,0:T(8,128)(2,1)S(1)}, bf16[96,128]{1,0:T(8,128)(2,1)S(1)}, u32[]{:S(2)}, u32[]{:S(2)}) collective-permute-start(bf16[96,128]{1,0:T(8,128)(2,1)S(1)} %get-tuple-element.77), channel_id=1, source_target_pairs={{0,3},{1,2},{2,1},{3,0},{4,7},{5,6},{6,5},{7,4},{8,11},{9,10},{10,... | collective-permute-start | bytes 73736 | tf_op jit(solution)/shard_map/ppermute | solution.py:372
  33.7 2.6 %copy-start = (bf16[768,768]{1,0:T(8,128)(2,1)S(1)}, bf16[768,768]{1,0:T(8,128)(2,1)}, u32[]{:S(2)}) copy-start(bf16[768,768]{1,0:T(8,128)(2,1)} %w_ref.1) | copy-start | bytes 3538948
